TPU v7x, 32 devices: a whole 2x2x4 slice. The times are simulated.
32 devices in a mesh: visit: 8 (over y, x, core), sky: 4 (over z).
Axes of the slice: x: 2, y: 2, z: 4, core: 2. Of those that a mesh axis runs over, the one named last changes fastest.
Arguments:
- science: float32 [8, 16, 128, 128], P('visit', 'sky'), may hold values from -6 to 6
- coef_first: float32 [8, 16, 3, 49], P('visit', 'sky'), may hold values from -4 to 4
- coef_second: float32 [8, 16, 3, 49], P('visit', 'sky'), may hold values from -4 to 4
- weight: float32 [8, 16], P('visit', 'sky'), may hold values from 0.3 to 3
- slot_tile: int32 [8, 16], P('visit', 'sky'), may hold values from 0 to 3, as said below
- offsets: int32 [8, 16, 2], P('visit', 'sky'), may hold values from 0 to 128
- counts: int32 [8, 4], P('visit', 'sky'), may hold values from 3 to 4, as said below
- tile_place: int32 [4], replicated, may hold values from 0 to 3, as said below
Outputs:
- template: float32 [4, 256, 256], P('sky')
- difference: float32 [8, 16, 128, 128], P('visit', 'sky')
Inputs may be any that keep to these rules, and one draw needn't show every extreme that they name: `slot_tile`: among the usable slots of one device's list at most 2 name tiles of one owner; in every visit the tile of some owner gets exactly 2 usable slots from every device of the sky axis. A permutation: tile t is owned by the device of sky index tile_place[t]. The first counts[v, s] slots of a device's list are usable; in every visit some device has all 4 usable.
All inputs are finite; a program needn't handle non-finite values.
Results may differ from a plain program's by a relative error of at most 0.00011.
Values sent between devices are 32-bit elements; how exact they have to be, the bound alone decides.
No kernel may reach another device: no remote copies, remote signals or barrier semaphores. Data moves between devices by JAX's collectives and lax.ppermute only.
A program may use at most 64 MiB of HBM per device.

v0:
```python
import jax
import jax.numpy as jnp
from jax import lax
from jax.sharding import PartitionSpec as P

TILE = 256
TAPS = 21
PROFILES = 7


WIDTHS = (1.0, 1.0, 1.0, 2.5, 2.5, 2.5, 5.0)
POWERS = (0, 1, 2, 0, 1, 2, 0)
PRECISE = lax.Precision.HIGHEST


def profile_filters(side):
    reach = (TAPS - 1) // 2
    places = jnp.arange(side).astype(jnp.float32)
    spacing = places[None, :] - places[:, None]
    support = jnp.arange(TAPS).astype(jnp.float32) - reach
    stacked = []
    for number in range(PROFILES):
        sample = support ** POWERS[number] * jnp.exp(
            -support * support / (2.0 * WIDTHS[number] ** 2)
        )
        norming = jnp.sqrt(jnp.sum(sample * sample))
        values = spacing ** POWERS[number] * jnp.exp(
            -spacing * spacing / (2.0 * WIDTHS[number] ** 2)
        )
        stacked.append(jnp.where(jnp.abs(spacing) <= reach, values / norming, 0.0))
    return jnp.stack(stacked)


def positions(side):
    places = jnp.arange(side).astype(jnp.float32)
    return (2.0 * places - (side - 1)) / (side - 1)


def kernel_pass(block, coeffs, filters, spread):
    across_x = jnp.einsum("yw,ixw->iyx", block, filters, precision=PRECISE)
    layout = coeffs.reshape(3, PROFILES, PROFILES)
    plain = jnp.einsum("ij,jab->iab", layout[0], filters, precision=PRECISE)
    along = jnp.einsum("ij,jab->iab", layout[2], filters, precision=PRECISE) * spread[None, :, None]
    sideways = jnp.einsum("ij,jab->iab", layout[1], filters, precision=PRECISE)
    steady = jnp.einsum("iab,ibx->ax", plain + along, across_x, precision=PRECISE)
    varying = jnp.einsum("iab,ibx->ax", sideways, across_x, precision=PRECISE)
    return steady + varying * spread[None, :]


def body(science, coef_first, coef_second, weight, slot_tile, offsets, counts, tile_place):
    slots = science.shape[1]
    side = science.shape[2]
    owners_count = lax.axis_size("sky")
    capacity = max(2, (slots + owners_count - 1) // owners_count)
    buffer_slots = owners_count * capacity
    filters = profile_filters(side)
    spread = positions(side)
    listed = jnp.arange(slots)
    usable = listed < counts[0, 0]
    tile_ids = jnp.arange(tile_place.shape[0])
    owners = jnp.sum(
        jnp.where(slot_tile[0][:, None] == tile_ids[None, :], tile_place[None, :], 0), axis=1
    )
    convolved = lax.map(
        lambda operands: kernel_pass(operands[0], operands[1], filters, spread),
        (science[0], coef_first[0]),
    )
    sharing = (
        (owners[:, None] == owners[None, :]) & usable[None, :] & (listed[None, :] < listed[:, None])
    )
    earlier = jnp.sum(sharing.astype(jnp.int32), axis=1)
    target = jnp.where(usable, owners * capacity + earlier, -1)
    routing = (target[None, :] == jnp.arange(buffer_slots)[:, None]).astype(jnp.float32)
    packed = jnp.dot(routing, convolved.reshape(slots, side * side), precision=PRECISE).reshape(
        buffer_slots, side, side
    )
    sent_weight = jnp.dot(routing, weight[0], precision=PRECISE)
    sent_corner = jnp.dot(routing, offsets[0].astype(jnp.float32), precision=PRECISE)
    arrived, arrived_weight, arrived_corner = (
        lax.all_to_all(packed, "sky", split_axis=0, concat_axis=0, tiled=True),
        lax.all_to_all(sent_weight, "sky", split_axis=0, concat_axis=0, tiled=True),
        lax.all_to_all(sent_corner, "sky", split_axis=0, concat_axis=0, tiled=True),
    )
    corners = arrived_corner.astype(jnp.int32)

    def place_block(position, totals):
        weighted, coverage = totals
        corner_top = corners[position, 0]
        corner_left = corners[position, 1]
        block_weight = arrived_weight[position]
        region = lax.dynamic_slice(weighted, (corner_top, corner_left), (side, side))
        weighted = lax.dynamic_update_slice(
            weighted, region + block_weight * arrived[position], (corner_top, corner_left)
        )
        region = lax.dynamic_slice(coverage, (corner_top, corner_left), (side, side))
        coverage = lax.dynamic_update_slice(
            coverage, region + block_weight, (corner_top, corner_left)
        )
        return (weighted, coverage)

    empty = jnp.zeros((TILE, TILE), jnp.float32)
    weighted, coverage = lax.fori_loop(0, buffer_slots, place_block, (empty, empty))
    weighted, coverage = lax.psum((weighted, coverage), "visit")
    template = weighted / (coverage + 1.0)
    cut_back = jax.vmap(
        lambda corner: lax.dynamic_slice(template, (corner[0], corner[1]), (side, side))
    )(corners)
    returned = lax.all_to_all(cut_back, "sky", split_axis=0, concat_axis=0, tiled=True)
    cutouts = jnp.dot(
        routing.T, returned.reshape(buffer_slots, side * side), precision=PRECISE
    ).reshape(slots, side, side)
    matched = lax.map(
        lambda operands: kernel_pass(operands[0], operands[1], filters, spread),
        (cutouts, coef_second[0]),
    )
    difference = jnp.where(usable[:, None, None], science[0] - matched, 0.0)
    return (template[None], difference[None])


def solution(mesh):
    in_specs = (
        P("visit", "sky", None, None),
        P("visit", "sky", None, None),
        P("visit", "sky", None, None),
        P("visit", "sky"),
        P("visit", "sky"),
        P("visit", "sky", None),
        P("visit", "sky"),
        P(),
    )
    out_specs = (P("sky", None, None), P("visit", "sky", None, None))
    return jax.shard_map(body, mesh=mesh, in_specs=in_specs, out_specs=out_specs, check_vma=False)
```

profile of v0, /device:TPU:0, one launch (start us, length us, event | category | flops | bytes accessed | tf_op | source)
XLA Modules:
  0.0 269.4 jit_solution(13443177923790171623)
XLA Ops:
  9.8 6.3 %all-to-all-start.1 = ((f32[4,2,1]{1,2,0:T(1,128)}), f32[4,2,1]{1,2,0:T(1,128)S(1)}, u32[]{:S(2)}, u32[]{:S(2)}) async-start(f32[4,2,1]{1,2,0:T(1,128)} %copy.57), calls=%async_computation.1 | async-start | bytes 4096 | tf_op jit(solution)/shard_map/all_to_all | solution.py:81
  26.9 0.9 copy-done.4
  27.8 15.7 %while.42 = (s32[]{:T(128)}, f32[4,128,128]{2,1,0:T(8,128)S(1)}, f32[4,3,49]{2,1,0:T(4,128)S(1)}, f32[7,128,128]{2,0,1:T(8,128)S(1)}, f32[4,128,128]{2,1,0:T(8,128)S(1)}, /*index=5*/s32[]{:T(128)}) while((s32[]{:T(128)}, f32[4,128,128]{2,1,0:T(8,128)S(1)}, f32[4,3,49]{2,1,0:T(4,128)S(1)}, ...), condition=%wide.region_10.11_spmd.clone.clone, body=%wide.region_9.10_spmd.clone.clone.sunk | while | flops 557646336 | bytes 6362725 | solution.py:64
  45.0 5.1 %all-to-all-start = ((f32[4,2,2]{2,1,0:T(2,128)}), f32[4,2,2]{2,1,0:T(2,128)S(1)}, u32[]{:S(2)}, u32[]{:S(2)}) async-start(f32[4,2,2]{2,1,0:T(2,128)} %fusion.28), calls=%async_computation | async-start | bytes 8192 | tf_op jit(solution)/shard_map/all_to_all | solution.py:82
  50.1 0.9 copy.59
  51.0 4.7 %all-to-all-done = f32[4,2,2]{2,1,0:T(2,128)S(1)} async-done(((f32[4,2,2]{2,1,0:T(2,128)}), f32[4,2,2]{2,1,0:T(2,128)S(1)}, u32[]{:S(2)}, u32[]{:S(2)}) %all-to-all-start) | async-done | bytes 96 | tf_op jit(solution)/shard_map/all_to_all | solution.py:82
  55.6 3.5 %all-to-all-start.2 = ((f32[8,128,128]{2,1,0:T(8,128)}), f32[8,128,128]{2,1,0:T(8,128)S(1)}, u32[]{:S(2)}, u32[]{:S(2)}) async-start(f32[8,128,128]{2,1,0:T(8,128)} %copy.59), calls=%async_computation.2 | async-start | bytes 1048576 | tf_op jit(solution)/shard_map/all_to_all | solution.py:80
  60.7 11.1 %all-to-all-done.2 = f32[8,128,128]{2,1,0:T(8,128)S(1)} async-done(((f32[8,128,128]{2,1,0:T(8,128)}), f32[8,128,128]{2,1,0:T(8,128)S(1)}, u32[]{:S(2)}, u32[]{:S(2)}) %all-to-all-start.2) | async-done | bytes 524320 | tf_op jit(solution)/shard_map/all_to_all | solution.py:80
  71.9 76.6 %while.40 = (s32[]{:T(128)}, f32[256,256]{1,0:T(8,128)S(1)}, f32[256,256]{1,0:T(8,128)S(1)}, s32[8,2]{0,1:T(2,128)S(1)}, f32[8]{0:T(128)S(1)}, /*index=5*/f32[8,...) while((s32[]{:T(128)}, f32[256,256]{1,0:T(8,128)S(1)}, f32[256,256]{1,0:T(8,128)S(1)}, ...), condition=%wide.region_12.13_spmd, body=%wide.region_11.12_spmd.sunk | while | flops 49160 | bytes 591569 | solution.py:102
  77.2 0.8 bitcast_add_fusion.2
  78.0 1.7 dynamic_update_slice.32
  79.7 1.7 dynamic_update_slice.31
  86.7 0.8 bitcast_add_fusion.2
  87.5 2.0 dynamic_update_slice.32
  89.4 2.0 dynamic_update_slice.31
  96.7 0.8 bitcast_add_fusion.2
  97.5 1.5 dynamic_update_slice.32
  99.0 1.5 dynamic_update_slice.31
  105.8 0.8 bitcast_add_fusion.2
  106.6 1.7 dynamic_update_slice.32
  108.3 1.7 dynamic_update_slice.31
  115.4 0.8 bitcast_add_fusion.2
  116.1 2.0 dynamic_update_slice.32
  118.2 2.0 dynamic_update_slice.31
  125.5 0.8 bitcast_add_fusion.2
  126.3 1.5 dynamic_update_slice.32
  127.8 1.5 dynamic_update_slice.31
  134.6 0.8 bitcast_add_fusion.2
  135.4 1.7 dynamic_update_slice.32
  137.1 1.7 dynamic_update_slice.31
  144.2 0.8 bitcast_add_fusion.2
  144.9 1.8 dynamic_update_slice.32
  146.7 1.8 dynamic_update_slice.31
  149.4 54.7 %all-reduce.3.cloned.1.call-done = (f32[256,256]{1,0:T(8,128)}, f32[256,256]{1,0:T(8,128)}) async-done(((f32[256,256]{1,0:T(8,128)}, f32[256,256]{1,0:T(8,128)}), (f32[256,256]{1,0:T(8,128)}, f32[256,256]{1,0:T(8,128)})) %all-reduce.3.cloned.1.call-update) | async-done | bytes 524304 | tf_op jit(solution)/shard_map/psum | solution.py:103
  204.1 1.1 add_divide_fusion
  205.2 20.8 %while.41 = (s32[]{:T(128)}, f32[256,256]{1,0:T(8,128)S(1)}, s32[8,2]{0,1:T(2,128)S(1)}, f32[8,128,128]{2,1,0:T(8,128)}, s32[]{:T(128)}) while((s32[]{:T(128)}, f32[256,256]{1,0:T(8,128)S(1)}, s32[8,2]{0,1:T(2,128)S(1)}, f32[8,128,128]{2,1,0:T(8,128)}, s32[]{:T(128)}) %tuple.118), condition=%wide.while_cond, body=%wide.while_body.sunk | while | flops 2 | bytes 132705 | solution.py:106
  205.8 2.0 bitcast_dynamic-update-slice_fusion.2
  208.4 2.0 bitcast_dynamic-update-slice_fusion.2
  211.0 2.0 bitcast_dynamic-update-slice_fusion.2
  213.6 2.0 bitcast_dynamic-update-slice_fusion.2
  216.2 2.0 bitcast_dynamic-update-slice_fusion.2
  218.8 2.0 bitcast_dynamic-update-slice_fusion.2
  221.4 2.0 bitcast_dynamic-update-slice_fusion.2
  224.0 2.0 bitcast_dynamic-update-slice_fusion.2
  226.7 4.6 %all-to-all-start.3 = ((f32[8,128,128]{2,1,0:T(8,128)}), f32[8,128,128]{2,1,0:T(8,128)S(1)}, u32[]{:S(2)}, u32[]{:S(2)}) async-start(f32[8,128,128]{2,1,0:T(8,128)} %get-tuple-element.193), calls=%async_computation.3 | async-start | bytes 1048576 | tf_op jit(solution)/shard_map/all_to_all | solution.py:108
  231.3 13.8 %all-to-all-done.3 = f32[8,128,128]{2,1,0:T(8,128)S(1)} async-done(((f32[8,128,128]{2,1,0:T(8,128)}), f32[8,128,128]{2,1,0:T(8,128)S(1)}, u32[]{:S(2)}, u32[]{:S(2)}) %all-to-all-start.3) | async-done | bytes 524320 | tf_op jit(solution)/shard_map/all_to_all | solution.py:108
  245.7 16.0 %while.43 = (s32[]{:T(128)}, f32[4,128,128]{2,1,0:T(8,128)S(1)}, f32[4,3,49]{2,1,0:T(4,128)S(1)}, f32[7,128,128]{2,0,1:T(8,128)S(1)}, f32[4,128,128]{2,0,1:T(4,128)S(1)}, /*index=5*/s32[]{:T(128)}) while((s32[]{:T(128)}, f32[4,128,128]{2,1,0:T(8,128)S(1)}, f32[4,3,49]{2,1,0:T(4,128)S(1)}, ...), condition=%wide.region_16.17_spmd.clone.clone, body=%wide.region_15.16_spmd.clone.clone.sunk | while | flops 557646336 | bytes 6428261 | solution.py:112
  261.7 0.8 select_bitcast_fusion
  (191 shorter events, 59.2 us)
Async XLA Ops:
  7.2 1.8 copy-start
  7.8 0.7 copy-start.8
  7.9 0.7 copy-start.9
  9.8 35.1 %all-to-all-start.1 = ((f32[4,2,1]{1,2,0:T(1,128)}), f32[4,2,1]{1,2,0:T(1,128)S(1)}, u32[]{:S(2)}, u32[]{:S(2)}) async-start(f32[4,2,1]{1,2,0:T(1,128)} %copy.57), calls=%async_computation.1 | async-start | bytes 4096 | tf_op jit(solution)/shard_map/all_to_all | solution.py:81
  22.7 2.7 %copy-start.5 = (f32[1,4,3,49]{3,1,2,0:T(4,128)S(1)}, f32[1,4,3,49]{3,1,2,0:T(4,128)}, u32[]{:S(2)}) copy-start(f32[1,4,3,49]{3,1,2,0:T(4,128)} %param.15) | copy-start | bytes 7060
  26.8 1.0 copy-start.4
  43.5 0.7 copy-start.7
  45.0 10.7 %all-to-all-start = ((f32[4,2,2]{2,1,0:T(2,128)}), f32[4,2,2]{2,1,0:T(2,128)S(1)}, u32[]{:S(2)}, u32[]{:S(2)}) async-start(f32[4,2,2]{2,1,0:T(2,128)} %fusion.28), calls=%async_computation | async-start | bytes 8192 | tf_op jit(solution)/shard_map/all_to_all | solution.py:82
  55.6 16.2 %all-to-all-start.2 = ((f32[8,128,128]{2,1,0:T(8,128)}), f32[8,128,128]{2,1,0:T(8,128)S(1)}, u32[]{:S(2)}, u32[]{:S(2)}) async-start(f32[8,128,128]{2,1,0:T(8,128)} %copy.59), calls=%async_computation.2 | async-start | bytes 1048576 | tf_op jit(solution)/shard_map/all_to_all | solution.py:80
  59.1 145.0 %all-reduce.3.cloned.1.call-start = ((), (), s32[]{:S(2)}) async-start(), calls=%async_computation.4 | async-start | bytes 1048576 | tf_op jit(solution)/shard_map/psum | solution.py:103
  148.6 0.7 copy-start.1
  148.6 0.8 copy-start.2
  226.0 0.7 copy-start.3
  226.0 5.3 %copy-start.6 = (f32[1,4,3,49]{3,1,2,0:T(4,128)S(1)}, f32[1,4,3,49]{3,1,2,0:T(4,128)}, u32[]{:S(2)}) copy-start(f32[1,4,3,49]{3,1,2,0:T(4,128)} %param.16) | copy-start | bytes 7060
  226.7 18.3 %all-to-all-start.3 = ((f32[8,128,128]{2,1,0:T(8,128)}), f32[8,128,128]{2,1,0:T(8,128)S(1)}, u32[]{:S(2)}, u32[]{:S(2)}) async-start(f32[8,128,128]{2,1,0:T(8,128)} %get-tuple-element.193), calls=%async_computation.3 | async-start | bytes 1048576 | tf_op jit(solution)/shard_map/all_to_all | solution.py:108
Sparse Core Ops, SparseCore 0:
  149.5 54.5 all-reduce.2
where the time goes:
time: 271 us; the launch traced here: 269 us
  waiting for transfers between devices  84.3 us (31%)
  local copies, waits for them, and re-layouts  67.8 us (25%)
  loops' own time  33 us (12%)
  matrix products  30.9 us (11%)
  between operations  19.6 us (7%)
  starting transfers between devices  19.5 us (7%)
  other arithmetic  14.3 us (5%)
    psum x1, waiting for transfers between devices, body(): weighted, coverage = lax.psum((weighted, coverage), 'visit')  54.7 us
    another operation x1, loops' own time, body(): lax.fori_loop(0, buffer_slots, place_block, (empty, empty))  32.4 us
    gather x24, local copies, waits for them, and re-layouts  20.8 us
    dynamic_update_slice x8, local copies, waits for them, and re-layouts, place_block(): lax.dynamic_update_slice(coverage, region + block_weight, (corner_top, co...  14.1 us
    dynamic_update_slice x8, local copies, waits for them, and re-layouts, place_block(): lax.dynamic_update_slice(weighted, region + block_weight * arrived[positi...  14.1 us
    all_to_all x1, waiting for transfers between devices, body(): lax.all_to_all(cut_back, 'sky', split_axis=0, concat_axis=0, tiled=True)  13.8 us
    all_to_all x1, waiting for transfers between devices, body(): lax.all_to_all(packed, 'sky', split_axis=0, concat_axis=0, tiled=True)  11.1 us
    all_to_all x1, starting transfers between devices, body(): lax.all_to_all(sent_weight, 'sky', split_axis=0, concat_axis=0, tiled=True)  6.35 us
  transfers between devices with their start and end apart: 5, of which 4 were waited for; matrix products, arithmetic and copies ran while one was open for 9% of the time, Pallas kernels for 0%

commit v1 on v0

v1 whole, which is shorter than its diff:
```python
import numpy as np
import jax
import jax.numpy as jnp
from jax import lax
from jax.experimental import pallas as pl
from jax.experimental.pallas import tpu as pltpu
from jax.sharding import PartitionSpec as P

TILE = 256
TAPS = 21
PROFILES = 7
WIDTHS = (1.0, 1.0, 1.0, 2.5, 2.5, 2.5, 5.0)
POWERS = (0, 1, 2, 0, 1, 2, 0)
LANES = 128
META = 8

F32 = jnp.float32
BF16 = jnp.bfloat16


def split_np(values):
    values = np.asarray(values, np.float32)
    high = values.astype(BF16)
    low = (values - high.astype(np.float32)).astype(BF16)
    return high, low


def constants(side, basis):
    reach = (TAPS - 1) // 2
    support = np.arange(TAPS).astype(np.float64) - reach
    taps = []
    for number in range(PROFILES):
        sample = support ** POWERS[number] * np.exp(
            -support * support / (2.0 * WIDTHS[number] ** 2)
        )
        taps.append(sample / np.sqrt(np.sum(sample * sample)))
    taps = np.stack(taps)
    places = np.arange(side)
    spacing = places[:, None] - places[None, :]
    inside = np.abs(spacing) <= reach
    across = np.concatenate(
        [np.where(inside, t[np.clip(spacing + reach, 0, TAPS - 1)], 0.0) for t in taps], axis=1
    )
    rows = np.zeros((LANES, PROFILES * side), np.float64)
    for i in range(PROFILES):
        for j in range(PROFILES):
            for t in range(-reach, reach + 1):
                rows[PROFILES * i + j, i * side + t % side] = taps[j, t + reach]
    return split_np(across) + split_np(rows)


def split(values):
    high = values.astype(BF16)
    low = (values - high.astype(F32)).astype(BF16)
    return high, low


def mm(a, b):
    return jnp.dot(a, b, preferred_element_type=F32)


def mm3(a_high, a_low, b_high, b_low):
    return mm(a_high, b_high) + (mm(a_high, b_low) + mm(a_low, b_high))


def spread_along(shape, axis, side):
    places = lax.broadcasted_iota(jnp.int32, shape, axis).astype(F32)
    return (2.0 * places - (side - 1)) / (side - 1)


def tap_rows(coef_ref, coef_buf, tap_buf, rows_high, rows_low, slots):
    coef_buf[...] = jnp.zeros(coef_buf.shape, F32)
    basis = coef_ref.shape[-1]
    for b in range(slots):
        coef_buf[pl.ds(8 * b, 3), pl.ds(0, basis)] = coef_ref[0, b]
    high, low = split(coef_buf[...])
    tap_buf[...] = mm3(high, low, rows_high[...], rows_low[...])


def kernel_pass(block, b, tap_buf, across_high, across_low, left_high, left_low, side):
    reach = (TAPS - 1) // 2
    square = (side, side)
    row = lax.broadcasted_iota(jnp.int32, square, 0)
    col = lax.broadcasted_iota(jnp.int32, square, 1)
    band = jnp.abs(col - row) <= reach
    spread_y = spread_along(square, 0, side)
    for i in range(PROFILES):
        lanes = slice(i * side, (i + 1) * side)
        plain = jnp.broadcast_to(tap_buf[8 * b : 8 * b + 1, lanes], square)
        sideways = jnp.broadcast_to(tap_buf[8 * b + 1 : 8 * b + 2, lanes], square)
        along = jnp.broadcast_to(tap_buf[8 * b + 2 : 8 * b + 3, lanes], square)
        for part, taps in ((0, plain + along * spread_y), (1, sideways)):
            rolled = pltpu.roll(taps, 0, 1, stride=1, stride_axis=0)
            high, low = split(jnp.where(band, rolled, 0.0))
            left_high[part * side : (part + 1) * side, lanes] = high
            left_low[part * side : (part + 1) * side, lanes] = low
    block_high, block_low = split(block)
    across = mm3(block_high, block_low, across_high[...], across_low[...])
    stacked = jnp.concatenate(
        [across[:, i * side : (i + 1) * side] for i in range(PROFILES)], axis=0
    )
    stacked_high, stacked_low = split(stacked)
    both = mm3(left_high[...], left_low[...], stacked_high, stacked_low)
    return both[:side] + both[side:] * spread_along(square, 1, side)


def first_kernel(
    slots, side, tiles, meta_blocks, halves,
    science, coef, rows_high, rows_low, across_high, across_low,
    weight, slot_tile, offsets, counts, tile_place,
    keep, send,
    coef_buf, tap_buf, left_high, left_low, total,
):
    visit = lax.axis_index("visit")
    sky = lax.axis_index("sky")
    core = visit % 2
    half = TILE // 2
    sky_size = tiles
    tap_rows(coef, coef_buf, tap_buf, rows_high, rows_low, slots)
    total[...] = jnp.zeros(total.shape, F32)
    first_lane = (visit * sky_size + sky) * slots
    lane = lax.broadcasted_iota(jnp.int32, (META, LANES), 1)
    field = lax.broadcasted_iota(jnp.int32, (META, LANES), 0)
    meta = [jnp.zeros((META, LANES), F32) for _ in range(meta_blocks)]
    col = lax.broadcasted_iota(jnp.int32, (side, side), 1)
    for b in range(slots):
        owner = tile_place[slot_tile[0, b]]
        usable = b < counts[0, 0]
        used = jnp.where(usable, weight[0, b], 0.0)
        top = offsets[0, b, 0]
        left = offsets[0, b, 1]
        entry = jnp.where(
            field == 0,
            used,
            jnp.where(
                field == 1,
                top.astype(F32),
                jnp.where(field == 2, left.astype(F32), jnp.where(field == 3, owner.astype(F32), 0.0)),
            ),
        )
        for m in range(meta_blocks):
            meta[m] = jnp.where(lane + m * LANES == first_lane + b, entry, meta[m])
        image = kernel_pass(
            science[0, b], b, tap_buf, across_high, across_low, left_high, left_low, side
        )
        image = jnp.where(usable, image * used, 0.0)
        moved = pltpu.roll(image, left, 1)
        total[owner, 0, pl.ds(top, side), :] += jnp.where(col >= left, moved, 0.0)
        total[owner, 1, pl.ds(top, side), :] += jnp.where(col < left, moved, 0.0)
    body = tiles * 2 * half
    for t in range(tiles):
        for h in range(2):
            base = (t * 2 + h) * half
            keep[pl.ds(base, half), :] = total[t, h, pl.ds(core * half, half), :]
            send[pl.ds(base, half), :] = total[t, h, pl.ds((1 - core) * half, half), :]
    for m in range(meta_blocks):
        keep[pl.ds(body + m * META, META), :] = meta[m]
        send[pl.ds(body + m * META, META), :] = meta[m]


def scatter_kernel(tiles, strip, peers, meta_rows, keep, received, *pieces):
    place = lax.axis_index("visit") // 2
    half = strip * peers
    body = tiles * 2 * half
    for j in range(peers):
        first = (place ^ j) * strip
        for g in range(tiles * 2):
            source = pl.ds(g * half + first, strip)
            pieces[j][pl.ds(g * strip, strip), :] = keep[source, :] + received[source, :]
        source = pl.ds(body, meta_rows)
        pieces[j][pl.ds(tiles * 2 * strip, meta_rows), :] = keep[source, :] + received[source, :]


def plane_kernel(tiles, strip, peers, meta_rows, *refs):
    sources, pieces = refs[:peers], refs[peers:]
    sky = lax.axis_index("sky")
    size = 2 * strip
    tail = pl.ds(tiles * size, meta_rows)
    meta = sources[0][tail, :]
    for p in range(1, peers):
        meta = meta + sources[p][tail, :]
    for j in range(tiles):
        rows = pl.ds((sky ^ j) * size, size)
        value = sources[0][rows, :]
        for p in range(1, peers):
            value = value + sources[p][rows, :]
        pieces[j][pl.ds(0, size), :] = value
        pieces[j][pl.ds(size, meta_rows), :] = meta


def template_kernel(tiles, strip, peers, meta_blocks, side, *refs):
    sources, out = refs[:tiles], refs[tiles]
    visit = lax.axis_index("visit")
    sky = lax.axis_index("sky")
    size = 2 * strip
    value = sources[0][...]
    for p in range(1, tiles):
        value = value + sources[p][...]
    first = (visit % 2) * (TILE // 2) + (visit // 2) * strip
    y = (lax.broadcasted_iota(jnp.int32, (strip, LANES), 0) + first).astype(F32)
    x = lax.broadcasted_iota(jnp.int32, (TILE, LANES), 0).astype(F32)
    coverage = jnp.zeros((strip, TILE), F32)
    for m in range(meta_blocks):
        meta = value[size + m * META : size + (m + 1) * META]
        used, top, left, owner = meta[0:1], meta[1:2], meta[2:3], meta[3:4]
        inside = (y >= top) & (y < top + side) & (owner == sky.astype(F32))
        amount = jnp.where(inside, jnp.broadcast_to(used, y.shape), 0.0)
        columns = jnp.where((x >= left) & (x < left + side), 1.0, 0.0).astype(BF16)
        one, rest = split(amount)
        two = (amount - one.astype(F32)).astype(BF16)
        three = (amount - one.astype(F32) - two.astype(F32)).astype(BF16)
        for part in (one, two, three):
            coverage = coverage + lax.dot_general(
                part, columns, (((1,), (1,)), ((), ())), preferred_element_type=F32
            )
    for h in range(2):
        out[pl.ds(h * strip, strip), :] = value[h * strip : (h + 1) * strip] / (
            coverage[:, h * LANES : (h + 1) * LANES] + 1.0
        )


def stack_kernel(tiles, strip, *refs):
    sources, out = refs[:tiles], refs[tiles]
    sky = lax.axis_index("sky")
    size = 2 * strip
    for j in range(tiles):
        out[pl.ds((sky ^ j) * size, size), :] = sources[j][...]


def second_kernel(
    slots, side, tiles, strip, peers,
    science, coef, rows_high, rows_low, across_high, across_low,
    slot_tile, offsets, counts, tile_place,
    *refs,
):
    pieces = refs[: 2 * peers]
    template, difference = refs[2 * peers : 2 * peers + 2]
    coef_buf, tap_buf, left_high, left_low, total = refs[2 * peers + 2 :]
    visit = lax.axis_index("visit")
    sky = lax.axis_index("sky")
    core = visit % 2
    place = visit // 2
    half = TILE // 2
    tap_rows(coef, coef_buf, tap_buf, rows_high, rows_low, slots)
    for c in range(2):
        for j in range(peers):
            first = (core ^ c) * half + (place ^ j) * strip
            for t in range(tiles):
                for h in range(2):
                    total[t, h, pl.ds(first, strip), :] = pieces[c * peers + j][
                        pl.ds((t * 2 + h) * strip, strip), :
                    ]
    for h in range(2):
        template[0, :, h * LANES : (h + 1) * LANES] = total[sky, h]
    col = lax.broadcasted_iota(jnp.int32, (side, side), 1)
    for b in range(slots):
        owner = tile_place[slot_tile[0, b]]
        usable = b < counts[0, 0]
        top = offsets[0, b, 0]
        left = offsets[0, b, 1]
        joined = jnp.where(
            col >= left, total[owner, 0, pl.ds(top, side), :], total[owner, 1, pl.ds(top, side), :]
        )
        cutout = pltpu.roll(joined, (side - left) % side, 1)
        matched = kernel_pass(
            cutout, b, tap_buf, across_high, across_low, left_high, left_low, side
        )
        difference[0, b] = jnp.where(usable, science[0, b] - matched, 0.0)


def body(science, coef_first, coef_second, weight, slot_tile, offsets, counts, tile_place):
    slots, side = science.shape[1], science.shape[2]
    basis = coef_first.shape[-1]
    visits = lax.axis_size("visit")
    tiles = lax.axis_size("sky")
    peers = visits // 2
    strip = TILE // visits
    meta_blocks = -(-visits * tiles * slots // LANES)
    meta_rows = meta_blocks * META
    across_high, across_low, rows_high, rows_low = (
        jnp.asarray(c) for c in constants(side, basis)
    )
    vmem = pl.BlockSpec(memory_space=pltpu.VMEM)
    smem = pl.BlockSpec(memory_space=pltpu.SMEM)

    def shape(*dims):
        return jax.ShapeDtypeStruct(dims, F32)

    def call(function, ins, outs, specs=None, scratch=(), name=None):
        return pl.pallas_call(
            function,
            out_shape=outs,
            in_specs=specs or [vmem] * len(ins),
            out_specs=jax.tree.map(lambda _: vmem, outs),
            scratch_shapes=list(scratch),
            name=name,
        )(*ins)

    scratch = [
        pltpu.VMEM((8 * slots, LANES), F32),
        pltpu.VMEM((8 * slots, PROFILES * side), F32),
        pltpu.VMEM((2 * side, PROFILES * side), BF16),
        pltpu.VMEM((2 * side, PROFILES * side), BF16),
        pltpu.VMEM((tiles, 2, TILE, LANES), F32),
    ]

    def flip(value, axis, size, mask):
        return lax.ppermute(value, axis, [(d, d ^ mask) for d in range(size)])

    keep, send = call(
        lambda *refs: first_kernel(slots, side, tiles, meta_blocks, peers, *refs),
        (science, coef_first, rows_high, rows_low, across_high, across_low,
         weight, slot_tile, offsets, counts, tile_place),
        [shape(tiles * TILE + meta_rows, LANES)] * 2,
        specs=[vmem] * 6 + [smem] * 5,
        scratch=scratch,
        name="first",
    )
    received = flip(send, "visit", visits, 1)
    pieces = call(
        lambda *refs: scatter_kernel(tiles, strip, peers, meta_rows, *refs),
        (keep, received),
        [shape(tiles * 2 * strip + meta_rows, LANES)] * peers,
        name="scatter",
    )
    arrived = [pieces[0]] + [flip(pieces[j], "visit", visits, 2 * j) for j in range(1, peers)]
    pieces = call(
        lambda *refs: plane_kernel(tiles, strip, peers, meta_rows, *refs),
        arrived,
        [shape(2 * strip + meta_rows, LANES)] * tiles,
        name="plane",
    )
    arrived = [pieces[0]] + [flip(pieces[j], "sky", tiles, j) for j in range(1, tiles)]
    strips = call(
        lambda *refs: template_kernel(tiles, strip, peers, meta_blocks, side, *refs),
        arrived,
        shape(2 * strip, LANES),
        name="template",
    )
    strips = [strips] + [flip(strips, "sky", tiles, j) for j in range(1, tiles)]
    piece = call(
        lambda *refs: stack_kernel(tiles, strip, *refs),
        strips,
        shape(tiles * 2 * strip, LANES),
        name="stack",
    )
    mine = [piece] + [flip(piece, "visit", visits, 2 * j) for j in range(1, peers)]
    theirs = [flip(p, "visit", visits, 1) for p in mine]
    template, difference = call(
        lambda *refs: second_kernel(slots, side, tiles, strip, peers, *refs),
        (science, coef_second, rows_high, rows_low, across_high, across_low,
         slot_tile, offsets, counts, tile_place, *mine, *theirs),
        [shape(1, TILE, TILE), shape(1, slots, side, side)],
        specs=[vmem] * 6 + [smem] * 4 + [vmem] * (2 * peers),
        scratch=scratch,
        name="second",
    )
    return template, difference


def solution(mesh):
    in_specs = (
        P("visit", "sky", None, None),
        P("visit", "sky", None, None),
        P("visit", "sky", None, None),
        P("visit", "sky"),
        P("visit", "sky"),
        P("visit", "sky", None),
        P("visit", "sky"),
        P(),
    )
    out_specs = (P("sky", None, None), P("visit", "sky", None, None))
    return jax.shard_map(body, mesh=mesh, in_specs=in_specs, out_specs=out_specs, check_vma=False)
```

time: 271 us -> 66.6 us (0.25)
  waiting for transfers between devices: 84.3 us -> 22.2 us
  local copies, waits for them, and re-layouts: 67.8 us -> 6.7 us
  loops' own time: 33 us -> 0 us
  matrix products: 30.9 us -> 0 us
  Pallas kernels: 0 us -> 18.8 us
  between operations: 19.6 us -> 1.37 us
  other arithmetic: 14.3 us -> 0 us
    psum x1 -> x0, waiting for transfers between devices: 54.7 us -> none  [body(): weighted, coverage = lax.psum((weighted, coverage), 'visit')]
    another operation x4 -> x0, loops' own time: 33 us -> none  [the longest x1 32.4 us: body(): lax.fori_loop(0, buffer_slots, place_block, (empty, empty))]
    dot_general x52 -> x0, matrix products: 30.9 us -> none  [the longest x8 5.19 us: kernel_pass(): across_x = jnp.einsum('yw,ixw->iyx', block, filters, precision=PRECISE)]
    all_to_all x4 -> x0, waiting for transfers between devices: 29.6 us -> none  [the longest x1 13.8 us: body(): lax.all_to_all(cut_back, 'sky', split_axis=0, concat_axis=0, tiled=True)]
    dynamic_update_slice x16 -> x0, local copies, waits for them, and re-layouts: 28.1 us -> none  [the longest x8 14.1 us: place_block(): lax.dynamic_update_slice(coverage, region + block_weight, (corner_top, co...]
    ppermute x0 -> x17, waiting for transfers between devices: none -> 22.2 us  [flip(): return lax.ppermute(value, axis, [(d, d ^ mask) for d in range(size)])]
    gather x24 -> x0, local copies, waits for them, and re-layouts: 20.8 us -> none
    all_to_all x4 -> x0, starting transfers between devices: 19.5 us -> none  [the longest x1 6.35 us: body(): lax.all_to_all(sent_weight, 'sky', split_axis=0, concat_axis=0, tiled=True)]
  transfers between devices with their start and end apart: 5 -> 17, of which waited for: 4 -> 12; matrix products, arithmetic and copies ran while one was open for 9% -> 1% of each run, Pallas kernels for 0% -> 0%
where the time goes in v1:
time: 66.6 us; the launch traced here: 66.2 us
  waiting for transfers between devices  22.2 us (33%)
  Pallas kernels  18.8 us (28%)
  starting transfers between devices  17.1 us (26%)
  local copies, waits for them, and re-layouts  6.7 us (10%)
  between operations  1.37 us (2%)
    ppermute x17, waiting for transfers between devices, flip(): return lax.ppermute(value, axis, [(d, d ^ mask) for d in range(size)])  22.2 us
    pallas_call x6, Pallas kernels, call(): pl.pallas_call(function, out_shape=outs, in_specs=specs or [vmem] * len(i...  18.8 us
    ppermute x17, starting transfers between devices, flip(): return lax.ppermute(value, axis, [(d, d ^ mask) for d in range(size)])  17.1 us
    unnamed x39, local copies, waits for them, and re-layouts  6.7 us
  transfers between devices with their start and end apart: 17, of which 12 were waited for; matrix products, arithmetic and copies ran while one was open for 1% of the time, Pallas kernels for 0%

profile of v1, /device:TPU:0, one launch (start us, length us, event | category | flops | bytes accessed | tf_op | source)
XLA Modules:
  0.0 66.2 jit_solution(9670454117973836377)
XLA Ops:
  0.6 1.3 %copy.17.refs_8_.refs_7_ = s32[1,4,2]{2,1,0:T(4,128)} copy(s32[1,4,2]{1,2,0:T(2,128)} %param.17) | data formatting | bytes 64 | tf_op args[5]
  2.6 1.3 %copy.14.refs_1_ = f32[1,4,3,49]{3,2,1,0:T(4,128)} copy(f32[1,4,3,49]{3,1,2,0:T(4,128)} %param.13) | data formatting | bytes 4704 | tf_op args[1]
  3.9 5.9 %first.1 = (f32[1032,128]{1,0:T(8,128)}, f32[1032,128]{1,0:T(8,128)}) custom-call(f32[1,4,128,128]{3,2,1,0:T(8,128)} %refs_0_.3, f32[1,4,3,49]{3,2,1,0:T(4,128)} %copy.14.refs_1_, bf16[128,896]{1,0:T(8,128)(2,1)} %constant.10.clone.refs_2_, bf16[128,896]{1,0:T(8,128)(2,1)} %constant.11.clone.refs_3_, bf16[128,896]{1,0:T(8,128)(2,1)} %constant.8.clone.refs_4_, ...), custom_call_target="tpu_custom_call" | custom-call | tf_op jit(solution)/shard_map/first/pallas_call | solution.py:290
  9.8 0.5 collective-permute-start
  10.3 1.8 %collective-permute-done.refs_1_ = f32[1032,128]{1,0:T(8,128)S(1)} collective-permute-done((f32[1032,128]{1,0:T(8,128)}, f32[1032,128]{1,0:T(8,128)S(1)}, u32[]{:S(2)}, u32[]{:S(2)}) %collective-permute-start) | collective-permute-done | bytes 528416 | tf_op jit(solution)/shard_map/ppermute | solution.py:308
  12.1 0.8 %copy-done = f32[1032,128]{1,0:T(8,128)} copy-done((f32[1032,128]{1,0:T(8,128)}, f32[1032,128]{1,0:T(8,128)S(1)}, u32[]{:S(2)}) %copy-start) | copy-done | bytes 528408
  12.9 2.1 %scatter.1 = (f32[264,128]{1,0:T(8,128)}, f32[264,128]{1,0:T(8,128)}, f32[264,128]{1,0:T(8,128)}, f32[264,128]{1,0:T(8,128)}) custom-call(f32[1032,128]{1,0:T(8,128)} %get-tuple-element.12.refs_0_, f32[1032,128]{1,0:T(8,128)} %copy-done), custom_call_target="tpu_custom_call" | custom-call | tf_op jit(solution)/shard_map/scatter/pallas_call | solution.py:290
  15.0 2.9 %collective-permute-start.1 = (f32[264,128]{1,0:T(8,128)}, f32[264,128]{1,0:T(8,128)S(1)}, u32[]{:S(2)}, u32[]{:S(2)}) collective-permute-start(f32[264,128]{1,0:T(8,128)} %get-tuple-element.15), channel_id=1, source_target_pairs={{0,8},{4,12},{8,0},{12,4},{16,24},{20,28},{24,16},{28,20},{1,9},{5... | collective-permute-start | bytes 405512 | tf_op jit(solution)/shard_map/ppermute | solution.py:308
  17.8 1.5 %collective-permute-start.2 = (f32[264,128]{1,0:T(8,128)}, f32[264,128]{1,0:T(8,128)S(1)}, u32[]{:S(2)}, u32[]{:S(2)}) collective-permute-start(f32[264,128]{1,0:T(8,128)} %get-tuple-element.16), channel_id=1, source_target_pairs={{0,16},{4,20},{8,24},{12,28},{16,0},{20,4},{24,8},{28,12},{1,17},{... | collective-permute-start | bytes 405512 | tf_op jit(solution)/shard_map/ppermute | solution.py:308
  19.3 0.0 collective-permute-start.3
  19.3 2.8 %collective-permute-done.1.refs_1_ = f32[264,128]{1,0:T(8,128)S(1)} collective-permute-done((f32[264,128]{1,0:T(8,128)}, f32[264,128]{1,0:T(8,128)S(1)}, u32[]{:S(2)}, u32[]{:S(2)}) %collective-permute-start.1) | collective-permute-done | bytes 135200 | tf_op jit(solution)/shard_map/ppermute | solution.py:308
  22.2 4.1 %collective-permute-done.2.refs_2_ = f32[264,128]{1,0:T(8,128)S(1)} collective-permute-done((f32[264,128]{1,0:T(8,128)}, f32[264,128]{1,0:T(8,128)S(1)}, u32[]{:S(2)}, u32[]{:S(2)}) %collective-permute-start.2) | collective-permute-done | bytes 135200 | tf_op jit(solution)/shard_map/ppermute | solution.py:308
  26.3 0.0 collective-permute-done.3.refs_3_
  26.3 0.6 copy-done.2
  26.9 0.1 copy-done.3
  27.0 1.8 %plane.1 = (f32[72,128]{1,0:T(8,128)}, f32[72,128]{1,0:T(8,128)}, f32[72,128]{1,0:T(8,128)}, f32[72,128]{1,0:T(8,128)}) custom-call(f32[264,128]{1,0:T(8,128)} %get-tuple-element.14.refs_0_, f32[264,128]{1,0:T(8,128)} %copy-done.1, f32[264,128]{1,0:T(8,128)} %copy-done.2, f32[264,128]{1,0:T(8,128)} %copy-done.3), custom_call_target="tpu_custom_call" | custom-call | tf_op jit(solution)/shard_map/plane/pallas_call | solution.py:290
  28.8 1.6 %collective-permute-start.4 = (f32[72,128]{1,0:T(8,128)}, f32[72,128]{1,0:T(8,128)S(1)}, u32[]{:S(2)}, u32[]{:S(2)}) collective-permute-start(f32[72,128]{1,0:T(8,128)} %get-tuple-element.19), channel_id=1, source_target_pairs={{0,1},{1,0},{2,3},{3,2},{4,5},{5,4},{6,7},{7,6},{8,9},{9,8},{10,11... | collective-permute-start | bytes 110600 | tf_op jit(solution)/shard_map/ppermute | solution.py:308
  30.4 2.6 %collective-permute-start.5 = (f32[72,128]{1,0:T(8,128)}, f32[72,128]{1,0:T(8,128)S(1)}, u32[]{:S(2)}, u32[]{:S(2)}) collective-permute-start(f32[72,128]{1,0:T(8,128)} %get-tuple-element.20), channel_id=1, source_target_pairs={{0,2},{1,3},{2,0},{3,1},{4,6},{5,7},{6,4},{7,5},{8,10},{9,11},{10,... | collective-permute-start | bytes 110600 | tf_op jit(solution)/shard_map/ppermute | solution.py:308
  33.0 0.2 collective-permute-start.6
  33.2 0.1 collective-permute-done.4.refs_1_
  33.3 2.5 %collective-permute-done.5.refs_2_ = f32[72,128]{1,0:T(8,128)S(1)} collective-permute-done((f32[72,128]{1,0:T(8,128)}, f32[72,128]{1,0:T(8,128)S(1)}, u32[]{:S(2)}, u32[]{:S(2)}) %collective-permute-start.5) | collective-permute-done | bytes 36896 | tf_op jit(solution)/shard_map/ppermute | solution.py:308
  35.8 3.1 %collective-permute-done.6.refs_3_ = f32[72,128]{1,0:T(8,128)S(1)} collective-permute-done((f32[72,128]{1,0:T(8,128)}, f32[72,128]{1,0:T(8,128)S(1)}, u32[]{:S(2)}, u32[]{:S(2)}) %collective-permute-start.6) | collective-permute-done | bytes 36896 | tf_op jit(solution)/shard_map/ppermute | solution.py:308
  38.9 0.6 copy-done.13
  39.5 1.6 %template.1.refs_0_ = f32[64,128]{1,0:T(8,128)} custom-call(f32[72,128]{1,0:T(8,128)} %get-tuple-element.18.refs_0_, f32[72,128]{1,0:T(8,128)} %copy-done.11, f32[72,128]{1,0:T(8,128)} %copy-done.12, f32[72,128]{1,0:T(8,128)} %copy-done.13), custom_call_target="tpu_custom_call" | custom-call | tf_op jit(solution)/shard_map/template/pallas_call | solution.py:290
  41.2 0.0 collective-permute-start.7
  41.2 1.0 %collective-permute-start.8 = (f32[64,128]{1,0:T(8,128)}, f32[64,128]{1,0:T(8,128)S(1)}, u32[]{:S(2)}, u32[]{:S(2)}) collective-permute-start(f32[64,128]{1,0:T(8,128)} %template.1.refs_0_), channel_id=1, source_target_pairs={{0,2},{1,3},{2,0},{3,1},{4,6},{5,7},{6,4},{7,5},{8,10},{9,11},{10,... | collective-permute-start | bytes 98312 | tf_op jit(solution)/shard_map/ppermute | solution.py:308
  42.1 3.4 %collective-permute-start.9 = (f32[64,128]{1,0:T(8,128)}, f32[64,128]{1,0:T(8,128)S(1)}, u32[]{:S(2)}, u32[]{:S(2)}) collective-permute-start(f32[64,128]{1,0:T(8,128)} %template.1.refs_0_), channel_id=1, source_target_pairs={{0,3},{1,2},{2,1},{3,0},{4,7},{5,6},{6,5},{7,4},{8,11},{9,10},{10,... | collective-permute-start | bytes 98312 | tf_op jit(solution)/shard_map/ppermute | solution.py:308
  45.5 0.0 collective-permute-done.7.refs_1_
  45.5 0.6 collective-permute-done.8.refs_2_
  46.2 1.9 %collective-permute-done.9.refs_3_ = f32[64,128]{1,0:T(8,128)S(1)} collective-permute-done((f32[64,128]{1,0:T(8,128)}, f32[64,128]{1,0:T(8,128)S(1)}, u32[]{:S(2)}, u32[]{:S(2)}) %collective-permute-start.9) | collective-permute-done | bytes 32800 | tf_op jit(solution)/shard_map/ppermute | solution.py:308
  48.0 0.6 copy-done.16
  48.6 1.5 %stack.1.refs_10_ = f32[256,128]{1,0:T(8,128)} custom-call(f32[64,128]{1,0:T(8,128)} %template.1.refs_0_, f32[64,128]{1,0:T(8,128)} %copy-done.14, f32[64,128]{1,0:T(8,128)} %copy-done.15, f32[64,128]{1,0:T(8,128)} %copy-done.16), custom_call_target="tpu_custom_call" | custom-call | tf_op jit(solution)/shard_map/stack/pallas_call | solution.py:290
  50.1 1.2 %collective-permute-start.10 = (f32[256,128]{1,0:T(8,128)}, f32[256,128]{1,0:T(8,128)S(1)}, u32[]{:S(2)}, u32[]{:S(2)}) collective-permute-start(f32[256,128]{1,0:T(8,128)} %stack.1.refs_10_), channel_id=1, source_target_pairs={{0,8},{4,12},{8,0},{12,4},{16,24},{20,28},{24,16},{28,20},{1,9},{5... | collective-permute-start | bytes 393224 | tf_op jit(solution)/shard_map/ppermute | solution.py:308
  51.3 0.9 %collective-permute-start.11 = (f32[256,128]{1,0:T(8,128)}, f32[256,128]{1,0:T(8,128)S(1)}, u32[]{:S(2)}, u32[]{:S(2)}) collective-permute-start(f32[256,128]{1,0:T(8,128)} %stack.1.refs_10_), channel_id=1, source_target_pairs={{0,16},{4,20},{8,24},{12,28},{16,0},{20,4},{24,8},{28,12},{1,17},{... | collective-permute-start | bytes 393224 | tf_op jit(solution)/shard_map/ppermute | solution.py:308
  52.2 1.4 %collective-permute-start.12 = (f32[256,128]{1,0:T(8,128)}, f32[256,128]{1,0:T(8,128)S(1)}, u32[]{:S(2)}, u32[]{:S(2)}) collective-permute-start(f32[256,128]{1,0:T(8,128)} %stack.1.refs_10_), channel_id=1, source_target_pairs={{0,24},{4,28},{8,16},{12,20},{16,8},{20,12},{24,0},{28,4},{1,25},{... | collective-permute-start | bytes 393224 | tf_op jit(solution)/shard_map/ppermute | solution.py:308
  53.6 1.7 %collective-permute-done.10.refs_11_ = f32[256,128]{1,0:T(8,128)S(1)} collective-permute-done((f32[256,128]{1,0:T(8,128)}, f32[256,128]{1,0:T(8,128)S(1)}, u32[]{:S(2)}, u32[]{:S(2)}) %collective-permute-start.10) | collective-permute-done | bytes 131104 | tf_op jit(solution)/shard_map/ppermute | solution.py:308
  55.3 0.0 collective-permute-start.14
  55.3 1.2 %collective-permute-done.11.refs_12_ = f32[256,128]{1,0:T(8,128)S(1)} collective-permute-done((f32[256,128]{1,0:T(8,128)}, f32[256,128]{1,0:T(8,128)S(1)}, u32[]{:S(2)}, u32[]{:S(2)}) %collective-permute-start.11) | collective-permute-done | bytes 131104 | tf_op jit(solution)/shard_map/ppermute | solution.py:308
  56.5 0.0 collective-permute-start.15
  56.5 1.8 %collective-permute-done.12.refs_13_ = f32[256,128]{1,0:T(8,128)S(1)} collective-permute-done((f32[256,128]{1,0:T(8,128)}, f32[256,128]{1,0:T(8,128)S(1)}, u32[]{:S(2)}, u32[]{:S(2)}) %collective-permute-start.12) | collective-permute-done | bytes 131104 | tf_op jit(solution)/shard_map/ppermute | solution.py:308
  58.2 0.0 collective-permute-start.16
  58.3 0.7 copy.16.refs_1_
  58.9 0.0 collective-permute-done.14.refs_15_
  58.9 0.0 collective-permute-done.15.refs_16_
  58.9 0.6 collective-permute-done.16.refs_17_
  59.6 0.1 copy-done.9
  59.7 0.6 copy-done.10
  60.3 5.9 %second.1 = (f32[1,256,256]{2,1,0:T(8,128)}, f32[1,4,128,128]{3,2,1,0:T(8,128)}) custom-call(f32[1,4,128,128]{3,2,1,0:T(8,128)} %refs_0_.3, f32[1,4,3,49]{3,2,1,0:T(4,128)} %copy.16.refs_1_, bf16[128,896]{1,0:T(8,128)(2,1)} %constant.10.clone.refs_2_, bf16[128,896]{1,0:T(8,128)(2,1)} %constant.11.clone.refs_3_, bf16[128,896]{1,0:T(8,128)(2,1)} %constant.8.clone.refs_4_, ...), custom_call_target="tpu_custom_call" | custom-call | tf_op jit(solution)/shard_map/second/pallas_call | solution.py:290
  (31 shorter events, 0.1 us)
Async XLA Ops:
  9.8 2.2 %collective-permute-start = (f32[1032,128]{1,0:T(8,128)}, f32[1032,128]{1,0:T(8,128)S(1)}, u32[]{:S(2)}, u32[]{:S(2)}) collective-permute-start(f32[1032,128]{1,0:T(8,128)} %get-tuple-element.13), channel_id=1, source_target_pairs={{0,4},{4,0},{8,12},{12,8},{16,20},{20,16},{24,28},{28,24},{1,5},{5... | collective-permute-start | bytes 1585160 | tf_op jit(solution)/shard_map/ppermute | solution.py:308
  12.1 0.8 %copy-start = (f32[1032,128]{1,0:T(8,128)}, f32[1032,128]{1,0:T(8,128)S(1)}, u32[]{:S(2)}) copy-start(f32[1032,128]{1,0:T(8,128)S(1)} %collective-permute-done.refs_1_) | copy-start | bytes 1585156
  15.0 7.2 %collective-permute-start.1 = (f32[264,128]{1,0:T(8,128)}, f32[264,128]{1,0:T(8,128)S(1)}, u32[]{:S(2)}, u32[]{:S(2)}) collective-permute-start(f32[264,128]{1,0:T(8,128)} %get-tuple-element.15), channel_id=1, source_target_pairs={{0,8},{4,12},{8,0},{12,4},{16,24},{20,28},{24,16},{28,20},{1,9},{5... | collective-permute-start | bytes 405512 | tf_op jit(solution)/shard_map/ppermute | solution.py:308
  17.8 8.5 %collective-permute-start.2 = (f32[264,128]{1,0:T(8,128)}, f32[264,128]{1,0:T(8,128)S(1)}, u32[]{:S(2)}, u32[]{:S(2)}) collective-permute-start(f32[264,128]{1,0:T(8,128)} %get-tuple-element.16), channel_id=1, source_target_pairs={{0,16},{4,20},{8,24},{12,28},{16,0},{20,4},{24,8},{28,12},{1,17},{... | collective-permute-start | bytes 405512 | tf_op jit(solution)/shard_map/ppermute | solution.py:308
  19.3 6.9 %collective-permute-start.3 = (f32[264,128]{1,0:T(8,128)}, f32[264,128]{1,0:T(8,128)S(1)}, u32[]{:S(2)}, u32[]{:S(2)}) collective-permute-start(f32[264,128]{1,0:T(8,128)} %get-tuple-element.17), channel_id=1, source_target_pairs={{0,24},{4,28},{8,16},{12,20},{16,8},{20,12},{24,0},{28,4},{1,25},{... | collective-permute-start | bytes 405512 | tf_op jit(solution)/shard_map/ppermute | solution.py:308
  22.2 4.1 %copy-start.1 = (f32[264,128]{1,0:T(8,128)}, f32[264,128]{1,0:T(8,128)S(1)}, u32[]{:S(2)}) copy-start(f32[264,128]{1,0:T(8,128)S(1)} %collective-permute-done.1.refs_1_) | copy-start | bytes 405508
  26.3 0.6 copy-start.2
  26.3 0.7 %copy-start.3 = (f32[264,128]{1,0:T(8,128)}, f32[264,128]{1,0:T(8,128)S(1)}, u32[]{:S(2)}) copy-start(f32[264,128]{1,0:T(8,128)S(1)} %collective-permute-done.3.refs_3_) | copy-start | bytes 405508
  28.8 4.5 %collective-permute-start.4 = (f32[72,128]{1,0:T(8,128)}, f32[72,128]{1,0:T(8,128)S(1)}, u32[]{:S(2)}, u32[]{:S(2)}) collective-permute-start(f32[72,128]{1,0:T(8,128)} %get-tuple-element.19), channel_id=1, source_target_pairs={{0,1},{1,0},{2,3},{3,2},{4,5},{5,4},{6,7},{7,6},{8,9},{9,8},{10,11... | collective-permute-start | bytes 110600 | tf_op jit(solution)/shard_map/ppermute | solution.py:308
  30.4 5.4 %collective-permute-start.5 = (f32[72,128]{1,0:T(8,128)}, f32[72,128]{1,0:T(8,128)S(1)}, u32[]{:S(2)}, u32[]{:S(2)}) collective-permute-start(f32[72,128]{1,0:T(8,128)} %get-tuple-element.20), channel_id=1, source_target_pairs={{0,2},{1,3},{2,0},{3,1},{4,6},{5,7},{6,4},{7,5},{8,10},{9,11},{10,... | collective-permute-start | bytes 110600 | tf_op jit(solution)/shard_map/ppermute | solution.py:308
  33.0 6.0 %collective-permute-start.6 = (f32[72,128]{1,0:T(8,128)}, f32[72,128]{1,0:T(8,128)S(1)}, u32[]{:S(2)}, u32[]{:S(2)}) collective-permute-start(f32[72,128]{1,0:T(8,128)} %get-tuple-element.21), channel_id=1, source_target_pairs={{0,3},{1,2},{2,1},{3,0},{4,7},{5,6},{6,5},{7,4},{8,11},{9,10},{10,... | collective-permute-start | bytes 110600 | tf_op jit(solution)/shard_map/ppermute | solution.py:308
  33.3 5.6 %copy-start.11 = (f32[72,128]{1,0:T(8,128)}, f32[72,128]{1,0:T(8,128)S(1)}, u32[]{:S(2)}) copy-start(f32[72,128]{1,0:T(8,128)S(1)} %collective-permute-done.4.refs_1_) | copy-start | bytes 110596
  35.8 3.2 %copy-start.12 = (f32[72,128]{1,0:T(8,128)}, f32[72,128]{1,0:T(8,128)S(1)}, u32[]{:S(2)}) copy-start(f32[72,128]{1,0:T(8,128)S(1)} %collective-permute-done.5.refs_2_) | copy-start | bytes 110596
  38.9 0.6 copy-start.13
  41.2 17.1 %copy-start.17 = (f32[1,4,3,49]{3,1,2,0:T(4,128)S(1)}, f32[1,4,3,49]{3,1,2,0:T(4,128)}, u32[]{:S(2)}) copy-start(f32[1,4,3,49]{3,1,2,0:T(4,128)} %param.14) | copy-start | bytes 7060
  41.2 4.4 %collective-permute-start.7 = (f32[64,128]{1,0:T(8,128)}, f32[64,128]{1,0:T(8,128)S(1)}, u32[]{:S(2)}, u32[]{:S(2)}) collective-permute-start(f32[64,128]{1,0:T(8,128)} %template.1.refs_0_), channel_id=1, source_target_pairs={{0,1},{1,0},{2,3},{3,2},{4,5},{5,4},{6,7},{7,6},{8,9},{9,8},{10,11... | collective-permute-start | bytes 98312 | tf_op jit(solution)/shard_map/ppermute | solution.py:308
  41.2 5.0 %collective-permute-start.8 = (f32[64,128]{1,0:T(8,128)}, f32[64,128]{1,0:T(8,128)S(1)}, u32[]{:S(2)}, u32[]{:S(2)}) collective-permute-start(f32[64,128]{1,0:T(8,128)} %template.1.refs_0_), channel_id=1, source_target_pairs={{0,2},{1,3},{2,0},{3,1},{4,6},{5,7},{6,4},{7,5},{8,10},{9,11},{10,... | collective-permute-start | bytes 98312 | tf_op jit(solution)/shard_map/ppermute | solution.py:308
  42.1 5.9 %collective-permute-start.9 = (f32[64,128]{1,0:T(8,128)}, f32[64,128]{1,0:T(8,128)S(1)}, u32[]{:S(2)}, u32[]{:S(2)}) collective-permute-start(f32[64,128]{1,0:T(8,128)} %template.1.refs_0_), channel_id=1, source_target_pairs={{0,3},{1,2},{2,1},{3,0},{4,7},{5,6},{6,5},{7,4},{8,11},{9,10},{10,... | collective-permute-start | bytes 98312 | tf_op jit(solution)/shard_map/ppermute | solution.py:308
  45.5 2.5 %copy-start.14 = (f32[64,128]{1,0:T(8,128)}, f32[64,128]{1,0:T(8,128)S(1)}, u32[]{:S(2)}) copy-start(f32[64,128]{1,0:T(8,128)S(1)} %collective-permute-done.7.refs_1_) | copy-start | bytes 98308
  46.2 1.9 %copy-start.15 = (f32[64,128]{1,0:T(8,128)}, f32[64,128]{1,0:T(8,128)S(1)}, u32[]{:S(2)}) copy-start(f32[64,128]{1,0:T(8,128)S(1)} %collective-permute-done.8.refs_2_) | copy-start | bytes 98308
  48.0 0.6 copy-start.16
  50.1 5.2 %collective-permute-start.10 = (f32[256,128]{1,0:T(8,128)}, f32[256,128]{1,0:T(8,128)S(1)}, u32[]{:S(2)}, u32[]{:S(2)}) collective-permute-start(f32[256,128]{1,0:T(8,128)} %stack.1.refs_10_), channel_id=1, source_target_pairs={{0,8},{4,12},{8,0},{12,4},{16,24},{20,28},{24,16},{28,20},{1,9},{5... | collective-permute-start | bytes 393224 | tf_op jit(solution)/shard_map/ppermute | solution.py:308
  51.3 5.2 %collective-permute-start.11 = (f32[256,128]{1,0:T(8,128)}, f32[256,128]{1,0:T(8,128)S(1)}, u32[]{:S(2)}, u32[]{:S(2)}) collective-permute-start(f32[256,128]{1,0:T(8,128)} %stack.1.refs_10_), channel_id=1, source_target_pairs={{0,16},{4,20},{8,24},{12,28},{16,0},{20,4},{24,8},{28,12},{1,17},{... | collective-permute-start | bytes 393224 | tf_op jit(solution)/shard_map/ppermute | solution.py:308
  52.2 6.1 %collective-permute-start.12 = (f32[256,128]{1,0:T(8,128)}, f32[256,128]{1,0:T(8,128)S(1)}, u32[]{:S(2)}, u32[]{:S(2)}) collective-permute-start(f32[256,128]{1,0:T(8,128)} %stack.1.refs_10_), channel_id=1, source_target_pairs={{0,24},{4,28},{8,16},{12,20},{16,8},{20,12},{24,0},{28,4},{1,25},{... | collective-permute-start | bytes 393224 | tf_op jit(solution)/shard_map/ppermute | solution.py:308
  53.6 5.3 %collective-permute-start.13 = (f32[256,128]{1,0:T(8,128)}, f32[256,128]{1,0:T(8,128)S(1)}, u32[]{:S(2)}, u32[]{:S(2)}) collective-permute-start(f32[256,128]{1,0:T(8,128)} %stack.1.refs_10_), channel_id=1, source_target_pairs={{0,4},{4,0},{8,12},{12,8},{16,20},{20,16},{24,28},{28,24},{1,5},{5... | collective-permute-start | bytes 393224 | tf_op jit(solution)/shard_map/ppermute | solution.py:308
  55.3 4.3 %copy-start.4 = (f32[256,128]{1,0:T(8,128)}, f32[256,128]{1,0:T(8,128)S(1)}, u32[]{:S(2)}) copy-start(f32[256,128]{1,0:T(8,128)S(1)} %collective-permute-done.10.refs_11_) | copy-start | bytes 393220
  55.3 3.6 %collective-permute-start.14 = (f32[256,128]{1,0:T(8,128)S(1)}, f32[256,128]{1,0:T(8,128)S(1)}, u32[]{:S(2)}, u32[]{:S(2)}) collective-permute-start(f32[256,128]{1,0:T(8,128)S(1)} %collective-permute-done.10.refs_11_), channel_id=1, source_target_pairs={{0,4},{4,0},{8,12},{12,8},{16,20},{20,16},{24,28},{28,24},{1,5},{5... | collective-permute-start | bytes 393224 | tf_op jit(solution)/shard_map/ppermute | solution.py:308
  56.5 3.1 %copy-start.5 = (f32[256,128]{1,0:T(8,128)}, f32[256,128]{1,0:T(8,128)S(1)}, u32[]{:S(2)}) copy-start(f32[256,128]{1,0:T(8,128)S(1)} %collective-permute-done.11.refs_12_) | copy-start | bytes 393220
  56.5 2.5 %collective-permute-start.15 = (f32[256,128]{1,0:T(8,128)S(1)}, f32[256,128]{1,0:T(8,128)S(1)}, u32[]{:S(2)}, u32[]{:S(2)}) collective-permute-start(f32[256,128]{1,0:T(8,128)S(1)} %collective-permute-done.11.refs_12_), channel_id=1, source_target_pairs={{0,4},{4,0},{8,12},{12,8},{16,20},{20,16},{24,28},{28,24},{1,5},{5... | collective-permute-start | bytes 393224 | tf_op jit(solution)/shard_map/ppermute | solution.py:308
  58.2 1.4 %copy-start.6 = (f32[256,128]{1,0:T(8,128)}, f32[256,128]{1,0:T(8,128)S(1)}, u32[]{:S(2)}) copy-start(f32[256,128]{1,0:T(8,128)S(1)} %collective-permute-done.12.refs_13_) | copy-start | bytes 393220
  58.2 1.3 %collective-permute-start.16 = (f32[256,128]{1,0:T(8,128)S(1)}, f32[256,128]{1,0:T(8,128)S(1)}, u32[]{:S(2)}, u32[]{:S(2)}) collective-permute-start(f32[256,128]{1,0:T(8,128)S(1)} %collective-permute-done.12.refs_13_), channel_id=1, source_target_pairs={{0,4},{4,0},{8,12},{12,8},{16,20},{20,16},{24,28},{28,24},{1,5},{5... | collective-permute-start | bytes 393224 | tf_op jit(solution)/shard_map/ppermute | solution.py:308
  58.9 0.7 %copy-start.7 = (f32[256,128]{1,0:T(8,128)}, f32[256,128]{1,0:T(8,128)S(1)}, u32[]{:S(2)}) copy-start(f32[256,128]{1,0:T(8,128)S(1)} %collective-permute-done.13.refs_14_) | copy-start | bytes 393220
  58.9 0.7 %copy-start.8 = (f32[256,128]{1,0:T(8,128)}, f32[256,128]{1,0:T(8,128)S(1)}, u32[]{:S(2)}) copy-start(f32[256,128]{1,0:T(8,128)S(1)} %collective-permute-done.14.refs_15_) | copy-start | bytes 393220
  58.9 0.7 %copy-start.9 = (f32[256,128]{1,0:T(8,128)}, f32[256,128]{1,0:T(8,128)S(1)}, u32[]{:S(2)}) copy-start(f32[256,128]{1,0:T(8,128)S(1)} %collective-permute-done.15.refs_16_) | copy-start | bytes 393220
  59.7 0.6 copy-start.10

commit v2 on v1

--- a/solution.py
+++ b/solution.py
@@ -6,6 +6,7 @@
 from jax.experimental.pallas import tpu as pltpu
 from jax.sharding import PartitionSpec as P
 
+
 TILE = 256
 TAPS = 21
 PROFILES = 7
@@ -13,6 +14,7 @@
 POWERS = (0, 1, 2, 0, 1, 2, 0)
 LANES = 128
 META = 8
+VMEM_BYTES = 24 * 2**20
 
 F32 = jnp.float32
 BF16 = jnp.bfloat16
@@ -25,7 +27,7 @@
     return high, low
 
 
-def constants(side, basis):
+def constants(side):
     reach = (TAPS - 1) // 2
     support = np.arange(TAPS).astype(np.float64) - reach
     taps = []
@@ -71,8 +73,9 @@
 def tap_rows(coef_ref, coef_buf, tap_buf, rows_high, rows_low, slots):
     coef_buf[...] = jnp.zeros(coef_buf.shape, F32)
     basis = coef_ref.shape[-1]
-    for b in range(slots):
-        coef_buf[pl.ds(8 * b, 3), pl.ds(0, basis)] = coef_ref[0, b]
+    pitch = coef_buf.shape[0] // 3
+    for k in range(3):
+        coef_buf[pl.ds(pitch * k, slots), pl.ds(0, basis)] = coef_ref[0, k]
     high, low = split(coef_buf[...])
     tap_buf[...] = mm3(high, low, rows_high[...], rows_low[...])
 
@@ -84,11 +87,12 @@
     col = lax.broadcasted_iota(jnp.int32, square, 1)
     band = jnp.abs(col - row) <= reach
     spread_y = spread_along(square, 0, side)
+    pitch = tap_buf.shape[0] // 3
     for i in range(PROFILES):
         lanes = slice(i * side, (i + 1) * side)
-        plain = jnp.broadcast_to(tap_buf[8 * b : 8 * b + 1, lanes], square)
-        sideways = jnp.broadcast_to(tap_buf[8 * b + 1 : 8 * b + 2, lanes], square)
-        along = jnp.broadcast_to(tap_buf[8 * b + 2 : 8 * b + 3, lanes], square)
+        plain = jnp.broadcast_to(tap_buf[b : b + 1, lanes], square)
+        sideways = jnp.broadcast_to(tap_buf[pitch + b : pitch + b + 1, lanes], square)
+        along = jnp.broadcast_to(tap_buf[2 * pitch + b : 2 * pitch + b + 1, lanes], square)
         for part, taps in ((0, plain + along * spread_y), (1, sideways)):
             rolled = pltpu.roll(taps, 0, 1, stride=1, stride_axis=0)
             high, low = split(jnp.where(band, rolled, 0.0))
@@ -105,7 +109,7 @@
 
 
 def first_kernel(
-    slots, side, tiles, meta_blocks, halves,
+    slots, side, tiles, meta_blocks,
     science, coef, rows_high, rows_low, across_high, across_low,
     weight, slot_tile, offsets, counts, tile_place,
     keep, send,
@@ -127,8 +131,8 @@
         owner = tile_place[slot_tile[0, b]]
         usable = b < counts[0, 0]
         used = jnp.where(usable, weight[0, b], 0.0)
-        top = offsets[0, b, 0]
-        left = offsets[0, b, 1]
+        top = offsets[0, 0, b]
+        left = offsets[0, 1, b]
         entry = jnp.where(
             field == 0,
             used,
@@ -159,6 +163,7 @@
 
 
 def scatter_kernel(tiles, strip, peers, meta_rows, keep, received, *pieces):
+    pieces = pieces[::-1]
     place = lax.axis_index("visit") // 2
     half = strip * peers
     body = tiles * 2 * half
@@ -172,7 +177,7 @@
 
 
 def plane_kernel(tiles, strip, peers, meta_rows, *refs):
-    sources, pieces = refs[:peers], refs[peers:]
+    sources, pieces = refs[:peers], refs[peers:][::-1]
     sky = lax.axis_index("sky")
     size = 2 * strip
     tail = pl.ds(tiles * size, meta_rows)
@@ -188,7 +193,7 @@
         pieces[j][pl.ds(size, meta_rows), :] = meta
 
 
-def template_kernel(tiles, strip, peers, meta_blocks, side, *refs):
+def template_kernel(tiles, strip, meta_blocks, side, *refs):
     sources, out = refs[:tiles], refs[tiles]
     visit = lax.axis_index("visit")
     sky = lax.axis_index("sky")
@@ -206,7 +211,7 @@
         inside = (y >= top) & (y < top + side) & (owner == sky.astype(F32))
         amount = jnp.where(inside, jnp.broadcast_to(used, y.shape), 0.0)
         columns = jnp.where((x >= left) & (x < left + side), 1.0, 0.0).astype(BF16)
-        one, rest = split(amount)
+        one, _ = split(amount)
         two = (amount - one.astype(F32)).astype(BF16)
         three = (amount - one.astype(F32) - two.astype(F32)).astype(BF16)
         for part in (one, two, three):
@@ -256,8 +261,8 @@
     for b in range(slots):
         owner = tile_place[slot_tile[0, b]]
         usable = b < counts[0, 0]
-        top = offsets[0, b, 0]
-        left = offsets[0, b, 1]
+        top = offsets[0, 0, b]
+        left = offsets[0, 1, b]
         joined = jnp.where(
             col >= left, total[owner, 0, pl.ds(top, side), :], total[owner, 1, pl.ds(top, side), :]
         )
@@ -270,7 +275,6 @@
 
 def body(science, coef_first, coef_second, weight, slot_tile, offsets, counts, tile_place):
     slots, side = science.shape[1], science.shape[2]
-    basis = coef_first.shape[-1]
     visits = lax.axis_size("visit")
     tiles = lax.axis_size("sky")
     peers = visits // 2
@@ -278,27 +282,38 @@
     meta_blocks = -(-visits * tiles * slots // LANES)
     meta_rows = meta_blocks * META
     across_high, across_low, rows_high, rows_low = (
-        jnp.asarray(c) for c in constants(side, basis)
+        jnp.asarray(c) for c in constants(side)
     )
     vmem = pl.BlockSpec(memory_space=pltpu.VMEM)
     smem = pl.BlockSpec(memory_space=pltpu.SMEM)
 
+    coef_first = coef_first.transpose(0, 2, 1, 3)
+    coef_second = coef_second.transpose(0, 2, 1, 3)
+    offsets = offsets.transpose(0, 2, 1)
+
     def shape(*dims):
-        return jax.ShapeDtypeStruct(dims, F32)
-
-    def call(function, ins, outs, specs=None, scratch=(), name=None):
+        return pltpu.VMEM(dims, F32)
+
+    def far(value):
+        return pltpu.with_memory_space_constraint(value, pltpu.HBM)
+
+    def near(value):
+        return pltpu.with_memory_space_constraint(value, pltpu.VMEM)
+
+    def call(function, ins, outs, specs=None, scratch=()):
         return pl.pallas_call(
             function,
             out_shape=outs,
             in_specs=specs or [vmem] * len(ins),
             out_specs=jax.tree.map(lambda _: vmem, outs),
             scratch_shapes=list(scratch),
-            name=name,
+            compiler_params=pltpu.CompilerParams(vmem_limit_bytes=VMEM_BYTES),
         )(*ins)
 
+    pitch = -(-slots // 8) * 8
     scratch = [
-        pltpu.VMEM((8 * slots, LANES), F32),
-        pltpu.VMEM((8 * slots, PROFILES * side), F32),
+        pltpu.VMEM((3 * pitch, LANES), F32),
+        pltpu.VMEM((3 * pitch, PROFILES * side), F32),
         pltpu.VMEM((2 * side, PROFILES * side), BF16),
         pltpu.VMEM((2 * side, PROFILES * side), BF16),
         pltpu.VMEM((tiles, 2, TILE, LANES), F32),
@@ -307,53 +322,53 @@
     def flip(value, axis, size, mask):
         return lax.ppermute(value, axis, [(d, d ^ mask) for d in range(size)])
 
+    def exchange(values, axis, size, step):
+        out = [values[0]]
+        for j in range(1, len(values)):
+            out.append(flip(values[j], axis, size, step * j))
+        return out
+
     keep, send = call(
-        lambda *refs: first_kernel(slots, side, tiles, meta_blocks, peers, *refs),
-        (science, coef_first, rows_high, rows_low, across_high, across_low,
+        lambda *refs: first_kernel(slots, side, tiles, meta_blocks, *refs),
+        (*map(far, (science, coef_first, rows_high, rows_low, across_high, across_low)),
          weight, slot_tile, offsets, counts, tile_place),
         [shape(tiles * TILE + meta_rows, LANES)] * 2,
         specs=[vmem] * 6 + [smem] * 5,
         scratch=scratch,
-        name="first",
     )
     received = flip(send, "visit", visits, 1)
     pieces = call(
         lambda *refs: scatter_kernel(tiles, strip, peers, meta_rows, *refs),
-        (keep, received),
+        (near(keep), near(received)),
         [shape(tiles * 2 * strip + meta_rows, LANES)] * peers,
-        name="scatter",
-    )
-    arrived = [pieces[0]] + [flip(pieces[j], "visit", visits, 2 * j) for j in range(1, peers)]
+    )[::-1]
+    arrived = exchange(pieces, "visit", visits, 2)
     pieces = call(
         lambda *refs: plane_kernel(tiles, strip, peers, meta_rows, *refs),
-        arrived,
+        [near(a) for a in arrived],
         [shape(2 * strip + meta_rows, LANES)] * tiles,
-        name="plane",
-    )
-    arrived = [pieces[0]] + [flip(pieces[j], "sky", tiles, j) for j in range(1, tiles)]
+    )[::-1]
+    arrived = exchange(pieces, "sky", tiles, 1)
     strips = call(
-        lambda *refs: template_kernel(tiles, strip, peers, meta_blocks, side, *refs),
-        arrived,
+        lambda *refs: template_kernel(tiles, strip, meta_blocks, side, *refs),
+        [near(a) for a in arrived],
         shape(2 * strip, LANES),
-        name="template",
-    )
-    strips = [strips] + [flip(strips, "sky", tiles, j) for j in range(1, tiles)]
+    )
+    strips = exchange([strips] * tiles, "sky", tiles, 1)
     piece = call(
         lambda *refs: stack_kernel(tiles, strip, *refs),
-        strips,
+        [near(a) for a in strips],
         shape(tiles * 2 * strip, LANES),
-        name="stack",
-    )
-    mine = [piece] + [flip(piece, "visit", visits, 2 * j) for j in range(1, peers)]
+    )
+    mine = exchange([piece] * peers, "visit", visits, 2)
     theirs = [flip(p, "visit", visits, 1) for p in mine]
     template, difference = call(
         lambda *refs: second_kernel(slots, side, tiles, strip, peers, *refs),
         (science, coef_second, rows_high, rows_low, across_high, across_low,
-         slot_tile, offsets, counts, tile_place, *mine, *theirs),
-        [shape(1, TILE, TILE), shape(1, slots, side, side)],
+         slot_tile, offsets, counts, tile_place, *map(near, mine), *map(near, theirs)),
+        [jax.ShapeDtypeStruct(d, F32) for d in ((1, TILE, TILE), (1, slots, side, side))],
         specs=[vmem] * 6 + [smem] * 4 + [vmem] * (2 * peers),
         scratch=scratch,
-        name="second",
     )
     return template, difference
 
@@ -370,4 +385,5 @@
         P(),
     )
     out_specs = (P("sky", None, None), P("visit", "sky", None, None))
+
     return jax.shard_map(body, mesh=mesh, in_specs=in_specs, out_specs=out_specs, check_vma=False)

time: 66.6 us -> 51.1 us (0.77)
  Pallas kernels: 18.8 us -> 10.2 us
  local copies, waits for them, and re-layouts: 6.7 us -> 0.7 us
  waiting for transfers between devices: 22.2 us -> 21 us
    pallas_call x6, Pallas kernels: 18.8 us -> 10.2 us  [call(): pl.pallas_call(function, out_shape=outs, in_specs=specs or [vmem] * len(i...]
    unnamed x39 -> x20, local copies, waits for them, and re-layouts: 6.7 us -> 0.7 us
    ppermute x17, waiting for transfers between devices: 22.2 us -> 21 us  [flip(): return lax.ppermute(value, axis, [(d, d ^ mask) for d in range(size)])]
  transfers between devices with their start and end apart: 17 -> 17, of which waited for: 12 -> 12; matrix products, arithmetic and copies ran while one was open for 1% -> 0% of each run, Pallas kernels for 0% -> 0%
where the time goes in v2:
time: 51.1 us; the launch traced here: 50.9 us
  waiting for transfers between devices  21 us (41%)
  starting transfers between devices  17.6 us (34%)
  Pallas kernels  10.2 us (20%)
  between operations  1.4 us (3%)
  local copies, waits for them, and re-layouts  0.7 us (1%)
    ppermute x17, waiting for transfers between devices, flip(): return lax.ppermute(value, axis, [(d, d ^ mask) for d in range(size)])  21 us
    ppermute x17, starting transfers between devices, flip(): return lax.ppermute(value, axis, [(d, d ^ mask) for d in range(size)])  17.6 us
    pallas_call x6, Pallas kernels, call(): pl.pallas_call(function, out_shape=outs, in_specs=specs or [vmem] * len(i...  10.2 us
  transfers between devices with their start and end apart: 17, of which 12 were waited for; matrix products, arithmetic and copies ran while one was open for 0% of the time, Pallas kernels for 0%

profile of v2, /device:TPU:0, one launch (start us, length us, event | category | flops | bytes accessed | tf_op | source)
XLA Modules:
  0.0 50.9 jit_solution(12670045684405350557)
XLA Ops:
  1.3 0.0 copy-start.8
  1.3 0.0 copy-start.9
  1.3 0.0 copy-start.6
  1.3 0.0 copy-start.7
  1.3 0.6 %copy-done.8 = s32[4]{0:T(128)S(1)} copy-done((s32[4]{0:T(128)S(1)}, s32[4]{0:T(128)}, u32[]{:S(2)}) %copy-start.8) | copy-done | bytes 40
  1.9 0.0 copy-done.9
  2.0 0.0 copy-done.6
  2.0 5.0 %shard_map.131 = (f32[1032,128]{1,0:T(8,128)S(1)}, f32[1032,128]{1,0:T(8,128)S(1)}) custom-call(f32[1,4,128,128]{3,2,1,0:T(8,128)} %refs_0_.3, f32[1,3,4,49]{3,2,1,0:T(4,128)} %bitcast.6, bf16[128,896]{1,0:T(8,128)(2,1)} %constant.10.clone.refs_2_, bf16[128,896]{1,0:T(8,128)(2,1)} %constant.11.clone.refs_3_, bf16[128,896]{1,0:T(8,128)(2,1)} %constant.8.clone.refs_4_, ...), custom_call_target="tpu_custom_call" | custom-call | tf_op jit(solution)/shard_map/pallas_call | solution.py:304
  7.0 0.6 %collective-permute-start = (f32[1032,128]{1,0:T(8,128)S(1)}, f32[1032,128]{1,0:T(8,128)S(1)}, u32[]{:S(2)}, u32[]{:S(2)}) collective-permute-start(f32[1032,128]{1,0:T(8,128)S(1)} %get-tuple-element.13), channel_id=1, source_target_pairs={{0,4},{4,0},{8,12},{12,8},{16,20},{20,16},{24,28},{28,24},{1,5},{5... | collective-permute-start | bytes 1585160 | tf_op jit(solution)/shard_map/ppermute | solution.py:323
  7.5 1.5 %collective-permute-done.refs_1_ = f32[1032,128]{1,0:T(8,128)S(1)} collective-permute-done((f32[1032,128]{1,0:T(8,128)S(1)}, f32[1032,128]{1,0:T(8,128)S(1)}, u32[]{:S(2)}, u32[]{:S(2)}) %collective-permute-start) | collective-permute-done | bytes 528416 | tf_op jit(solution)/shard_map/ppermute | solution.py:323
  9.1 0.1 shard_map.132
  9.2 2.9 %collective-permute-start.1 = (f32[264,128]{1,0:T(8,128)S(1)}, f32[264,128]{1,0:T(8,128)S(1)}, u32[]{:S(2)}, u32[]{:S(2)}) collective-permute-start(f32[264,128]{1,0:T(8,128)S(1)} %get-tuple-element.15), channel_id=1, source_target_pairs={{0,8},{4,12},{8,0},{12,4},{16,24},{20,28},{24,16},{28,20},{1,9},{5... | collective-permute-start | bytes 405512 | tf_op jit(solution)/shard_map/ppermute | solution.py:323
  12.1 1.5 %collective-permute-start.2 = (f32[264,128]{1,0:T(8,128)S(1)}, f32[264,128]{1,0:T(8,128)S(1)}, u32[]{:S(2)}, u32[]{:S(2)}) collective-permute-start(f32[264,128]{1,0:T(8,128)S(1)} %get-tuple-element.16), channel_id=1, source_target_pairs={{0,16},{4,20},{8,24},{12,28},{16,0},{20,4},{24,8},{28,12},{1,17},{... | collective-permute-start | bytes 405512 | tf_op jit(solution)/shard_map/ppermute | solution.py:323
  13.6 0.0 collective-permute-start.3
  13.6 2.6 %collective-permute-done.1.refs_1_ = f32[264,128]{1,0:T(8,128)S(1)} collective-permute-done((f32[264,128]{1,0:T(8,128)S(1)}, f32[264,128]{1,0:T(8,128)S(1)}, u32[]{:S(2)}, u32[]{:S(2)}) %collective-permute-start.1) | collective-permute-done | bytes 135200 | tf_op jit(solution)/shard_map/ppermute | solution.py:323
  16.2 4.1 %collective-permute-done.2.refs_2_ = f32[264,128]{1,0:T(8,128)S(1)} collective-permute-done((f32[264,128]{1,0:T(8,128)S(1)}, f32[264,128]{1,0:T(8,128)S(1)}, u32[]{:S(2)}, u32[]{:S(2)}) %collective-permute-start.2) | collective-permute-done | bytes 135200 | tf_op jit(solution)/shard_map/ppermute | solution.py:323
  20.3 0.0 collective-permute-done.3.refs_3_
  20.3 0.1 shard_map.133
  20.4 1.6 %collective-permute-start.4 = (f32[72,128]{1,0:T(8,128)S(1)}, f32[72,128]{1,0:T(8,128)S(1)}, u32[]{:S(2)}, u32[]{:S(2)}) collective-permute-start(f32[72,128]{1,0:T(8,128)S(1)} %get-tuple-element.19), channel_id=1, source_target_pairs={{0,1},{1,0},{2,3},{3,2},{4,5},{5,4},{6,7},{7,6},{8,9},{9,8},{10,11... | collective-permute-start | bytes 110600 | tf_op jit(solution)/shard_map/ppermute | solution.py:323
  22.0 2.6 %collective-permute-start.5 = (f32[72,128]{1,0:T(8,128)S(1)}, f32[72,128]{1,0:T(8,128)S(1)}, u32[]{:S(2)}, u32[]{:S(2)}) collective-permute-start(f32[72,128]{1,0:T(8,128)S(1)} %get-tuple-element.20), channel_id=1, source_target_pairs={{0,2},{1,3},{2,0},{3,1},{4,6},{5,7},{6,4},{7,5},{8,10},{9,11},{10,... | collective-permute-start | bytes 110600 | tf_op jit(solution)/shard_map/ppermute | solution.py:323
  24.6 0.2 collective-permute-start.6
  24.9 0.0 collective-permute-done.4.refs_1_
  24.9 2.4 %collective-permute-done.5.refs_2_ = f32[72,128]{1,0:T(8,128)S(1)} collective-permute-done((f32[72,128]{1,0:T(8,128)S(1)}, f32[72,128]{1,0:T(8,128)S(1)}, u32[]{:S(2)}, u32[]{:S(2)}) %collective-permute-start.5) | collective-permute-done | bytes 36896 | tf_op jit(solution)/shard_map/ppermute | solution.py:323
  27.2 3.1 %collective-permute-done.6.refs_3_ = f32[72,128]{1,0:T(8,128)S(1)} collective-permute-done((f32[72,128]{1,0:T(8,128)S(1)}, f32[72,128]{1,0:T(8,128)S(1)}, u32[]{:S(2)}, u32[]{:S(2)}) %collective-permute-start.6) | collective-permute-done | bytes 36896 | tf_op jit(solution)/shard_map/ppermute | solution.py:323
  30.4 0.2 shard_map.134.refs_0_
  30.6 0.5 collective-permute-start.9
  31.0 0.0 collective-permute-start.8
  31.1 4.0 %collective-permute-start.7 = (f32[64,128]{1,0:T(8,128)S(1)}, f32[64,128]{1,0:T(8,128)S(1)}, u32[]{:S(2)}, u32[]{:S(2)}) collective-permute-start(f32[64,128]{1,0:T(8,128)S(1)} %shard_map.134.refs_0_), channel_id=1, source_target_pairs={{0,1},{1,0},{2,3},{3,2},{4,5},{5,4},{6,7},{7,6},{8,9},{9,8},{10,11... | collective-permute-start | bytes 98312 | tf_op jit(solution)/shard_map/ppermute | solution.py:323
  35.0 1.3 %collective-permute-done.9.refs_3_ = f32[64,128]{1,0:T(8,128)S(1)} collective-permute-done((f32[64,128]{1,0:T(8,128)S(1)}, f32[64,128]{1,0:T(8,128)S(1)}, u32[]{:S(2)}, u32[]{:S(2)}) %collective-permute-start.9) | collective-permute-done | bytes 32800 | tf_op jit(solution)/shard_map/ppermute | solution.py:323
  36.4 0.0 collective-permute-done.8.refs_2_
  36.4 0.6 %collective-permute-done.7.refs_1_ = f32[64,128]{1,0:T(8,128)S(1)} collective-permute-done((f32[64,128]{1,0:T(8,128)S(1)}, f32[64,128]{1,0:T(8,128)S(1)}, u32[]{:S(2)}, u32[]{:S(2)}) %collective-permute-start.7) | collective-permute-done | bytes 32800 | tf_op jit(solution)/shard_map/ppermute | solution.py:323
  37.0 1.6 %collective-permute-start.12 = (f32[256,128]{1,0:T(8,128)S(1)}, f32[256,128]{1,0:T(8,128)S(1)}, u32[]{:S(2)}, u32[]{:S(2)}) collective-permute-start(f32[256,128]{1,0:T(8,128)S(1)} %shard_map.135.refs_10_), channel_id=1, source_target_pairs={{0,24},{4,28},{8,16},{12,20},{16,8},{20,12},{24,0},{28,4},{1,25},{... | collective-permute-start | bytes 393224 | tf_op jit(solution)/shard_map/ppermute | solution.py:323
  38.5 1.2 %collective-permute-start.11 = (f32[256,128]{1,0:T(8,128)S(1)}, f32[256,128]{1,0:T(8,128)S(1)}, u32[]{:S(2)}, u32[]{:S(2)}) collective-permute-start(f32[256,128]{1,0:T(8,128)S(1)} %shard_map.135.refs_10_), channel_id=1, source_target_pairs={{0,16},{4,20},{8,24},{12,28},{16,0},{20,4},{24,8},{28,12},{1,17},{... | collective-permute-start | bytes 393224 | tf_op jit(solution)/shard_map/ppermute | solution.py:323
  39.7 0.8 %collective-permute-start.10 = (f32[256,128]{1,0:T(8,128)S(1)}, f32[256,128]{1,0:T(8,128)S(1)}, u32[]{:S(2)}, u32[]{:S(2)}) collective-permute-start(f32[256,128]{1,0:T(8,128)S(1)} %shard_map.135.refs_10_), channel_id=1, source_target_pairs={{0,8},{4,12},{8,0},{12,4},{16,24},{20,28},{24,16},{28,20},{1,9},{5... | collective-permute-start | bytes 393224 | tf_op jit(solution)/shard_map/ppermute | solution.py:323
  40.5 0.0 collective-permute-start.13
  40.5 2.5 %collective-permute-done.12.refs_13_ = f32[256,128]{1,0:T(8,128)S(1)} collective-permute-done((f32[256,128]{1,0:T(8,128)S(1)}, f32[256,128]{1,0:T(8,128)S(1)}, u32[]{:S(2)}, u32[]{:S(2)}) %collective-permute-start.12) | collective-permute-done | bytes 131104 | tf_op jit(solution)/shard_map/ppermute | solution.py:323
  43.0 0.0 collective-permute-start.16
  43.0 1.3 %collective-permute-done.11.refs_12_ = f32[256,128]{1,0:T(8,128)S(1)} collective-permute-done((f32[256,128]{1,0:T(8,128)S(1)}, f32[256,128]{1,0:T(8,128)S(1)}, u32[]{:S(2)}, u32[]{:S(2)}) %collective-permute-start.11) | collective-permute-done | bytes 131104 | tf_op jit(solution)/shard_map/ppermute | solution.py:323
  44.3 0.0 collective-permute-start.15
  44.3 0.4 collective-permute-done.10.refs_11_
  44.7 0.1 collective-permute-start.14
  44.8 0.0 collective-permute-done.13.refs_14_
  44.8 0.0 collective-permute-done.16.refs_17_
  44.8 0.8 %collective-permute-done.15.refs_16_ = f32[256,128]{1,0:T(8,128)S(1)} collective-permute-done((f32[256,128]{1,0:T(8,128)S(1)}, f32[256,128]{1,0:T(8,128)S(1)}, u32[]{:S(2)}, u32[]{:S(2)}) %collective-permute-start.15) | collective-permute-done | bytes 131104 | tf_op jit(solution)/shard_map/ppermute | solution.py:323
  45.6 0.4 collective-permute-done.14.refs_15_
  46.0 0.0 copy-done.4
  46.0 0.0 copy-done.2
  46.1 4.8 %shard_map.136 = (f32[1,256,256]{2,1,0:T(8,128)}, f32[1,4,128,128]{3,2,1,0:T(8,128)}) custom-call(f32[1,4,128,128]{3,2,1,0:T(8,128)S(1)} %copy-done, f32[1,3,4,49]{3,2,1,0:T(4,128)S(1)} %bitcast.3, bf16[128,896]{1,0:T(8,128)(2,1)S(1)} %copy-done.2, bf16[128,896]{1,0:T(8,128)(2,1)S(1)} %copy-done.1, bf16[128,896]{1,0:T(8,128)(2,1)S(1)} %copy-done.4, ...), custom_call_target="tpu_custom_call" | custom-call | tf_op jit(solution)/shard_map/pallas_call | solution.py:304
  (12 shorter events, 0.0 us)
Async XLA Ops:
  1.3 0.7 %copy-start.8 = (s32[4]{0:T(128)S(1)}, s32[4]{0:T(128)}, u32[]{:S(2)}) copy-start(s32[4]{0:T(128)} %refs_9_.2) | copy-start | bytes 52
  1.3 0.7 %copy-start.9 = (f32[1,4]{1,0:T(1,128)S(1)}, f32[1,4]{1,0:T(1,128)}, u32[]{:S(2)}) copy-start(f32[1,4]{1,0:T(1,128)} %refs_6_.2) | copy-start | bytes 52
  1.3 0.7 %copy-start.6 = (s32[1,4,2]{1,2,0:T(2,128)S(1)}, s32[1,4,2]{1,2,0:T(2,128)}, u32[]{:S(2)}) copy-start(s32[1,4,2]{1,2,0:T(2,128)} %param.17) | copy-start | bytes 100
  1.3 0.7 %copy-start.7 = (s32[1,4]{1,0:T(1,128)S(1)}, s32[1,4]{1,0:T(1,128)}, u32[]{:S(2)}) copy-start(s32[1,4]{1,0:T(1,128)} %refs_6_.3) | copy-start | bytes 52
  7.0 2.1 %collective-permute-start = (f32[1032,128]{1,0:T(8,128)S(1)}, f32[1032,128]{1,0:T(8,128)S(1)}, u32[]{:S(2)}, u32[]{:S(2)}) collective-permute-start(f32[1032,128]{1,0:T(8,128)S(1)} %get-tuple-element.13), channel_id=1, source_target_pairs={{0,4},{4,0},{8,12},{12,8},{16,20},{20,16},{24,28},{28,24},{1,5},{5... | collective-permute-start | bytes 1585160 | tf_op jit(solution)/shard_map/ppermute | solution.py:323
  9.1 36.9 %copy-start.4 = (bf16[128,896]{1,0:T(8,128)(2,1)S(1)}, bf16[128,896]{1,0:T(8,128)(2,1)}, u32[]{:S(2)}) copy-start(bf16[128,896]{1,0:T(8,128)(2,1)} %constant.8.clone.refs_4_) | copy-start | bytes 688132
  9.2 7.1 %collective-permute-start.1 = (f32[264,128]{1,0:T(8,128)S(1)}, f32[264,128]{1,0:T(8,128)S(1)}, u32[]{:S(2)}, u32[]{:S(2)}) collective-permute-start(f32[264,128]{1,0:T(8,128)S(1)} %get-tuple-element.15), channel_id=1, source_target_pairs={{0,8},{4,12},{8,0},{12,4},{16,24},{20,28},{24,16},{28,20},{1,9},{5... | collective-permute-start | bytes 405512 | tf_op jit(solution)/shard_map/ppermute | solution.py:323
  12.1 8.2 %collective-permute-start.2 = (f32[264,128]{1,0:T(8,128)S(1)}, f32[264,128]{1,0:T(8,128)S(1)}, u32[]{:S(2)}, u32[]{:S(2)}) collective-permute-start(f32[264,128]{1,0:T(8,128)S(1)} %get-tuple-element.16), channel_id=1, source_target_pairs={{0,16},{4,20},{8,24},{12,28},{16,0},{20,4},{24,8},{28,12},{1,17},{... | collective-permute-start | bytes 405512 | tf_op jit(solution)/shard_map/ppermute | solution.py:323
  13.6 6.7 %collective-permute-start.3 = (f32[264,128]{1,0:T(8,128)S(1)}, f32[264,128]{1,0:T(8,128)S(1)}, u32[]{:S(2)}, u32[]{:S(2)}) collective-permute-start(f32[264,128]{1,0:T(8,128)S(1)} %get-tuple-element.17), channel_id=1, source_target_pairs={{0,24},{4,28},{8,16},{12,20},{16,8},{20,12},{24,0},{28,4},{1,25},{... | collective-permute-start | bytes 405512 | tf_op jit(solution)/shard_map/ppermute | solution.py:323
  20.3 25.7 %copy-start.1 = (bf16[128,896]{1,0:T(8,128)(2,1)S(1)}, bf16[128,896]{1,0:T(8,128)(2,1)}, u32[]{:S(2)}) copy-start(bf16[128,896]{1,0:T(8,128)(2,1)} %constant.11.clone.refs_3_) | copy-start | bytes 688132
  20.3 25.7 %copy-start.2 = (bf16[128,896]{1,0:T(8,128)(2,1)S(1)}, bf16[128,896]{1,0:T(8,128)(2,1)}, u32[]{:S(2)}) copy-start(bf16[128,896]{1,0:T(8,128)(2,1)} %constant.10.clone.refs_2_) | copy-start | bytes 688132
  20.3 25.7 %copy-start.3 = (bf16[128,896]{1,0:T(8,128)(2,1)S(1)}, bf16[128,896]{1,0:T(8,128)(2,1)}, u32[]{:S(2)}) copy-start(bf16[128,896]{1,0:T(8,128)(2,1)} %constant.9.clone.refs_5_) | copy-start | bytes 688132
  20.4 25.7 %copy-start = (f32[1,4,128,128]{3,2,1,0:T(8,128)S(1)}, f32[1,4,128,128]{3,2,1,0:T(8,128)}, u32[]{:S(2)}) copy-start(f32[1,4,128,128]{3,2,1,0:T(8,128)} %refs_0_.3) | copy-start | bytes 786436
  20.4 4.5 %collective-permute-start.4 = (f32[72,128]{1,0:T(8,128)S(1)}, f32[72,128]{1,0:T(8,128)S(1)}, u32[]{:S(2)}, u32[]{:S(2)}) collective-permute-start(f32[72,128]{1,0:T(8,128)S(1)} %get-tuple-element.19), channel_id=1, source_target_pairs={{0,1},{1,0},{2,3},{3,2},{4,5},{5,4},{6,7},{7,6},{8,9},{9,8},{10,11... | collective-permute-start | bytes 110600 | tf_op jit(solution)/shard_map/ppermute | solution.py:323
  22.0 5.2 %collective-permute-start.5 = (f32[72,128]{1,0:T(8,128)S(1)}, f32[72,128]{1,0:T(8,128)S(1)}, u32[]{:S(2)}, u32[]{:S(2)}) collective-permute-start(f32[72,128]{1,0:T(8,128)S(1)} %get-tuple-element.20), channel_id=1, source_target_pairs={{0,2},{1,3},{2,0},{3,1},{4,6},{5,7},{6,4},{7,5},{8,10},{9,11},{10,... | collective-permute-start | bytes 110600 | tf_op jit(solution)/shard_map/ppermute | solution.py:323
  24.6 5.8 %collective-permute-start.6 = (f32[72,128]{1,0:T(8,128)S(1)}, f32[72,128]{1,0:T(8,128)S(1)}, u32[]{:S(2)}, u32[]{:S(2)}) collective-permute-start(f32[72,128]{1,0:T(8,128)S(1)} %get-tuple-element.21), channel_id=1, source_target_pairs={{0,3},{1,2},{2,1},{3,0},{4,7},{5,6},{6,5},{7,4},{8,11},{9,10},{10,... | collective-permute-start | bytes 110600 | tf_op jit(solution)/shard_map/ppermute | solution.py:323
  30.6 5.8 %collective-permute-start.9 = (f32[64,128]{1,0:T(8,128)S(1)}, f32[64,128]{1,0:T(8,128)S(1)}, u32[]{:S(2)}, u32[]{:S(2)}) collective-permute-start(f32[64,128]{1,0:T(8,128)S(1)} %shard_map.134.refs_0_), channel_id=1, source_target_pairs={{0,3},{1,2},{2,1},{3,0},{4,7},{5,6},{6,5},{7,4},{8,11},{9,10},{10,... | collective-permute-start | bytes 98312 | tf_op jit(solution)/shard_map/ppermute | solution.py:323
  31.0 5.3 %collective-permute-start.8 = (f32[64,128]{1,0:T(8,128)S(1)}, f32[64,128]{1,0:T(8,128)S(1)}, u32[]{:S(2)}, u32[]{:S(2)}) collective-permute-start(f32[64,128]{1,0:T(8,128)S(1)} %shard_map.134.refs_0_), channel_id=1, source_target_pairs={{0,2},{1,3},{2,0},{3,1},{4,6},{5,7},{6,4},{7,5},{8,10},{9,11},{10,... | collective-permute-start | bytes 98312 | tf_op jit(solution)/shard_map/ppermute | solution.py:323
  31.1 5.9 %collective-permute-start.7 = (f32[64,128]{1,0:T(8,128)S(1)}, f32[64,128]{1,0:T(8,128)S(1)}, u32[]{:S(2)}, u32[]{:S(2)}) collective-permute-start(f32[64,128]{1,0:T(8,128)S(1)} %shard_map.134.refs_0_), channel_id=1, source_target_pairs={{0,1},{1,0},{2,3},{3,2},{4,5},{5,4},{6,7},{7,6},{8,9},{9,8},{10,11... | collective-permute-start | bytes 98312 | tf_op jit(solution)/shard_map/ppermute | solution.py:323
  36.9 9.1 %copy-start.5 = (f32[1,4,3,49]{3,1,2,0:T(4,128)S(1)}, f32[1,4,3,49]{3,1,2,0:T(4,128)}, u32[]{:S(2)}) copy-start(f32[1,4,3,49]{3,1,2,0:T(4,128)} %param.14) | copy-start | bytes 7060
  37.0 6.0 %collective-permute-start.12 = (f32[256,128]{1,0:T(8,128)S(1)}, f32[256,128]{1,0:T(8,128)S(1)}, u32[]{:S(2)}, u32[]{:S(2)}) collective-permute-start(f32[256,128]{1,0:T(8,128)S(1)} %shard_map.135.refs_10_), channel_id=1, source_target_pairs={{0,24},{4,28},{8,16},{12,20},{16,8},{20,12},{24,0},{28,4},{1,25},{... | collective-permute-start | bytes 393224 | tf_op jit(solution)/shard_map/ppermute | solution.py:323
  38.5 5.8 %collective-permute-start.11 = (f32[256,128]{1,0:T(8,128)S(1)}, f32[256,128]{1,0:T(8,128)S(1)}, u32[]{:S(2)}, u32[]{:S(2)}) collective-permute-start(f32[256,128]{1,0:T(8,128)S(1)} %shard_map.135.refs_10_), channel_id=1, source_target_pairs={{0,16},{4,20},{8,24},{12,28},{16,0},{20,4},{24,8},{28,12},{1,17},{... | collective-permute-start | bytes 393224 | tf_op jit(solution)/shard_map/ppermute | solution.py:323
  39.7 5.0 %collective-permute-start.10 = (f32[256,128]{1,0:T(8,128)S(1)}, f32[256,128]{1,0:T(8,128)S(1)}, u32[]{:S(2)}, u32[]{:S(2)}) collective-permute-start(f32[256,128]{1,0:T(8,128)S(1)} %shard_map.135.refs_10_), channel_id=1, source_target_pairs={{0,8},{4,12},{8,0},{12,4},{16,24},{20,28},{24,16},{28,20},{1,9},{5... | collective-permute-start | bytes 393224 | tf_op jit(solution)/shard_map/ppermute | solution.py:323
  40.5 4.3 %collective-permute-start.13 = (f32[256,128]{1,0:T(8,128)S(1)}, f32[256,128]{1,0:T(8,128)S(1)}, u32[]{:S(2)}, u32[]{:S(2)}) collective-permute-start(f32[256,128]{1,0:T(8,128)S(1)} %shard_map.135.refs_10_), channel_id=1, source_target_pairs={{0,4},{4,0},{8,12},{12,8},{16,20},{20,16},{24,28},{28,24},{1,5},{5... | collective-permute-start | bytes 393224 | tf_op jit(solution)/shard_map/ppermute | solution.py:323
  43.0 1.8 %collective-permute-start.16 = (f32[256,128]{1,0:T(8,128)S(1)}, f32[256,128]{1,0:T(8,128)S(1)}, u32[]{:S(2)}, u32[]{:S(2)}) collective-permute-start(f32[256,128]{1,0:T(8,128)S(1)} %collective-permute-done.12.refs_13_), channel_id=1, source_target_pairs={{0,4},{4,0},{8,12},{12,8},{16,20},{20,16},{24,28},{28,24},{1,5},{5... | collective-permute-start | bytes 393224 | tf_op jit(solution)/shard_map/ppermute | solution.py:323
  44.3 1.3 %collective-permute-start.15 = (f32[256,128]{1,0:T(8,128)S(1)}, f32[256,128]{1,0:T(8,128)S(1)}, u32[]{:S(2)}, u32[]{:S(2)}) collective-permute-start(f32[256,128]{1,0:T(8,128)S(1)} %collective-permute-done.11.refs_12_), channel_id=1, source_target_pairs={{0,4},{4,0},{8,12},{12,8},{16,20},{20,16},{24,28},{28,24},{1,5},{5... | collective-permute-start | bytes 393224 | tf_op jit(solution)/shard_map/ppermute | solution.py:323
  44.7 1.3 %collective-permute-start.14 = (f32[256,128]{1,0:T(8,128)S(1)}, f32[256,128]{1,0:T(8,128)S(1)}, u32[]{:S(2)}, u32[]{:S(2)}) collective-permute-start(f32[256,128]{1,0:T(8,128)S(1)} %collective-permute-done.10.refs_11_), channel_id=1, source_target_pairs={{0,4},{4,0},{8,12},{12,8},{16,20},{20,16},{24,28},{28,24},{1,5},{5... | collective-permute-start | bytes 393224 | tf_op jit(solution)/shard_map/ppermute | solution.py:323

commit v3 on v2

--- a/solution.py
+++ b/solution.py
@@ -27,7 +27,7 @@
     return high, low
 
 
-def constants(side):
+def constants(side, basis):
     reach = (TAPS - 1) // 2
     support = np.arange(TAPS).astype(np.float64) - reach
     taps = []
@@ -43,7 +43,7 @@
     across = np.concatenate(
         [np.where(inside, t[np.clip(spacing + reach, 0, TAPS - 1)], 0.0) for t in taps], axis=1
     )
-    rows = np.zeros((LANES, PROFILES * side), np.float64)
+    rows = np.zeros((-(-basis // 64) * 64, PROFILES * side), np.float64)
     for i in range(PROFILES):
         for j in range(PROFILES):
             for t in range(-reach, reach + 1):
@@ -51,6 +51,10 @@
     return split_np(across) + split_np(rows)
 
 
+def row_pitch(slots):
+    return -(-slots // 8) * 8
+
+
 def split(values):
     high = values.astype(BF16)
     low = (values - high.astype(F32)).astype(BF16)
@@ -61,10 +65,6 @@
     return jnp.dot(a, b, preferred_element_type=F32)
 
 
-def mm3(a_high, a_low, b_high, b_low):
-    return mm(a_high, b_high) + (mm(a_high, b_low) + mm(a_low, b_high))
-
-
 def spread_along(shape, axis, side):
     places = lax.broadcasted_iota(jnp.int32, shape, axis).astype(F32)
     return (2.0 * places - (side - 1)) / (side - 1)
@@ -73,21 +73,24 @@
 def tap_rows(coef_ref, coef_buf, tap_buf, rows_high, rows_low, slots):
     coef_buf[...] = jnp.zeros(coef_buf.shape, F32)
     basis = coef_ref.shape[-1]
-    pitch = coef_buf.shape[0] // 3
+    depth = rows_high.shape[0]
+    pitch = row_pitch(slots)
+    rows = coef_buf.shape[0]
     for k in range(3):
         coef_buf[pl.ds(pitch * k, slots), pl.ds(0, basis)] = coef_ref[0, k]
-    high, low = split(coef_buf[...])
-    tap_buf[...] = mm3(high, low, rows_high[...], rows_low[...])
-
-
-def kernel_pass(block, b, tap_buf, across_high, across_low, left_high, left_low, side):
+    high, low = split(coef_buf[:, :depth])
+    both = mm(jnp.concatenate([high, low], axis=0), rows_high[...])
+    tap_buf[...] = both[:rows] + (both[rows:] + mm(high, rows_low[...]))
+
+
+def build_left(b, slots, side, tap_buf, left):
     reach = (TAPS - 1) // 2
     square = (side, side)
     row = lax.broadcasted_iota(jnp.int32, square, 0)
     col = lax.broadcasted_iota(jnp.int32, square, 1)
     band = jnp.abs(col - row) <= reach
     spread_y = spread_along(square, 0, side)
-    pitch = tap_buf.shape[0] // 3
+    pitch = row_pitch(slots)
     for i in range(PROFILES):
         lanes = slice(i * side, (i + 1) * side)
         plain = jnp.broadcast_to(tap_buf[b : b + 1, lanes], square)
@@ -96,16 +99,36 @@
         for part, taps in ((0, plain + along * spread_y), (1, sideways)):
             rolled = pltpu.roll(taps, 0, 1, stride=1, stride_axis=0)
             high, low = split(jnp.where(band, rolled, 0.0))
-            left_high[part * side : (part + 1) * side, lanes] = high
-            left_low[part * side : (part + 1) * side, lanes] = low
-    block_high, block_low = split(block)
-    across = mm3(block_high, block_low, across_high[...], across_low[...])
-    stacked = jnp.concatenate(
-        [across[:, i * side : (i + 1) * side] for i in range(PROFILES)], axis=0
-    )
-    stacked_high, stacked_low = split(stacked)
-    both = mm3(left_high[...], left_low[...], stacked_high, stacked_low)
-    return both[:side] + both[side:] * spread_along(square, 1, side)
+            left[b, part * side : (part + 1) * side, lanes] = high
+            left[b, (part + 2) * side : (part + 3) * side, lanes] = low
+
+
+def put_block(block, b, side, images):
+    high, low = split(block)
+    images[b * side : (b + 1) * side, :side] = high
+    images[b * side : (b + 1) * side, side:] = low
+
+
+def across_stage(slots, side, images, across_high, across_low, right):
+    for first in range(0, PROFILES, 2):
+        last = min(first + 2, PROFILES)
+        lanes = slice(first * side, last * side)
+        high = across_high[:, lanes]
+        doubled = jnp.concatenate([high, high], axis=0)
+        result = mm(images[...], doubled) + mm(images[:, :side], across_low[:, lanes])
+        for i in range(first, last):
+            part_high, part_low = split(result[:, (i - first) * side : (i - first + 1) * side])
+            for b in range(slots):
+                rows = slice(i * side, (i + 1) * side)
+                right[b, rows, :side] = part_high[b * side : (b + 1) * side]
+                right[b, rows, side:] = part_low[b * side : (b + 1) * side]
+
+
+def down_stage(b, side, left, right):
+    result = mm(left[b], right[b])
+    half = 2 * side
+    both = result[:half, :side] + (result[:half, side:] + result[half:, :side])
+    return both[:side] + both[side:] * spread_along((side, side), 1, side)
 
 
 def first_kernel(
@@ -113,7 +136,7 @@
     science, coef, rows_high, rows_low, across_high, across_low,
     weight, slot_tile, offsets, counts, tile_place,
     keep, send,
-    coef_buf, tap_buf, left_high, left_low, total,
+    coef_buf, tap_buf, left, images, right, total,
 ):
     visit = lax.axis_index("visit")
     sky = lax.axis_index("sky")
@@ -121,6 +144,10 @@
     half = TILE // 2
     sky_size = tiles
     tap_rows(coef, coef_buf, tap_buf, rows_high, rows_low, slots)
+    for b in range(slots):
+        put_block(science[0, b], b, side, images)
+        build_left(b, slots, side, tap_buf, left)
+    across_stage(slots, side, images, across_high, across_low, right)
     total[...] = jnp.zeros(total.shape, F32)
     first_lane = (visit * sky_size + sky) * slots
     lane = lax.broadcasted_iota(jnp.int32, (META, LANES), 1)
@@ -132,25 +159,23 @@
         usable = b < counts[0, 0]
         used = jnp.where(usable, weight[0, b], 0.0)
         top = offsets[0, 0, b]
-        left = offsets[0, 1, b]
+        left_edge = offsets[0, 1, b]
         entry = jnp.where(
             field == 0,
             used,
             jnp.where(
                 field == 1,
                 top.astype(F32),
-                jnp.where(field == 2, left.astype(F32), jnp.where(field == 3, owner.astype(F32), 0.0)),
+                jnp.where(field == 2, left_edge.astype(F32), jnp.where(field == 3, owner.astype(F32), 0.0)),
             ),
         )
         for m in range(meta_blocks):
             meta[m] = jnp.where(lane + m * LANES == first_lane + b, entry, meta[m])
-        image = kernel_pass(
-            science[0, b], b, tap_buf, across_high, across_low, left_high, left_low, side
-        )
+        image = down_stage(b, side, left, right)
         image = jnp.where(usable, image * used, 0.0)
-        moved = pltpu.roll(image, left, 1)
-        total[owner, 0, pl.ds(top, side), :] += jnp.where(col >= left, moved, 0.0)
-        total[owner, 1, pl.ds(top, side), :] += jnp.where(col < left, moved, 0.0)
+        moved = pltpu.roll(image, left_edge, 1)
+        total[owner, 0, pl.ds(top, side), :] += jnp.where(col >= left_edge, moved, 0.0)
+        total[owner, 1, pl.ds(top, side), :] += jnp.where(col < left_edge, moved, 0.0)
     body = tiles * 2 * half
     for t in range(tiles):
         for h in range(2):
@@ -234,19 +259,18 @@
 
 def second_kernel(
     slots, side, tiles, strip, peers,
-    science, coef, rows_high, rows_low, across_high, across_low,
+    science, left, across_high, across_low,
     slot_tile, offsets, counts, tile_place,
     *refs,
 ):
     pieces = refs[: 2 * peers]
     template, difference = refs[2 * peers : 2 * peers + 2]
-    coef_buf, tap_buf, left_high, left_low, total = refs[2 * peers + 2 :]
+    images, right, total = refs[2 * peers + 2 :]
     visit = lax.axis_index("visit")
     sky = lax.axis_index("sky")
     core = visit % 2
     place = visit // 2
     half = TILE // 2
-    tap_rows(coef, coef_buf, tap_buf, rows_high, rows_low, slots)
     for c in range(2):
         for j in range(peers):
             first = (core ^ c) * half + (place ^ j) * strip
@@ -260,21 +284,27 @@
     col = lax.broadcasted_iota(jnp.int32, (side, side), 1)
     for b in range(slots):
         owner = tile_place[slot_tile[0, b]]
-        usable = b < counts[0, 0]
         top = offsets[0, 0, b]
-        left = offsets[0, 1, b]
+        left_edge = offsets[0, 1, b]
         joined = jnp.where(
-            col >= left, total[owner, 0, pl.ds(top, side), :], total[owner, 1, pl.ds(top, side), :]
+            col >= left_edge, total[owner, 0, pl.ds(top, side), :], total[owner, 1, pl.ds(top, side), :]
         )
-        cutout = pltpu.roll(joined, (side - left) % side, 1)
-        matched = kernel_pass(
-            cutout, b, tap_buf, across_high, across_low, left_high, left_low, side
-        )
-        difference[0, b] = jnp.where(usable, science[0, b] - matched, 0.0)
+        put_block(pltpu.roll(joined, (side - left_edge) % side, 1), b, side, images)
+    across_stage(slots, side, images, across_high, across_low, right)
+    for b in range(slots):
+        matched = down_stage(b, side, left, right)
+        difference[0, b] = jnp.where(b < counts[0, 0], science[0, b] - matched, 0.0)
+
+
+def prepare_kernel(slots, side, coef, rows_high, rows_low, left, coef_buf, tap_buf):
+    tap_rows(coef, coef_buf, tap_buf, rows_high, rows_low, slots)
+    for b in range(slots):
+        build_left(b, slots, side, tap_buf, left)
 
 
 def body(science, coef_first, coef_second, weight, slot_tile, offsets, counts, tile_place):
     slots, side = science.shape[1], science.shape[2]
+    basis = coef_first.shape[-1]
     visits = lax.axis_size("visit")
     tiles = lax.axis_size("sky")
     peers = visits // 2
@@ -282,7 +312,7 @@
     meta_blocks = -(-visits * tiles * slots // LANES)
     meta_rows = meta_blocks * META
     across_high, across_low, rows_high, rows_low = (
-        jnp.asarray(c) for c in constants(side)
+        jnp.asarray(c) for c in constants(side, basis)
     )
     vmem = pl.BlockSpec(memory_space=pltpu.VMEM)
     smem = pl.BlockSpec(memory_space=pltpu.SMEM)
@@ -310,12 +340,14 @@
             compiler_params=pltpu.CompilerParams(vmem_limit_bytes=VMEM_BYTES),
         )(*ins)
 
-    pitch = -(-slots // 8) * 8
-    scratch = [
-        pltpu.VMEM((3 * pitch, LANES), F32),
-        pltpu.VMEM((3 * pitch, PROFILES * side), F32),
-        pltpu.VMEM((2 * side, PROFILES * side), BF16),
-        pltpu.VMEM((2 * side, PROFILES * side), BF16),
+    tap_scratch = [
+        pltpu.VMEM((-(-3 * row_pitch(slots) // 16) * 16, LANES), F32),
+        pltpu.VMEM((-(-3 * row_pitch(slots) // 16) * 16, PROFILES * side), F32),
+    ]
+    left_shape = (slots, 4 * side, PROFILES * side)
+    pass_scratch = [
+        pltpu.VMEM((slots * side, 2 * side), BF16),
+        pltpu.VMEM((slots, PROFILES * side, 2 * side), BF16),
         pltpu.VMEM((tiles, 2, TILE, LANES), F32),
     ]
 
@@ -331,10 +363,16 @@
     keep, send = call(
         lambda *refs: first_kernel(slots, side, tiles, meta_blocks, *refs),
         (*map(far, (science, coef_first, rows_high, rows_low, across_high, across_low)),
-         weight, slot_tile, offsets, counts, tile_place),
+         *map(far, (weight, slot_tile, offsets)), counts, far(tile_place)),
         [shape(tiles * TILE + meta_rows, LANES)] * 2,
         specs=[vmem] * 6 + [smem] * 5,
-        scratch=scratch,
+        scratch=tap_scratch + [pltpu.VMEM(left_shape, BF16)] + pass_scratch,
+    )
+    left = call(
+        lambda *refs: prepare_kernel(slots, side, *refs),
+        (coef_second, rows_high, rows_low),
+        pltpu.VMEM(left_shape, BF16),
+        scratch=tap_scratch,
     )
     received = flip(send, "visit", visits, 1)
     pieces = call(
@@ -364,11 +402,11 @@
     theirs = [flip(p, "visit", visits, 1) for p in mine]
     template, difference = call(
         lambda *refs: second_kernel(slots, side, tiles, strip, peers, *refs),
-        (science, coef_second, rows_high, rows_low, across_high, across_low,
+        (science, near(left), across_high, across_low,
          slot_tile, offsets, counts, tile_place, *map(near, mine), *map(near, theirs)),
         [jax.ShapeDtypeStruct(d, F32) for d in ((1, TILE, TILE), (1, slots, side, side))],
-        specs=[vmem] * 6 + [smem] * 4 + [vmem] * (2 * peers),
-        scratch=scratch,
+        specs=[vmem] * 4 + [smem] * 4 + [vmem] * (2 * peers),
+        scratch=pass_scratch,
     )
     return template, difference
 

time: 51.1 us -> 50.2 us (0.982)
  local copies, waits for them, and re-layouts: 0.7 us -> 2.52 us
  Pallas kernels: 10.2 us -> 8.43 us
  waiting for transfers between devices: 21 us -> 19.8 us
    unnamed x20 -> x18, local copies, waits for them, and re-layouts: 0.7 us -> 2.52 us
    pallas_call x6 -> x7, Pallas kernels: 10.2 us -> 8.43 us  [call(): pl.pallas_call(function, out_shape=outs, in_specs=specs or [vmem] * len(i...]
    ppermute x17, waiting for transfers between devices: 21 us -> 19.8 us  [flip(): return lax.ppermute(value, axis, [(d, d ^ mask) for d in range(size)])]
  transfers between devices with their start and end apart: 17 -> 17, of which waited for: 12 -> 10; matrix products, arithmetic and copies ran while one was open for 0% -> 0% of each run, Pallas kernels for 0% -> 2%
where the time goes in v3:
time: 50.2 us; the launch traced here: 49.9 us
  waiting for transfers between devices  19.8 us (39%)
  starting transfers between devices  17.6 us (35%)
  Pallas kernels  8.43 us (17%)
  local copies, waits for them, and re-layouts  2.52 us (5%)
  between operations  1.53 us (3%)
    ppermute x17, waiting for transfers between devices, flip(): return lax.ppermute(value, axis, [(d, d ^ mask) for d in range(size)])  19.8 us
    ppermute x17, starting transfers between devices, flip(): return lax.ppermute(value, axis, [(d, d ^ mask) for d in range(size)])  17.6 us
    pallas_call x7, Pallas kernels, call(): pl.pallas_call(function, out_shape=outs, in_specs=specs or [vmem] * len(i...  8.43 us
    unnamed x18, local copies, waits for them, and re-layouts  2.52 us
  transfers between devices with their start and end apart: 17, of which 10 were waited for; matrix products, arithmetic and copies ran while one was open for 0% of the time, Pallas kernels for 2%

profile of v3, /device:TPU:0, one launch (start us, length us, event | category | flops | bytes accessed | tf_op | source)
XLA Modules:
  0.0 49.9 jit_solution(840918449324219687)
XLA Ops:
  0.6 0.0 copy-start.1
  0.6 0.0 copy-start.2
  0.7 0.0 copy-start.8
  0.7 0.0 copy-start.7
  0.7 0.0 copy-start
  0.7 0.0 copy-start.6
  1.4 3.6 %shard_map.132 = (f32[1032,128]{1,0:T(8,128)S(1)}, f32[1032,128]{1,0:T(8,128)S(1)}) custom-call(f32[1,4,128,128]{3,2,1,0:T(8,128)} %refs_0_.3, f32[1,3,4,49]{3,2,1,0:T(4,128)} %bitcast.6, bf16[64,896]{1,0:T(8,128)(2,1)} %constant.10.clone.refs_1_.refs_2_, bf16[64,896]{1,0:T(8,128)(2,1)} %constant.11.clone.refs_2_.refs_3_, ...), custom_call_target="tpu_custom_call" | custom-call | tf_op jit(solution)/shard_map/pallas_call | solution.py:334
  5.0 0.6 %collective-permute-start = (f32[1032,128]{1,0:T(8,128)S(1)}, f32[1032,128]{1,0:T(8,128)S(1)}, u32[]{:S(2)}, u32[]{:S(2)}) collective-permute-start(f32[1032,128]{1,0:T(8,128)S(1)} %get-tuple-element.13), channel_id=1, source_target_pairs={{0,4},{4,0},{8,12},{12,8},{16,20},{20,16},{24,28},{28,24},{1,5},{5... | collective-permute-start | bytes 1585160 | tf_op jit(solution)/shard_map/ppermute | solution.py:355
  5.6 1.5 %collective-permute-done.refs_1_ = f32[1032,128]{1,0:T(8,128)S(1)} collective-permute-done((f32[1032,128]{1,0:T(8,128)S(1)}, f32[1032,128]{1,0:T(8,128)S(1)}, u32[]{:S(2)}, u32[]{:S(2)}) %collective-permute-start) | collective-permute-done | bytes 528416 | tf_op jit(solution)/shard_map/ppermute | solution.py:355
  7.2 0.1 shard_map.133
  7.2 2.9 %collective-permute-start.1 = (f32[264,128]{1,0:T(8,128)S(1)}, f32[264,128]{1,0:T(8,128)S(1)}, u32[]{:S(2)}, u32[]{:S(2)}) collective-permute-start(f32[264,128]{1,0:T(8,128)S(1)} %get-tuple-element.15), channel_id=1, source_target_pairs={{0,8},{4,12},{8,0},{12,4},{16,24},{20,28},{24,16},{28,20},{1,9},{5... | collective-permute-start | bytes 405512 | tf_op jit(solution)/shard_map/ppermute | solution.py:355
  10.1 1.5 %collective-permute-start.2 = (f32[264,128]{1,0:T(8,128)S(1)}, f32[264,128]{1,0:T(8,128)S(1)}, u32[]{:S(2)}, u32[]{:S(2)}) collective-permute-start(f32[264,128]{1,0:T(8,128)S(1)} %get-tuple-element.16), channel_id=1, source_target_pairs={{0,16},{4,20},{8,24},{12,28},{16,0},{20,4},{24,8},{28,12},{1,17},{... | collective-permute-start | bytes 405512 | tf_op jit(solution)/shard_map/ppermute | solution.py:355
  11.7 0.0 collective-permute-start.3
  11.7 2.6 %collective-permute-done.1.refs_1_ = f32[264,128]{1,0:T(8,128)S(1)} collective-permute-done((f32[264,128]{1,0:T(8,128)S(1)}, f32[264,128]{1,0:T(8,128)S(1)}, u32[]{:S(2)}, u32[]{:S(2)}) %collective-permute-start.1) | collective-permute-done | bytes 135200 | tf_op jit(solution)/shard_map/ppermute | solution.py:355
  14.3 4.1 %collective-permute-done.2.refs_2_ = f32[264,128]{1,0:T(8,128)S(1)} collective-permute-done((f32[264,128]{1,0:T(8,128)S(1)}, f32[264,128]{1,0:T(8,128)S(1)}, u32[]{:S(2)}, u32[]{:S(2)}) %collective-permute-start.2) | collective-permute-done | bytes 135200 | tf_op jit(solution)/shard_map/ppermute | solution.py:355
  18.4 0.0 collective-permute-done.3.refs_3_
  18.4 1.6 %collective-permute-start.4 = (f32[72,128]{1,0:T(8,128)S(1)}, f32[72,128]{1,0:T(8,128)S(1)}, u32[]{:S(2)}, u32[]{:S(2)}) collective-permute-start(f32[72,128]{1,0:T(8,128)S(1)} %get-tuple-element.19), channel_id=1, source_target_pairs={{0,1},{1,0},{2,3},{3,2},{4,5},{5,4},{6,7},{7,6},{8,9},{9,8},{10,11... | collective-permute-start | bytes 110600 | tf_op jit(solution)/shard_map/ppermute | solution.py:355
  20.1 2.6 %collective-permute-start.5 = (f32[72,128]{1,0:T(8,128)S(1)}, f32[72,128]{1,0:T(8,128)S(1)}, u32[]{:S(2)}, u32[]{:S(2)}) collective-permute-start(f32[72,128]{1,0:T(8,128)S(1)} %get-tuple-element.20), channel_id=1, source_target_pairs={{0,2},{1,3},{2,0},{3,1},{4,6},{5,7},{6,4},{7,5},{8,10},{9,11},{10,... | collective-permute-start | bytes 110600 | tf_op jit(solution)/shard_map/ppermute | solution.py:355
  22.7 0.2 collective-permute-start.6
  22.9 0.0 collective-permute-done.4.refs_1_
  22.9 2.4 %collective-permute-done.5.refs_2_ = f32[72,128]{1,0:T(8,128)S(1)} collective-permute-done((f32[72,128]{1,0:T(8,128)S(1)}, f32[72,128]{1,0:T(8,128)S(1)}, u32[]{:S(2)}, u32[]{:S(2)}) %collective-permute-start.5) | collective-permute-done | bytes 36896 | tf_op jit(solution)/shard_map/ppermute | solution.py:355
  25.3 3.1 %collective-permute-done.6.refs_3_ = f32[72,128]{1,0:T(8,128)S(1)} collective-permute-done((f32[72,128]{1,0:T(8,128)S(1)}, f32[72,128]{1,0:T(8,128)S(1)}, u32[]{:S(2)}, u32[]{:S(2)}) %collective-permute-start.6) | collective-permute-done | bytes 36896 | tf_op jit(solution)/shard_map/ppermute | solution.py:355
  28.4 0.2 shard_map.135.refs_0_
  28.6 0.5 collective-permute-start.9
  29.1 0.0 collective-permute-start.8
  29.1 4.0 %collective-permute-start.7 = (f32[64,128]{1,0:T(8,128)S(1)}, f32[64,128]{1,0:T(8,128)S(1)}, u32[]{:S(2)}, u32[]{:S(2)}) collective-permute-start(f32[64,128]{1,0:T(8,128)S(1)} %shard_map.135.refs_0_), channel_id=1, source_target_pairs={{0,1},{1,0},{2,3},{3,2},{4,5},{5,4},{6,7},{7,6},{8,9},{9,8},{10,11... | collective-permute-start | bytes 98312 | tf_op jit(solution)/shard_map/ppermute | solution.py:355
  33.1 1.3 %collective-permute-done.9.refs_3_ = f32[64,128]{1,0:T(8,128)S(1)} collective-permute-done((f32[64,128]{1,0:T(8,128)S(1)}, f32[64,128]{1,0:T(8,128)S(1)}, u32[]{:S(2)}, u32[]{:S(2)}) %collective-permute-start.9) | collective-permute-done | bytes 32800 | tf_op jit(solution)/shard_map/ppermute | solution.py:355
  34.4 0.0 collective-permute-done.8.refs_2_
  34.4 0.6 %collective-permute-done.7.refs_1_ = f32[64,128]{1,0:T(8,128)S(1)} collective-permute-done((f32[64,128]{1,0:T(8,128)S(1)}, f32[64,128]{1,0:T(8,128)S(1)}, u32[]{:S(2)}, u32[]{:S(2)}) %collective-permute-start.7) | collective-permute-done | bytes 32800 | tf_op jit(solution)/shard_map/ppermute | solution.py:355
  35.0 1.6 %collective-permute-start.12 = (f32[256,128]{1,0:T(8,128)S(1)}, f32[256,128]{1,0:T(8,128)S(1)}, u32[]{:S(2)}, u32[]{:S(2)}) collective-permute-start(f32[256,128]{1,0:T(8,128)S(1)} %shard_map.136.refs_8_), channel_id=1, source_target_pairs={{0,24},{4,28},{8,16},{12,20},{16,8},{20,12},{24,0},{28,4},{1,25},{... | collective-permute-start | bytes 393224 | tf_op jit(solution)/shard_map/ppermute | solution.py:355
  36.6 1.2 %collective-permute-start.11 = (f32[256,128]{1,0:T(8,128)S(1)}, f32[256,128]{1,0:T(8,128)S(1)}, u32[]{:S(2)}, u32[]{:S(2)}) collective-permute-start(f32[256,128]{1,0:T(8,128)S(1)} %shard_map.136.refs_8_), channel_id=1, source_target_pairs={{0,16},{4,20},{8,24},{12,28},{16,0},{20,4},{24,8},{28,12},{1,17},{... | collective-permute-start | bytes 393224 | tf_op jit(solution)/shard_map/ppermute | solution.py:355
  37.8 0.8 %collective-permute-start.10 = (f32[256,128]{1,0:T(8,128)S(1)}, f32[256,128]{1,0:T(8,128)S(1)}, u32[]{:S(2)}, u32[]{:S(2)}) collective-permute-start(f32[256,128]{1,0:T(8,128)S(1)} %shard_map.136.refs_8_), channel_id=1, source_target_pairs={{0,8},{4,12},{8,0},{12,4},{16,24},{20,28},{24,16},{28,20},{1,9},{5... | collective-permute-start | bytes 393224 | tf_op jit(solution)/shard_map/ppermute | solution.py:355
  38.5 0.0 collective-permute-start.13
  38.6 2.5 %collective-permute-done.12.refs_11_ = f32[256,128]{1,0:T(8,128)S(1)} collective-permute-done((f32[256,128]{1,0:T(8,128)S(1)}, f32[256,128]{1,0:T(8,128)S(1)}, u32[]{:S(2)}, u32[]{:S(2)}) %collective-permute-start.12) | collective-permute-done | bytes 131104 | tf_op jit(solution)/shard_map/ppermute | solution.py:355
  41.0 0.0 collective-permute-start.16
  41.0 1.3 %collective-permute-done.11.refs_10_ = f32[256,128]{1,0:T(8,128)S(1)} collective-permute-done((f32[256,128]{1,0:T(8,128)S(1)}, f32[256,128]{1,0:T(8,128)S(1)}, u32[]{:S(2)}, u32[]{:S(2)}) %collective-permute-start.11) | collective-permute-done | bytes 131104 | tf_op jit(solution)/shard_map/ppermute | solution.py:355
  42.3 0.0 collective-permute-start.15
  42.3 0.4 collective-permute-done.10.refs_9_
  42.7 0.1 collective-permute-start.14
  42.8 0.9 %copy-done.3 = bf16[64,896]{1,0:T(8,128)(2,1)S(1)} copy-done((bf16[64,896]{1,0:T(8,128)(2,1)S(1)}, bf16[64,896]{1,0:T(8,128)(2,1)}, u32[]{:S(2)}) %copy-start.3) | copy-done | bytes 114712
  43.7 0.9 %copy-done.4 = bf16[64,896]{1,0:T(8,128)(2,1)S(1)} copy-done((bf16[64,896]{1,0:T(8,128)(2,1)S(1)}, bf16[64,896]{1,0:T(8,128)(2,1)}, u32[]{:S(2)}) %copy-start.4) | copy-done | bytes 114712
  44.6 0.7 %copy-done.5 = f32[1,4,3,49]{3,1,2,0:T(4,128)S(1)} copy-done((f32[1,4,3,49]{3,1,2,0:T(4,128)S(1)}, f32[1,4,3,49]{3,1,2,0:T(4,128)}, u32[]{:S(2)}) %copy-start.5) | copy-done | bytes 2376
  45.3 1.2 %shard_map.131.refs_1_ = bf16[4,512,896]{2,1,0:T(8,128)(2,1)S(1)} custom-call(f32[1,3,4,49]{3,2,1,0:T(4,128)S(1)} %bitcast.3, bf16[64,896]{1,0:T(8,128)(2,1)S(1)} %copy-done.4, bf16[64,896]{1,0:T(8,128)(2,1)S(1)} %copy-done.3), custom_call_target="tpu_custom_call" | custom-call | tf_op jit(solution)/shard_map/pallas_call | solution.py:334
  46.5 0.0 collective-permute-done.13.refs_12_
  46.6 0.0 collective-permute-done.16.refs_15_
  46.6 0.0 collective-permute-done.15.refs_14_
  46.6 0.0 collective-permute-done.14.refs_13_
  46.6 3.3 %shard_map.137 = (f32[1,256,256]{2,1,0:T(8,128)}, f32[1,4,128,128]{3,2,1,0:T(8,128)}) custom-call(f32[1,4,128,128]{3,2,1,0:T(8,128)S(1)} %copy-done, bf16[4,512,896]{2,1,0:T(8,128)(2,1)S(1)} %shard_map.131.refs_1_, bf16[128,896]{1,0:T(8,128)(2,1)S(1)} %copy-done.2, bf16[128,896]{1,0:T(8,128)(2,1)S(1)} %copy-done.1, s32[1,4]{1,0:T(1,128)S(1)} %copy-done.7, ...), custom_call_target="tpu_custom_call" | custom-call | tf_op jit(solution)/shard_map/pallas_call | solution.py:334
  (11 shorter events, 0.1 us)
Async XLA Ops:
  0.6 46.0 %copy-start.1 = (bf16[128,896]{1,0:T(8,128)(2,1)S(1)}, bf16[128,896]{1,0:T(8,128)(2,1)}, u32[]{:S(2)}) copy-start(bf16[128,896]{1,0:T(8,128)(2,1)} %constant.9.clone.refs_5_.refs_3_) | copy-start | bytes 688132
  0.6 46.0 %copy-start.2 = (bf16[128,896]{1,0:T(8,128)(2,1)S(1)}, bf16[128,896]{1,0:T(8,128)(2,1)}, u32[]{:S(2)}) copy-start(bf16[128,896]{1,0:T(8,128)(2,1)} %constant.8.clone.refs_4_.refs_2_) | copy-start | bytes 688132
  0.7 45.9 %copy-start.8 = (s32[4]{0:T(128)S(1)}, s32[4]{0:T(128)}, u32[]{:S(2)}) copy-start(s32[4]{0:T(128)} %refs_7_.3) | copy-start | bytes 52
  0.7 45.9 %copy-start.7 = (s32[1,4]{1,0:T(1,128)S(1)}, s32[1,4]{1,0:T(1,128)}, u32[]{:S(2)}) copy-start(s32[1,4]{1,0:T(1,128)} %refs_4_.2) | copy-start | bytes 52
  0.7 45.9 %copy-start = (f32[1,4,128,128]{3,2,1,0:T(8,128)S(1)}, f32[1,4,128,128]{3,2,1,0:T(8,128)}, u32[]{:S(2)}) copy-start(f32[1,4,128,128]{3,2,1,0:T(8,128)} %refs_0_.3) | copy-start | bytes 786436
  0.7 45.9 %copy-start.6 = (s32[1,4,2]{1,2,0:T(2,128)S(1)}, s32[1,4,2]{1,2,0:T(2,128)}, u32[]{:S(2)}) copy-start(s32[1,4,2]{1,2,0:T(2,128)} %param.17) | copy-start | bytes 100
  5.0 2.1 %collective-permute-start = (f32[1032,128]{1,0:T(8,128)S(1)}, f32[1032,128]{1,0:T(8,128)S(1)}, u32[]{:S(2)}, u32[]{:S(2)}) collective-permute-start(f32[1032,128]{1,0:T(8,128)S(1)} %get-tuple-element.13), channel_id=1, source_target_pairs={{0,4},{4,0},{8,12},{12,8},{16,20},{20,16},{24,28},{28,24},{1,5},{5... | collective-permute-start | bytes 1585160 | tf_op jit(solution)/shard_map/ppermute | solution.py:355
  7.2 7.0 %collective-permute-start.1 = (f32[264,128]{1,0:T(8,128)S(1)}, f32[264,128]{1,0:T(8,128)S(1)}, u32[]{:S(2)}, u32[]{:S(2)}) collective-permute-start(f32[264,128]{1,0:T(8,128)S(1)} %get-tuple-element.15), channel_id=1, source_target_pairs={{0,8},{4,12},{8,0},{12,4},{16,24},{20,28},{24,16},{28,20},{1,9},{5... | collective-permute-start | bytes 405512 | tf_op jit(solution)/shard_map/ppermute | solution.py:355
  10.1 8.2 %collective-permute-start.2 = (f32[264,128]{1,0:T(8,128)S(1)}, f32[264,128]{1,0:T(8,128)S(1)}, u32[]{:S(2)}, u32[]{:S(2)}) collective-permute-start(f32[264,128]{1,0:T(8,128)S(1)} %get-tuple-element.16), channel_id=1, source_target_pairs={{0,16},{4,20},{8,24},{12,28},{16,0},{20,4},{24,8},{28,12},{1,17},{... | collective-permute-start | bytes 405512 | tf_op jit(solution)/shard_map/ppermute | solution.py:355
  11.7 6.7 %collective-permute-start.3 = (f32[264,128]{1,0:T(8,128)S(1)}, f32[264,128]{1,0:T(8,128)S(1)}, u32[]{:S(2)}, u32[]{:S(2)}) collective-permute-start(f32[264,128]{1,0:T(8,128)S(1)} %get-tuple-element.17), channel_id=1, source_target_pairs={{0,24},{4,28},{8,16},{12,20},{16,8},{20,12},{24,0},{28,4},{1,25},{... | collective-permute-start | bytes 405512 | tf_op jit(solution)/shard_map/ppermute | solution.py:355
  18.4 4.5 %collective-permute-start.4 = (f32[72,128]{1,0:T(8,128)S(1)}, f32[72,128]{1,0:T(8,128)S(1)}, u32[]{:S(2)}, u32[]{:S(2)}) collective-permute-start(f32[72,128]{1,0:T(8,128)S(1)} %get-tuple-element.19), channel_id=1, source_target_pairs={{0,1},{1,0},{2,3},{3,2},{4,5},{5,4},{6,7},{7,6},{8,9},{9,8},{10,11... | collective-permute-start | bytes 110600 | tf_op jit(solution)/shard_map/ppermute | solution.py:355
  20.1 5.2 %collective-permute-start.5 = (f32[72,128]{1,0:T(8,128)S(1)}, f32[72,128]{1,0:T(8,128)S(1)}, u32[]{:S(2)}, u32[]{:S(2)}) collective-permute-start(f32[72,128]{1,0:T(8,128)S(1)} %get-tuple-element.20), channel_id=1, source_target_pairs={{0,2},{1,3},{2,0},{3,1},{4,6},{5,7},{6,4},{7,5},{8,10},{9,11},{10,... | collective-permute-start | bytes 110600 | tf_op jit(solution)/shard_map/ppermute | solution.py:355
  22.7 5.8 %collective-permute-start.6 = (f32[72,128]{1,0:T(8,128)S(1)}, f32[72,128]{1,0:T(8,128)S(1)}, u32[]{:S(2)}, u32[]{:S(2)}) collective-permute-start(f32[72,128]{1,0:T(8,128)S(1)} %get-tuple-element.21), channel_id=1, source_target_pairs={{0,3},{1,2},{2,1},{3,0},{4,7},{5,6},{6,5},{7,4},{8,11},{9,10},{10,... | collective-permute-start | bytes 110600 | tf_op jit(solution)/shard_map/ppermute | solution.py:355
  28.6 5.8 %collective-permute-start.9 = (f32[64,128]{1,0:T(8,128)S(1)}, f32[64,128]{1,0:T(8,128)S(1)}, u32[]{:S(2)}, u32[]{:S(2)}) collective-permute-start(f32[64,128]{1,0:T(8,128)S(1)} %shard_map.135.refs_0_), channel_id=1, source_target_pairs={{0,3},{1,2},{2,1},{3,0},{4,7},{5,6},{6,5},{7,4},{8,11},{9,10},{10,... | collective-permute-start | bytes 98312 | tf_op jit(solution)/shard_map/ppermute | solution.py:355
  29.1 5.3 %collective-permute-start.8 = (f32[64,128]{1,0:T(8,128)S(1)}, f32[64,128]{1,0:T(8,128)S(1)}, u32[]{:S(2)}, u32[]{:S(2)}) collective-permute-start(f32[64,128]{1,0:T(8,128)S(1)} %shard_map.135.refs_0_), channel_id=1, source_target_pairs={{0,2},{1,3},{2,0},{3,1},{4,6},{5,7},{6,4},{7,5},{8,10},{9,11},{10,... | collective-permute-start | bytes 98312 | tf_op jit(solution)/shard_map/ppermute | solution.py:355
  29.1 5.9 %collective-permute-start.7 = (f32[64,128]{1,0:T(8,128)S(1)}, f32[64,128]{1,0:T(8,128)S(1)}, u32[]{:S(2)}, u32[]{:S(2)}) collective-permute-start(f32[64,128]{1,0:T(8,128)S(1)} %shard_map.135.refs_0_), channel_id=1, source_target_pairs={{0,1},{1,0},{2,3},{3,2},{4,5},{5,4},{6,7},{7,6},{8,9},{9,8},{10,11... | collective-permute-start | bytes 98312 | tf_op jit(solution)/shard_map/ppermute | solution.py:355
  35.0 6.0 %collective-permute-start.12 = (f32[256,128]{1,0:T(8,128)S(1)}, f32[256,128]{1,0:T(8,128)S(1)}, u32[]{:S(2)}, u32[]{:S(2)}) collective-permute-start(f32[256,128]{1,0:T(8,128)S(1)} %shard_map.136.refs_8_), channel_id=1, source_target_pairs={{0,24},{4,28},{8,16},{12,20},{16,8},{20,12},{24,0},{28,4},{1,25},{... | collective-permute-start | bytes 393224 | tf_op jit(solution)/shard_map/ppermute | solution.py:355
  36.6 5.8 %collective-permute-start.11 = (f32[256,128]{1,0:T(8,128)S(1)}, f32[256,128]{1,0:T(8,128)S(1)}, u32[]{:S(2)}, u32[]{:S(2)}) collective-permute-start(f32[256,128]{1,0:T(8,128)S(1)} %shard_map.136.refs_8_), channel_id=1, source_target_pairs={{0,16},{4,20},{8,24},{12,28},{16,0},{20,4},{24,8},{28,12},{1,17},{... | collective-permute-start | bytes 393224 | tf_op jit(solution)/shard_map/ppermute | solution.py:355
  37.8 5.0 %collective-permute-start.10 = (f32[256,128]{1,0:T(8,128)S(1)}, f32[256,128]{1,0:T(8,128)S(1)}, u32[]{:S(2)}, u32[]{:S(2)}) collective-permute-start(f32[256,128]{1,0:T(8,128)S(1)} %shard_map.136.refs_8_), channel_id=1, source_target_pairs={{0,8},{4,12},{8,0},{12,4},{16,24},{20,28},{24,16},{28,20},{1,9},{5... | collective-permute-start | bytes 393224 | tf_op jit(solution)/shard_map/ppermute | solution.py:355
  38.5 8.0 %collective-permute-start.13 = (f32[256,128]{1,0:T(8,128)S(1)}, f32[256,128]{1,0:T(8,128)S(1)}, u32[]{:S(2)}, u32[]{:S(2)}) collective-permute-start(f32[256,128]{1,0:T(8,128)S(1)} %shard_map.136.refs_8_), channel_id=1, source_target_pairs={{0,4},{4,0},{8,12},{12,8},{16,20},{20,16},{24,28},{28,24},{1,5},{5... | collective-permute-start | bytes 393224 | tf_op jit(solution)/shard_map/ppermute | solution.py:355
  41.0 5.5 %collective-permute-start.16 = (f32[256,128]{1,0:T(8,128)S(1)}, f32[256,128]{1,0:T(8,128)S(1)}, u32[]{:S(2)}, u32[]{:S(2)}) collective-permute-start(f32[256,128]{1,0:T(8,128)S(1)} %collective-permute-done.12.refs_11_), channel_id=1, source_target_pairs={{0,4},{4,0},{8,12},{12,8},{16,20},{20,16},{24,28},{28,24},{1,5},{5... | collective-permute-start | bytes 393224 | tf_op jit(solution)/shard_map/ppermute | solution.py:355
  42.3 4.2 %collective-permute-start.15 = (f32[256,128]{1,0:T(8,128)S(1)}, f32[256,128]{1,0:T(8,128)S(1)}, u32[]{:S(2)}, u32[]{:S(2)}) collective-permute-start(f32[256,128]{1,0:T(8,128)S(1)} %collective-permute-done.11.refs_10_), channel_id=1, source_target_pairs={{0,4},{4,0},{8,12},{12,8},{16,20},{20,16},{24,28},{28,24},{1,5},{5... | collective-permute-start | bytes 393224 | tf_op jit(solution)/shard_map/ppermute | solution.py:355
  42.7 3.9 %collective-permute-start.14 = (f32[256,128]{1,0:T(8,128)S(1)}, f32[256,128]{1,0:T(8,128)S(1)}, u32[]{:S(2)}, u32[]{:S(2)}) collective-permute-start(f32[256,128]{1,0:T(8,128)S(1)} %collective-permute-done.10.refs_9_), channel_id=1, source_target_pairs={{0,4},{4,0},{8,12},{12,8},{16,20},{20,16},{24,28},{28,24},{1,5},{5... | collective-permute-start | bytes 393224 | tf_op jit(solution)/shard_map/ppermute | solution.py:355
  42.8 0.9 %copy-start.3 = (bf16[64,896]{1,0:T(8,128)(2,1)S(1)}, bf16[64,896]{1,0:T(8,128)(2,1)}, u32[]{:S(2)}) copy-start(bf16[64,896]{1,0:T(8,128)(2,1)} %constant.11.clone.refs_2_.refs_3_) | copy-start | bytes 344068
  43.7 0.9 %copy-start.4 = (bf16[64,896]{1,0:T(8,128)(2,1)S(1)}, bf16[64,896]{1,0:T(8,128)(2,1)}, u32[]{:S(2)}) copy-start(bf16[64,896]{1,0:T(8,128)(2,1)} %constant.10.clone.refs_1_.refs_2_) | copy-start | bytes 344068
  44.6 0.7 %copy-start.5 = (f32[1,4,3,49]{3,1,2,0:T(4,128)S(1)}, f32[1,4,3,49]{3,1,2,0:T(4,128)}, u32[]{:S(2)}) copy-start(f32[1,4,3,49]{3,1,2,0:T(4,128)} %param.14) | copy-start | bytes 7060

commit v4 on v3

--- a/solution.py
+++ b/solution.py
@@ -131,29 +131,49 @@
     return both[:side] + both[side:] * spread_along((side, side), 1, side)
 
 
+FIRST_FAR = 10
+SECOND_FAR = 4
+
+
+def fetch(sources, targets, semaphores):
+    copies = [
+        pltpu.make_async_copy(source, target, semaphores.at[n])
+        for n, (source, target) in enumerate(zip(sources, targets, strict=True))
+    ]
+    for copy in copies:
+        copy.start()
+
+    def wait(*numbers):
+        for n in numbers:
+            copies[n].wait()
+
+    return wait, targets
+
+
 def first_kernel(
-    slots, side, tiles, meta_blocks,
-    science, coef, rows_high, rows_low, across_high, across_low,
-    weight, slot_tile, offsets, counts, tile_place,
-    keep, send,
-    coef_buf, tap_buf, left, images, right, total,
+    slots, side, tiles, meta_blocks, visits,
+    *refs,
 ):
+    far, counts, keep, send = refs[:FIRST_FAR], *refs[FIRST_FAR : FIRST_FAR + 3]
+    coef_buf, tap_buf, left, images, right, moved = refs[FIRST_FAR + 3 : FIRST_FAR + 9]
+    wait, near = fetch(far, refs[FIRST_FAR + 9 : -1], refs[-1])
+    coef, rows_high, rows_low, science, across_high, across_low = near[:6]
+    weight, slot_tile, offsets, tile_place = near[6:]
     visit = lax.axis_index("visit")
     sky = lax.axis_index("sky")
     core = visit % 2
-    half = TILE // 2
-    sky_size = tiles
+    peers = visits // 2
+    share = side // visits
+    wait(*range(FIRST_FAR))
     tap_rows(coef, coef_buf, tap_buf, rows_high, rows_low, slots)
     for b in range(slots):
         put_block(science[0, b], b, side, images)
         build_left(b, slots, side, tap_buf, left)
     across_stage(slots, side, images, across_high, across_low, right)
-    total[...] = jnp.zeros(total.shape, F32)
-    first_lane = (visit * sky_size + sky) * slots
+    first_lane = (visit * tiles + sky) * slots
     lane = lax.broadcasted_iota(jnp.int32, (META, LANES), 1)
     field = lax.broadcasted_iota(jnp.int32, (META, LANES), 0)
     meta = [jnp.zeros((META, LANES), F32) for _ in range(meta_blocks)]
-    col = lax.broadcasted_iota(jnp.int32, (side, side), 1)
     for b in range(slots):
         owner = tile_place[slot_tile[0, b]]
         usable = b < counts[0, 0]
@@ -173,52 +193,106 @@
             meta[m] = jnp.where(lane + m * LANES == first_lane + b, entry, meta[m])
         image = down_stage(b, side, left, right)
         image = jnp.where(usable, image * used, 0.0)
-        moved = pltpu.roll(image, left_edge, 1)
-        total[owner, 0, pl.ds(top, side), :] += jnp.where(col >= left_edge, moved, 0.0)
-        total[owner, 1, pl.ds(top, side), :] += jnp.where(col < left_edge, moved, 0.0)
-    body = tiles * 2 * half
-    for t in range(tiles):
-        for h in range(2):
-            base = (t * 2 + h) * half
-            keep[pl.ds(base, half), :] = total[t, h, pl.ds(core * half, half), :]
-            send[pl.ds(base, half), :] = total[t, h, pl.ds((1 - core) * half, half), :]
+        moved[b] = pltpu.roll(image, left_edge, 1)
+        for h, out in ((0, keep), (1, send)):
+
+            def pick(q, b=b, h=h, out=out, top=top):
+                residue = 2 * q + (core ^ h)
+                start = first_row(top, residue, visits) * visits + residue - top
+                out[pl.ds((q * slots + b) * share, share), :] = moved[
+                    b, pl.ds(start, share, stride=visits), :
+                ]
+
+            repeat(peers, peers, pick)
+    body = peers * slots * share
     for m in range(meta_blocks):
         keep[pl.ds(body + m * META, META), :] = meta[m]
         send[pl.ds(body + m * META, META), :] = meta[m]
 
 
-def scatter_kernel(tiles, strip, peers, meta_rows, keep, received, *pieces):
-    pieces = pieces[::-1]
+def quotient(value, divisor):
+    if divisor & (divisor - 1) == 0:
+        return value >> (divisor.bit_length() - 1)
+    return lax.div(value, divisor)
+
+
+def repeat(count, width, step):
+    if width <= 4:
+        for n in range(count):
+            step(n)
+    else:
+        lax.fori_loop(0, count, lambda n, carry: (step(n), carry)[1], 0)
+
+
+def first_row(top, residue, visits):
+    return quotient(top - residue + (visits - 1), visits)
+
+
+def scatter_kernel(rows, peers, meta_rows, keep, received, *pieces):
     place = lax.axis_index("visit") // 2
-    half = strip * peers
-    body = tiles * 2 * half
+    tail = pl.ds(peers * rows, meta_rows)
+    meta = keep[tail, :] + received[tail, :]
     for j in range(peers):
-        first = (place ^ j) * strip
-        for g in range(tiles * 2):
-            source = pl.ds(g * half + first, strip)
-            pieces[j][pl.ds(g * strip, strip), :] = keep[source, :] + received[source, :]
-        source = pl.ds(body, meta_rows)
-        pieces[j][pl.ds(tiles * 2 * strip, meta_rows), :] = keep[source, :] + received[source, :]
-
-
-def plane_kernel(tiles, strip, peers, meta_rows, *refs):
-    sources, pieces = refs[:peers], refs[peers:][::-1]
+        source = pl.ds((place ^ j) * rows, rows)
+        pieces[j][pl.ds(0, rows), :] = keep[source, :]
+        pieces[j][pl.ds(rows, rows), :] = received[source, :]
+        pieces[j][pl.ds(2 * rows, meta_rows), :] = meta
+
+
+def plane_kernel(slots, side, tiles, visits, meta_rows, *refs):
+    peers = visits // 2
+    share = side // visits
+    size = 2 * (TILE // visits)
+    sources, pieces = refs[:peers], refs[peers : peers + tiles]
+    table, scalars, semaphore = refs[peers + tiles : peers + tiles + 3]
+    sums = refs[peers + tiles + 3 :]
+    visit = lax.axis_index("visit")
     sky = lax.axis_index("sky")
-    size = 2 * strip
-    tail = pl.ds(tiles * size, meta_rows)
+    core = visit % 2
+    place = visit // 2
+    tail = pl.ds(2 * slots * share, meta_rows)
     meta = sources[0][tail, :]
     for p in range(1, peers):
         meta = meta + sources[p][tail, :]
+    table[...] = meta
+    copy = pltpu.make_async_copy(table, scalars, semaphore)
+    copy.start()
+    for total in sums:
+        total[...] = jnp.zeros(total.shape, F32)
+    col = lax.broadcasted_iota(jnp.int32, (share, LANES), 1)
+    copy.wait()
+
+    def place_rows(h, b):
+        for p in range(peers):
+            total = sums[p % len(sums)]
+            sender = 2 * (place ^ p) + (core ^ h)
+            slot = (sender * tiles + sky) * slots + b
+            base, lane = 0, slot
+            if meta_rows > META:
+                base = quotient(slot, LANES)
+                lane = slot - base * LANES
+                base = base * META
+            top = scalars[base + 1, lane].astype(jnp.int32)
+            left_edge = scalars[base + 2, lane].astype(jnp.int32)
+            owner = scalars[base + 3, lane].astype(jnp.int32)
+            rows = sources[p][pl.ds((h * slots + b) * share, share), :]
+            where = pl.ds(first_row(top, visit, visits), share)
+            total[owner, 0, where, :] += jnp.where(col >= left_edge, rows, 0.0)
+            total[owner, 1, where, :] += jnp.where(col < left_edge, rows, 0.0)
+
+    for h in range(2):
+        repeat(slots, peers, lambda b, h=h: place_rows(h, b))
     for j in range(tiles):
-        rows = pl.ds((sky ^ j) * size, size)
-        value = sources[0][rows, :]
-        for p in range(1, peers):
-            value = value + sources[p][rows, :]
-        pieces[j][pl.ds(0, size), :] = value
+        tile = sky ^ j
+        for h in range(2):
+            value = sums[0][tile, h]
+            for total in sums[1:]:
+                value = value + total[tile, h]
+            pieces[j][pl.ds(h * (size // 2), size // 2), :] = value
         pieces[j][pl.ds(size, meta_rows), :] = meta
 
 
-def template_kernel(tiles, strip, meta_blocks, side, *refs):
+def template_kernel(tiles, strip, visits, meta_blocks, side, *refs):
     sources, out = refs[:tiles], refs[tiles]
     visit = lax.axis_index("visit")
     sky = lax.axis_index("sky")
@@ -226,8 +300,7 @@
     value = sources[0][...]
     for p in range(1, tiles):
         value = value + sources[p][...]
-    first = (visit % 2) * (TILE // 2) + (visit // 2) * strip
-    y = (lax.broadcasted_iota(jnp.int32, (strip, LANES), 0) + first).astype(F32)
+    y = (lax.broadcasted_iota(jnp.int32, (strip, LANES), 0) * visits + visit).astype(F32)
     x = lax.broadcasted_iota(jnp.int32, (TILE, LANES), 0).astype(F32)
     coverage = jnp.zeros((strip, TILE), F32)
     for m in range(meta_blocks):
@@ -259,28 +332,36 @@
 
 def second_kernel(
     slots, side, tiles, strip, peers,
-    science, left, across_high, across_low,
-    slot_tile, offsets, counts, tile_place,
+    left, across_high, across_low, counts,
     *refs,
 ):
-    pieces = refs[: 2 * peers]
-    template, difference = refs[2 * peers : 2 * peers + 2]
-    images, right, total = refs[2 * peers + 2 :]
+    far, refs = refs[:SECOND_FAR], refs[SECOND_FAR:]
+    pieces, refs = refs[: 2 * peers], refs[2 * peers :]
+    template, difference, images, right, total, staged, results = refs[:7]
+    wait, near = fetch(far, refs[7 : 7 + SECOND_FAR], refs[-2])
+    slot_tile, offsets, tile_place, science = near
+    outward = refs[-1]
     visit = lax.axis_index("visit")
     sky = lax.axis_index("sky")
     core = visit % 2
     place = visit // 2
-    half = TILE // 2
     for c in range(2):
         for j in range(peers):
-            first = (core ^ c) * half + (place ^ j) * strip
-            for t in range(tiles):
+            residue = 2 * (place ^ j) + (core ^ c)
+            piece = pieces[c * peers + j]
+
+            def spread_rows(t, residue=residue, piece=piece):
                 for h in range(2):
-                    total[t, h, pl.ds(first, strip), :] = pieces[c * peers + j][
+                    total[t, h, pl.ds(residue, strip, stride=2 * peers), :] = piece[
                         pl.ds((t * 2 + h) * strip, strip), :
                     ]
+
+            repeat(tiles, peers, spread_rows)
     for h in range(2):
-        template[0, :, h * LANES : (h + 1) * LANES] = total[sky, h]
+        staged[:, h * LANES : (h + 1) * LANES] = total[sky, h]
+    copies = [pltpu.make_async_copy(staged, template.at[0], outward.at[slots])]
+    copies[0].start()
+    wait(*range(SECOND_FAR))
     col = lax.broadcasted_iota(jnp.int32, (side, side), 1)
     for b in range(slots):
         owner = tile_place[slot_tile[0, b]]
@@ -293,7 +374,11 @@
     across_stage(slots, side, images, across_high, across_low, right)
     for b in range(slots):
         matched = down_stage(b, side, left, right)
-        difference[0, b] = jnp.where(b < counts[0, 0], science[0, b] - matched, 0.0)
+        results[b] = jnp.where(b < counts[0, 0], science[0, b] - matched, 0.0)
+        copies.append(pltpu.make_async_copy(results.at[b], difference.at[0, b], outward.at[b]))
+        copies[-1].start()
+    for copy in copies:
+        copy.wait()
 
 
 def prepare_kernel(slots, side, coef, rows_high, rows_low, left, coef_buf, tap_buf):
@@ -309,6 +394,7 @@
     tiles = lax.axis_size("sky")
     peers = visits // 2
     strip = TILE // visits
+    rows = slots * (side // visits)
     meta_blocks = -(-visits * tiles * slots // LANES)
     meta_rows = meta_blocks * META
     across_high, across_low, rows_high, rows_low = (
@@ -316,6 +402,7 @@
     )
     vmem = pl.BlockSpec(memory_space=pltpu.VMEM)
     smem = pl.BlockSpec(memory_space=pltpu.SMEM)
+    anywhere = pl.BlockSpec(memory_space=pl.ANY)
 
     coef_first = coef_first.transpose(0, 2, 1, 3)
     coef_second = coef_second.transpose(0, 2, 1, 3)
@@ -330,12 +417,12 @@
     def near(value):
         return pltpu.with_memory_space_constraint(value, pltpu.VMEM)
 
-    def call(function, ins, outs, specs=None, scratch=()):
+    def call(function, ins, outs, specs=None, scratch=(), out_space=vmem):
         return pl.pallas_call(
             function,
             out_shape=outs,
             in_specs=specs or [vmem] * len(ins),
-            out_specs=jax.tree.map(lambda _: vmem, outs),
+            out_specs=jax.tree.map(lambda _: out_space, outs),
             scratch_shapes=list(scratch),
             compiler_params=pltpu.CompilerParams(vmem_limit_bytes=VMEM_BYTES),
         )(*ins)
@@ -360,35 +447,50 @@
             out.append(flip(values[j], axis, size, step * j))
         return out
 
+    first_far = (
+        coef_first, rows_high, rows_low, science, across_high, across_low,
+        weight, slot_tile, offsets, tile_place,
+    )
     keep, send = call(
-        lambda *refs: first_kernel(slots, side, tiles, meta_blocks, *refs),
-        (*map(far, (science, coef_first, rows_high, rows_low, across_high, across_low)),
-         *map(far, (weight, slot_tile, offsets)), counts, far(tile_place)),
-        [shape(tiles * TILE + meta_rows, LANES)] * 2,
-        specs=[vmem] * 6 + [smem] * 5,
-        scratch=tap_scratch + [pltpu.VMEM(left_shape, BF16)] + pass_scratch,
+        lambda *refs: first_kernel(slots, side, tiles, meta_blocks, visits, *refs),
+        (*map(far, first_far), counts),
+        [shape(peers * rows + meta_rows, LANES)] * 2,
+        specs=[anywhere] * FIRST_FAR + [smem],
+        scratch=tap_scratch
+        + [pltpu.VMEM(left_shape, BF16)]
+        + pass_scratch[:2]
+        + [pltpu.VMEM((slots, side, LANES), F32)]
+        + [pltpu.VMEM(a.shape, a.dtype) for a in first_far[:6]]
+        + [pltpu.SMEM(a.shape, a.dtype) for a in first_far[6:]]
+        + [pltpu.SemaphoreType.DMA((FIRST_FAR,))],
     )
     left = call(
         lambda *refs: prepare_kernel(slots, side, *refs),
-        (coef_second, rows_high, rows_low),
+        (far(coef_second), far(rows_high), far(rows_low)),
         pltpu.VMEM(left_shape, BF16),
         scratch=tap_scratch,
     )
     received = flip(send, "visit", visits, 1)
     pieces = call(
-        lambda *refs: scatter_kernel(tiles, strip, peers, meta_rows, *refs),
+        lambda *refs: scatter_kernel(rows, peers, meta_rows, *refs),
         (near(keep), near(received)),
-        [shape(tiles * 2 * strip + meta_rows, LANES)] * peers,
-    )[::-1]
+        [shape(2 * rows + meta_rows, LANES)] * peers,
+    )
     arrived = exchange(pieces, "visit", visits, 2)
     pieces = call(
-        lambda *refs: plane_kernel(tiles, strip, peers, meta_rows, *refs),
+        lambda *refs: plane_kernel(slots, side, tiles, visits, meta_rows, *refs),
         [near(a) for a in arrived],
         [shape(2 * strip + meta_rows, LANES)] * tiles,
-    )[::-1]
+        scratch=[
+            pltpu.VMEM((meta_rows, LANES), F32),
+            pltpu.SMEM((meta_rows, LANES), F32),
+            pltpu.SemaphoreType.DMA,
+        ]
+        + [pltpu.VMEM((tiles, 2, strip, LANES), F32)] * min(peers, 4),
+    )
     arrived = exchange(pieces, "sky", tiles, 1)
     strips = call(
-        lambda *refs: template_kernel(tiles, strip, meta_blocks, side, *refs),
+        lambda *refs: template_kernel(tiles, strip, visits, meta_blocks, side, *refs),
         [near(a) for a in arrived],
         shape(2 * strip, LANES),
     )
@@ -400,13 +502,19 @@
     )
     mine = exchange([piece] * peers, "visit", visits, 2)
     theirs = [flip(p, "visit", visits, 1) for p in mine]
+    second_far = (slot_tile, offsets, tile_place, science)
     template, difference = call(
         lambda *refs: second_kernel(slots, side, tiles, strip, peers, *refs),
-        (science, near(left), across_high, across_low,
-         slot_tile, offsets, counts, tile_place, *map(near, mine), *map(near, theirs)),
+        (near(left), near(across_high), near(across_low), counts,
+         *map(far, second_far), *map(near, mine), *map(near, theirs)),
         [jax.ShapeDtypeStruct(d, F32) for d in ((1, TILE, TILE), (1, slots, side, side))],
-        specs=[vmem] * 4 + [smem] * 4 + [vmem] * (2 * peers),
-        scratch=pass_scratch,
+        specs=[vmem] * 3 + [smem] + [anywhere] * SECOND_FAR + [vmem] * (2 * peers),
+        scratch=pass_scratch
+        + [pltpu.VMEM((TILE, TILE), F32), pltpu.VMEM((slots, side, side), F32)]
+        + [pltpu.SMEM(a.shape, a.dtype) for a in second_far[:3]]
+        + [pltpu.VMEM(a.shape, a.dtype) for a in second_far[3:]]
+        + [pltpu.SemaphoreType.DMA((SECOND_FAR,)), pltpu.SemaphoreType.DMA((slots + 1,))],
+        out_space=anywhere,
     )
     return template, difference
 

time: 50.2 us -> 47.3 us (0.942)
  waiting for transfers between devices: 19.8 us -> 17.1 us
  local copies, waits for them, and re-layouts: 2.52 us -> 0.01 us
  Pallas kernels: 8.43 us -> 10.5 us
    ppermute x17, waiting for transfers between devices: 19.8 us -> 17.1 us  [flip(): return lax.ppermute(value, axis, [(d, d ^ mask) for d in range(size)])]
    unnamed x18 -> x4, local copies, waits for them, and re-layouts: 2.52 us -> 0.01 us
    pallas_call x7, Pallas kernels: 8.43 us -> 10.5 us  [call(): pl.pallas_call(function, out_shape=outs, in_specs=specs or [vmem] * len(i...]
  transfers between devices with their start and end apart: 17 -> 17, of which waited for: 10 -> 10; matrix products, arithmetic and copies ran while one was open for 0% -> 0% of each run, Pallas kernels for 2% -> 5%
where the time goes in v4:
time: 47.3 us; the launch traced here: 47 us
  starting transfers between devices  18 us (38%)
  waiting for transfers between devices  17.1 us (36%)
  Pallas kernels  10.5 us (22%)
  between operations  1.45 us (3%)
    ppermute x17, starting transfers between devices, flip(): return lax.ppermute(value, axis, [(d, d ^ mask) for d in range(size)])  18 us
    ppermute x17, waiting for transfers between devices, flip(): return lax.ppermute(value, axis, [(d, d ^ mask) for d in range(size)])  17.1 us
    pallas_call x7, Pallas kernels, call(): pl.pallas_call(function, out_shape=outs, in_specs=specs or [vmem] * len(i...  10.5 us
  transfers between devices with their start and end apart: 17, of which 10 were waited for; matrix products, arithmetic and copies ran while one was open for 0% of the time, Pallas kernels for 5%

profile of v4, /device:TPU:0, one launch (start us, length us, event | category | flops | bytes accessed | tf_op | source)
XLA Modules:
  0.0 47.0 jit_solution(12779008689520235264)
XLA Ops:
  0.6 0.0 copy-start
  0.6 0.0 copy-start.1
  1.4 3.6 %shard_map.132 = (f32[264,128]{1,0:T(8,128)S(1)}, f32[264,128]{1,0:T(8,128)S(1)}) custom-call(f32[1,3,4,49]{3,2,1,0:T(4,128)} %bitcast.3, bf16[64,896]{1,0:T(8,128)(2,1)} %constant.10.clone.refs_1_, bf16[64,896]{1,0:T(8,128)(2,1)} %constant.11.clone.refs_2_, f32[1,4,128,128]{3,2,1,0:T(8,128)} %refs_7_.3, bf16[128,896]{1,0:T(8,128)(2,1)} %constant.8.clone.refs_4_.refs_1_, ...), custom_call_target="tpu_custom_call" | custom-call | tf_op jit(solution)/shard_map/pallas_call | solution.py:421
  5.0 0.6 %collective-permute-start = (f32[264,128]{1,0:T(8,128)S(1)}, f32[264,128]{1,0:T(8,128)S(1)}, u32[]{:S(2)}, u32[]{:S(2)}) collective-permute-start(f32[264,128]{1,0:T(8,128)S(1)} %get-tuple-element.13), channel_id=1, source_target_pairs={{0,4},{4,0},{8,12},{12,8},{16,20},{20,16},{24,28},{28,24},{1,5},{5... | collective-permute-start | bytes 405512 | tf_op jit(solution)/shard_map/ppermute | solution.py:442
  5.6 1.0 %collective-permute-done.refs_1_ = f32[264,128]{1,0:T(8,128)S(1)} collective-permute-done((f32[264,128]{1,0:T(8,128)S(1)}, f32[264,128]{1,0:T(8,128)S(1)}, u32[]{:S(2)}, u32[]{:S(2)}) %collective-permute-start) | collective-permute-done | bytes 135200 | tf_op jit(solution)/shard_map/ppermute | solution.py:442
  6.6 2.9 %collective-permute-start.1 = (f32[136,128]{1,0:T(8,128)S(1)}, f32[136,128]{1,0:T(8,128)S(1)}, u32[]{:S(2)}, u32[]{:S(2)}) collective-permute-start(f32[136,128]{1,0:T(8,128)S(1)} %get-tuple-element.15), channel_id=1, source_target_pairs={{0,8},{4,12},{8,0},{12,4},{16,24},{20,28},{24,16},{28,20},{1,9},{5... | collective-permute-start | bytes 208904 | tf_op jit(solution)/shard_map/ppermute | solution.py:442
  9.5 1.5 %collective-permute-start.2 = (f32[136,128]{1,0:T(8,128)S(1)}, f32[136,128]{1,0:T(8,128)S(1)}, u32[]{:S(2)}, u32[]{:S(2)}) collective-permute-start(f32[136,128]{1,0:T(8,128)S(1)} %get-tuple-element.16), channel_id=1, source_target_pairs={{0,16},{4,20},{8,24},{12,28},{16,0},{20,4},{24,8},{28,12},{1,17},{... | collective-permute-start | bytes 208904 | tf_op jit(solution)/shard_map/ppermute | solution.py:442
  11.0 0.0 collective-permute-start.3
  11.0 1.0 %collective-permute-done.1.refs_1_ = f32[136,128]{1,0:T(8,128)S(1)} collective-permute-done((f32[136,128]{1,0:T(8,128)S(1)}, f32[136,128]{1,0:T(8,128)S(1)}, u32[]{:S(2)}, u32[]{:S(2)}) %collective-permute-start.1) | collective-permute-done | bytes 69664 | tf_op jit(solution)/shard_map/ppermute | solution.py:442
  12.0 1.8 %collective-permute-done.2.refs_2_ = f32[136,128]{1,0:T(8,128)S(1)} collective-permute-done((f32[136,128]{1,0:T(8,128)S(1)}, f32[136,128]{1,0:T(8,128)S(1)}, u32[]{:S(2)}, u32[]{:S(2)}) %collective-permute-start.2) | collective-permute-done | bytes 69664 | tf_op jit(solution)/shard_map/ppermute | solution.py:442
  13.8 2.4 %collective-permute-done.3.refs_3_ = f32[136,128]{1,0:T(8,128)S(1)} collective-permute-done((f32[136,128]{1,0:T(8,128)S(1)}, f32[136,128]{1,0:T(8,128)S(1)}, u32[]{:S(2)}, u32[]{:S(2)}) %collective-permute-start.3) | collective-permute-done | bytes 69664 | tf_op jit(solution)/shard_map/ppermute | solution.py:442
  16.2 1.0 %shard_map.134 = (f32[72,128]{1,0:T(8,128)S(1)}, f32[72,128]{1,0:T(8,128)S(1)}, f32[72,128]{1,0:T(8,128)S(1)}, f32[72,128]{1,0:T(8,128)S(1)}) custom-call(f32[136,128]{1,0:T(8,128)S(1)} %get-tuple-element.14.refs_0_, f32[136,128]{1,0:T(8,128)S(1)} %collective-permute-done.1.refs_1_, f32[136,128]{1,0:T(8,128)S(1)} %collective-permute-done.2.refs_2_, ...), custom_call_target="tpu_custom_call" | custom-call | tf_op jit(solution)/shard_map/pallas_call | solution.py:421
  17.2 1.6 %collective-permute-start.4 = (f32[72,128]{1,0:T(8,128)S(1)}, f32[72,128]{1,0:T(8,128)S(1)}, u32[]{:S(2)}, u32[]{:S(2)}) collective-permute-start(f32[72,128]{1,0:T(8,128)S(1)} %get-tuple-element.19), channel_id=1, source_target_pairs={{0,1},{1,0},{2,3},{3,2},{4,5},{5,4},{6,7},{7,6},{8,9},{9,8},{10,11... | collective-permute-start | bytes 110600 | tf_op jit(solution)/shard_map/ppermute | solution.py:442
  18.8 2.6 %collective-permute-start.5 = (f32[72,128]{1,0:T(8,128)S(1)}, f32[72,128]{1,0:T(8,128)S(1)}, u32[]{:S(2)}, u32[]{:S(2)}) collective-permute-start(f32[72,128]{1,0:T(8,128)S(1)} %get-tuple-element.20), channel_id=1, source_target_pairs={{0,2},{1,3},{2,0},{3,1},{4,6},{5,7},{6,4},{7,5},{8,10},{9,11},{10,... | collective-permute-start | bytes 110600 | tf_op jit(solution)/shard_map/ppermute | solution.py:442
  21.4 0.2 collective-permute-start.6
  21.6 0.0 collective-permute-done.4.refs_1_
  21.6 2.8 %collective-permute-done.5.refs_2_ = f32[72,128]{1,0:T(8,128)S(1)} collective-permute-done((f32[72,128]{1,0:T(8,128)S(1)}, f32[72,128]{1,0:T(8,128)S(1)}, u32[]{:S(2)}, u32[]{:S(2)}) %collective-permute-start.5) | collective-permute-done | bytes 36896 | tf_op jit(solution)/shard_map/ppermute | solution.py:442
  24.4 2.8 %collective-permute-done.6.refs_3_ = f32[72,128]{1,0:T(8,128)S(1)} collective-permute-done((f32[72,128]{1,0:T(8,128)S(1)}, f32[72,128]{1,0:T(8,128)S(1)}, u32[]{:S(2)}, u32[]{:S(2)}) %collective-permute-start.6) | collective-permute-done | bytes 36896 | tf_op jit(solution)/shard_map/ppermute | solution.py:442
  27.2 0.2 shard_map.135.refs_0_
  27.4 0.5 %collective-permute-start.9 = (f32[64,128]{1,0:T(8,128)S(1)}, f32[64,128]{1,0:T(8,128)S(1)}, u32[]{:S(2)}, u32[]{:S(2)}) collective-permute-start(f32[64,128]{1,0:T(8,128)S(1)} %shard_map.135.refs_0_), channel_id=1, source_target_pairs={{0,3},{1,2},{2,1},{3,0},{4,7},{5,6},{6,5},{7,4},{8,11},{9,10},{10,... | collective-permute-start | bytes 98312 | tf_op jit(solution)/shard_map/ppermute | solution.py:442
  27.9 0.0 collective-permute-start.8
  27.9 4.0 %collective-permute-start.7 = (f32[64,128]{1,0:T(8,128)S(1)}, f32[64,128]{1,0:T(8,128)S(1)}, u32[]{:S(2)}, u32[]{:S(2)}) collective-permute-start(f32[64,128]{1,0:T(8,128)S(1)} %shard_map.135.refs_0_), channel_id=1, source_target_pairs={{0,1},{1,0},{2,3},{3,2},{4,5},{5,4},{6,7},{7,6},{8,9},{9,8},{10,11... | collective-permute-start | bytes 98312 | tf_op jit(solution)/shard_map/ppermute | solution.py:442
  31.8 1.3 %collective-permute-done.9.refs_3_ = f32[64,128]{1,0:T(8,128)S(1)} collective-permute-done((f32[64,128]{1,0:T(8,128)S(1)}, f32[64,128]{1,0:T(8,128)S(1)}, u32[]{:S(2)}, u32[]{:S(2)}) %collective-permute-start.9) | collective-permute-done | bytes 32800 | tf_op jit(solution)/shard_map/ppermute | solution.py:442
  33.2 0.0 collective-permute-done.8.refs_2_
  33.2 0.6 %collective-permute-done.7.refs_1_ = f32[64,128]{1,0:T(8,128)S(1)} collective-permute-done((f32[64,128]{1,0:T(8,128)S(1)}, f32[64,128]{1,0:T(8,128)S(1)}, u32[]{:S(2)}, u32[]{:S(2)}) %collective-permute-start.7) | collective-permute-done | bytes 32800 | tf_op jit(solution)/shard_map/ppermute | solution.py:442
  33.8 0.6 %collective-permute-start.12 = (f32[256,128]{1,0:T(8,128)S(1)}, f32[256,128]{1,0:T(8,128)S(1)}, u32[]{:S(2)}, u32[]{:S(2)}) collective-permute-start(f32[256,128]{1,0:T(8,128)S(1)} %shard_map.136.refs_8_), channel_id=1, source_target_pairs={{0,24},{4,28},{8,16},{12,20},{16,8},{20,12},{24,0},{28,4},{1,25},{... | collective-permute-start | bytes 393224 | tf_op jit(solution)/shard_map/ppermute | solution.py:442
  34.4 1.4 %collective-permute-start.11 = (f32[256,128]{1,0:T(8,128)S(1)}, f32[256,128]{1,0:T(8,128)S(1)}, u32[]{:S(2)}, u32[]{:S(2)}) collective-permute-start(f32[256,128]{1,0:T(8,128)S(1)} %shard_map.136.refs_8_), channel_id=1, source_target_pairs={{0,16},{4,20},{8,24},{12,28},{16,0},{20,4},{24,8},{28,12},{1,17},{... | collective-permute-start | bytes 393224 | tf_op jit(solution)/shard_map/ppermute | solution.py:442
  35.8 1.5 %collective-permute-start.10 = (f32[256,128]{1,0:T(8,128)S(1)}, f32[256,128]{1,0:T(8,128)S(1)}, u32[]{:S(2)}, u32[]{:S(2)}) collective-permute-start(f32[256,128]{1,0:T(8,128)S(1)} %shard_map.136.refs_8_), channel_id=1, source_target_pairs={{0,8},{4,12},{8,0},{12,4},{16,24},{20,28},{24,16},{28,20},{1,9},{5... | collective-permute-start | bytes 393224 | tf_op jit(solution)/shard_map/ppermute | solution.py:442
  37.3 0.0 collective-permute-start.13
  37.3 2.5 %collective-permute-done.12.refs_11_ = f32[256,128]{1,0:T(8,128)S(1)} collective-permute-done((f32[256,128]{1,0:T(8,128)S(1)}, f32[256,128]{1,0:T(8,128)S(1)}, u32[]{:S(2)}, u32[]{:S(2)}) %collective-permute-start.12) | collective-permute-done | bytes 131104 | tf_op jit(solution)/shard_map/ppermute | solution.py:442
  39.8 0.0 collective-permute-start.16
  39.8 1.0 %collective-permute-done.11.refs_10_ = f32[256,128]{1,0:T(8,128)S(1)} collective-permute-done((f32[256,128]{1,0:T(8,128)S(1)}, f32[256,128]{1,0:T(8,128)S(1)}, u32[]{:S(2)}, u32[]{:S(2)}) %collective-permute-start.11) | collective-permute-done | bytes 131104 | tf_op jit(solution)/shard_map/ppermute | solution.py:442
  40.8 0.0 collective-permute-start.15
  40.8 0.0 collective-permute-done.10.refs_9_
  40.8 0.5 %collective-permute-start.14 = (f32[256,128]{1,0:T(8,128)S(1)}, f32[256,128]{1,0:T(8,128)S(1)}, u32[]{:S(2)}, u32[]{:S(2)}) collective-permute-start(f32[256,128]{1,0:T(8,128)S(1)} %collective-permute-done.10.refs_9_), channel_id=1, source_target_pairs={{0,4},{4,0},{8,12},{12,8},{16,20},{20,16},{24,28},{28,24},{1,5},{5... | collective-permute-start | bytes 393224 | tf_op jit(solution)/shard_map/ppermute | solution.py:442
  41.3 2.2 %shard_map.131.refs_0_ = bf16[4,512,896]{2,1,0:T(8,128)(2,1)S(1)} custom-call(f32[1,3,4,49]{3,2,1,0:T(4,128)} %bitcast.4, bf16[64,896]{1,0:T(8,128)(2,1)} %constant.10.clone.refs_1_, bf16[64,896]{1,0:T(8,128)(2,1)} %constant.11.clone.refs_2_), custom_call_target="tpu_custom_call" | custom-call | tf_op jit(solution)/shard_map/pallas_call | solution.py:421
  43.5 0.0 collective-permute-done.13.refs_12_
  43.5 0.0 collective-permute-done.16.refs_15_
  43.5 0.0 collective-permute-done.15.refs_14_
  43.5 0.0 collective-permute-done.14.refs_13_
  43.5 0.0 copy-done
  43.5 0.0 copy-done.1
  43.5 3.5 %shard_map.137 = (f32[1,256,256]{2,1,0:T(8,128)}, f32[1,4,128,128]{3,2,1,0:T(8,128)}) custom-call(bf16[4,512,896]{2,1,0:T(8,128)(2,1)S(1)} %shard_map.131.refs_0_, bf16[128,896]{1,0:T(8,128)(2,1)S(1)} %copy-done.1, bf16[128,896]{1,0:T(8,128)(2,1)S(1)} %copy-done, s32[1,1]{1,0:T(1,128)S(6)} %copy.14.refs_10_.refs_3_, s32[1,4]{1,0:T(1,128)} %refs_4_.2, ...), custom_call_target="tpu_custom_call" | custom-call | tf_op jit(solution)/shard_map/pallas_call | solution.py:421
  (2 shorter events, 0.0 us)
Async XLA Ops:
  0.6 42.9 %copy-start = (bf16[128,896]{1,0:T(8,128)(2,1)S(1)}, bf16[128,896]{1,0:T(8,128)(2,1)}, u32[]{:S(2)}) copy-start(bf16[128,896]{1,0:T(8,128)(2,1)} %constant.9.clone.refs_5_.refs_2_) | copy-start | bytes 688132
  0.6 42.9 %copy-start.1 = (bf16[128,896]{1,0:T(8,128)(2,1)S(1)}, bf16[128,896]{1,0:T(8,128)(2,1)}, u32[]{:S(2)}) copy-start(bf16[128,896]{1,0:T(8,128)(2,1)} %constant.8.clone.refs_4_.refs_1_) | copy-start | bytes 688132
  5.0 1.6 %collective-permute-start = (f32[264,128]{1,0:T(8,128)S(1)}, f32[264,128]{1,0:T(8,128)S(1)}, u32[]{:S(2)}, u32[]{:S(2)}) collective-permute-start(f32[264,128]{1,0:T(8,128)S(1)} %get-tuple-element.13), channel_id=1, source_target_pairs={{0,4},{4,0},{8,12},{12,8},{16,20},{20,16},{24,28},{28,24},{1,5},{5... | collective-permute-start | bytes 405512 | tf_op jit(solution)/shard_map/ppermute | solution.py:442
  6.6 5.4 %collective-permute-start.1 = (f32[136,128]{1,0:T(8,128)S(1)}, f32[136,128]{1,0:T(8,128)S(1)}, u32[]{:S(2)}, u32[]{:S(2)}) collective-permute-start(f32[136,128]{1,0:T(8,128)S(1)} %get-tuple-element.15), channel_id=1, source_target_pairs={{0,8},{4,12},{8,0},{12,4},{16,24},{20,28},{24,16},{28,20},{1,9},{5... | collective-permute-start | bytes 208904 | tf_op jit(solution)/shard_map/ppermute | solution.py:442
  9.5 4.3 %collective-permute-start.2 = (f32[136,128]{1,0:T(8,128)S(1)}, f32[136,128]{1,0:T(8,128)S(1)}, u32[]{:S(2)}, u32[]{:S(2)}) collective-permute-start(f32[136,128]{1,0:T(8,128)S(1)} %get-tuple-element.16), channel_id=1, source_target_pairs={{0,16},{4,20},{8,24},{12,28},{16,0},{20,4},{24,8},{28,12},{1,17},{... | collective-permute-start | bytes 208904 | tf_op jit(solution)/shard_map/ppermute | solution.py:442
  11.0 5.2 %collective-permute-start.3 = (f32[136,128]{1,0:T(8,128)S(1)}, f32[136,128]{1,0:T(8,128)S(1)}, u32[]{:S(2)}, u32[]{:S(2)}) collective-permute-start(f32[136,128]{1,0:T(8,128)S(1)} %get-tuple-element.17), channel_id=1, source_target_pairs={{0,24},{4,28},{8,16},{12,20},{16,8},{20,12},{24,0},{28,4},{1,25},{... | collective-permute-start | bytes 208904 | tf_op jit(solution)/shard_map/ppermute | solution.py:442
  17.2 4.5 %collective-permute-start.4 = (f32[72,128]{1,0:T(8,128)S(1)}, f32[72,128]{1,0:T(8,128)S(1)}, u32[]{:S(2)}, u32[]{:S(2)}) collective-permute-start(f32[72,128]{1,0:T(8,128)S(1)} %get-tuple-element.19), channel_id=1, source_target_pairs={{0,1},{1,0},{2,3},{3,2},{4,5},{5,4},{6,7},{7,6},{8,9},{9,8},{10,11... | collective-permute-start | bytes 110600 | tf_op jit(solution)/shard_map/ppermute | solution.py:442
  18.8 5.6 %collective-permute-start.5 = (f32[72,128]{1,0:T(8,128)S(1)}, f32[72,128]{1,0:T(8,128)S(1)}, u32[]{:S(2)}, u32[]{:S(2)}) collective-permute-start(f32[72,128]{1,0:T(8,128)S(1)} %get-tuple-element.20), channel_id=1, source_target_pairs={{0,2},{1,3},{2,0},{3,1},{4,6},{5,7},{6,4},{7,5},{8,10},{9,11},{10,... | collective-permute-start | bytes 110600 | tf_op jit(solution)/shard_map/ppermute | solution.py:442
  21.4 5.8 %collective-permute-start.6 = (f32[72,128]{1,0:T(8,128)S(1)}, f32[72,128]{1,0:T(8,128)S(1)}, u32[]{:S(2)}, u32[]{:S(2)}) collective-permute-start(f32[72,128]{1,0:T(8,128)S(1)} %get-tuple-element.21), channel_id=1, source_target_pairs={{0,3},{1,2},{2,1},{3,0},{4,7},{5,6},{6,5},{7,4},{8,11},{9,10},{10,... | collective-permute-start | bytes 110600 | tf_op jit(solution)/shard_map/ppermute | solution.py:442
  27.4 5.8 %collective-permute-start.9 = (f32[64,128]{1,0:T(8,128)S(1)}, f32[64,128]{1,0:T(8,128)S(1)}, u32[]{:S(2)}, u32[]{:S(2)}) collective-permute-start(f32[64,128]{1,0:T(8,128)S(1)} %shard_map.135.refs_0_), channel_id=1, source_target_pairs={{0,3},{1,2},{2,1},{3,0},{4,7},{5,6},{6,5},{7,4},{8,11},{9,10},{10,... | collective-permute-start | bytes 98312 | tf_op jit(solution)/shard_map/ppermute | solution.py:442
  27.9 5.3 %collective-permute-start.8 = (f32[64,128]{1,0:T(8,128)S(1)}, f32[64,128]{1,0:T(8,128)S(1)}, u32[]{:S(2)}, u32[]{:S(2)}) collective-permute-start(f32[64,128]{1,0:T(8,128)S(1)} %shard_map.135.refs_0_), channel_id=1, source_target_pairs={{0,2},{1,3},{2,0},{3,1},{4,6},{5,7},{6,4},{7,5},{8,10},{9,11},{10,... | collective-permute-start | bytes 98312 | tf_op jit(solution)/shard_map/ppermute | solution.py:442
  27.9 5.8 %collective-permute-start.7 = (f32[64,128]{1,0:T(8,128)S(1)}, f32[64,128]{1,0:T(8,128)S(1)}, u32[]{:S(2)}, u32[]{:S(2)}) collective-permute-start(f32[64,128]{1,0:T(8,128)S(1)} %shard_map.135.refs_0_), channel_id=1, source_target_pairs={{0,1},{1,0},{2,3},{3,2},{4,5},{5,4},{6,7},{7,6},{8,9},{9,8},{10,11... | collective-permute-start | bytes 98312 | tf_op jit(solution)/shard_map/ppermute | solution.py:442
  33.8 6.0 %collective-permute-start.12 = (f32[256,128]{1,0:T(8,128)S(1)}, f32[256,128]{1,0:T(8,128)S(1)}, u32[]{:S(2)}, u32[]{:S(2)}) collective-permute-start(f32[256,128]{1,0:T(8,128)S(1)} %shard_map.136.refs_8_), channel_id=1, source_target_pairs={{0,24},{4,28},{8,16},{12,20},{16,8},{20,12},{24,0},{28,4},{1,25},{... | collective-permute-start | bytes 393224 | tf_op jit(solution)/shard_map/ppermute | solution.py:442
  34.4 6.4 %collective-permute-start.11 = (f32[256,128]{1,0:T(8,128)S(1)}, f32[256,128]{1,0:T(8,128)S(1)}, u32[]{:S(2)}, u32[]{:S(2)}) collective-permute-start(f32[256,128]{1,0:T(8,128)S(1)} %shard_map.136.refs_8_), channel_id=1, source_target_pairs={{0,16},{4,20},{8,24},{12,28},{16,0},{20,4},{24,8},{28,12},{1,17},{... | collective-permute-start | bytes 393224 | tf_op jit(solution)/shard_map/ppermute | solution.py:442
  35.8 5.0 %collective-permute-start.10 = (f32[256,128]{1,0:T(8,128)S(1)}, f32[256,128]{1,0:T(8,128)S(1)}, u32[]{:S(2)}, u32[]{:S(2)}) collective-permute-start(f32[256,128]{1,0:T(8,128)S(1)} %shard_map.136.refs_8_), channel_id=1, source_target_pairs={{0,8},{4,12},{8,0},{12,4},{16,24},{20,28},{24,16},{28,20},{1,9},{5... | collective-permute-start | bytes 393224 | tf_op jit(solution)/shard_map/ppermute | solution.py:442
  37.3 6.1 %collective-permute-start.13 = (f32[256,128]{1,0:T(8,128)S(1)}, f32[256,128]{1,0:T(8,128)S(1)}, u32[]{:S(2)}, u32[]{:S(2)}) collective-permute-start(f32[256,128]{1,0:T(8,128)S(1)} %shard_map.136.refs_8_), channel_id=1, source_target_pairs={{0,4},{4,0},{8,12},{12,8},{16,20},{20,16},{24,28},{28,24},{1,5},{5... | collective-permute-start | bytes 393224 | tf_op jit(solution)/shard_map/ppermute | solution.py:442
  39.8 3.7 %collective-permute-start.16 = (f32[256,128]{1,0:T(8,128)S(1)}, f32[256,128]{1,0:T(8,128)S(1)}, u32[]{:S(2)}, u32[]{:S(2)}) collective-permute-start(f32[256,128]{1,0:T(8,128)S(1)} %collective-permute-done.12.refs_11_), channel_id=1, source_target_pairs={{0,4},{4,0},{8,12},{12,8},{16,20},{20,16},{24,28},{28,24},{1,5},{5... | collective-permute-start | bytes 393224 | tf_op jit(solution)/shard_map/ppermute | solution.py:442
  40.8 2.7 %collective-permute-start.15 = (f32[256,128]{1,0:T(8,128)S(1)}, f32[256,128]{1,0:T(8,128)S(1)}, u32[]{:S(2)}, u32[]{:S(2)}) collective-permute-start(f32[256,128]{1,0:T(8,128)S(1)} %collective-permute-done.11.refs_10_), channel_id=1, source_target_pairs={{0,4},{4,0},{8,12},{12,8},{16,20},{20,16},{24,28},{28,24},{1,5},{5... | collective-permute-start | bytes 393224 | tf_op jit(solution)/shard_map/ppermute | solution.py:442
  40.8 2.7 %collective-permute-start.14 = (f32[256,128]{1,0:T(8,128)S(1)}, f32[256,128]{1,0:T(8,128)S(1)}, u32[]{:S(2)}, u32[]{:S(2)}) collective-permute-start(f32[256,128]{1,0:T(8,128)S(1)} %collective-permute-done.10.refs_9_), channel_id=1, source_target_pairs={{0,4},{4,0},{8,12},{12,8},{16,20},{20,16},{24,28},{28,24},{1,5},{5... | collective-permute-start | bytes 393224 | tf_op jit(solution)/shard_map/ppermute | solution.py:442

commit v5 on v4

--- a/solution.py
+++ b/solution.py
@@ -132,7 +132,6 @@
 
 
 FIRST_FAR = 10
-SECOND_FAR = 4
 
 
 def fetch(sources, targets, semaphores):
@@ -324,23 +323,18 @@
 
 def stack_kernel(tiles, strip, *refs):
     sources, out = refs[:tiles], refs[tiles]
-    sky = lax.axis_index("sky")
     size = 2 * strip
     for j in range(tiles):
-        out[pl.ds((sky ^ j) * size, size), :] = sources[j][...]
+        out[pl.ds(j * size, size), :] = sources[j][...]
 
 
 def second_kernel(
     slots, side, tiles, strip, peers,
-    left, across_high, across_low, counts,
+    left, across_high, across_low, science, counts, places,
     *refs,
 ):
-    far, refs = refs[:SECOND_FAR], refs[SECOND_FAR:]
     pieces, refs = refs[: 2 * peers], refs[2 * peers :]
-    template, difference, images, right, total, staged, results = refs[:7]
-    wait, near = fetch(far, refs[7 : 7 + SECOND_FAR], refs[-2])
-    slot_tile, offsets, tile_place, science = near
-    outward = refs[-1]
+    template, difference, images, right, total, staged, results, outward = refs
     visit = lax.axis_index("visit")
     sky = lax.axis_index("sky")
     core = visit % 2
@@ -352,7 +346,7 @@
 
             def spread_rows(t, residue=residue, piece=piece):
                 for h in range(2):
-                    total[t, h, pl.ds(residue, strip, stride=2 * peers), :] = piece[
+                    total[sky ^ t, h, pl.ds(residue, strip, stride=2 * peers), :] = piece[
                         pl.ds((t * 2 + h) * strip, strip), :
                     ]
 
@@ -361,12 +355,9 @@
         staged[:, h * LANES : (h + 1) * LANES] = total[sky, h]
     copies = [pltpu.make_async_copy(staged, template.at[0], outward.at[slots])]
     copies[0].start()
-    wait(*range(SECOND_FAR))
     col = lax.broadcasted_iota(jnp.int32, (side, side), 1)
     for b in range(slots):
-        owner = tile_place[slot_tile[0, b]]
-        top = offsets[0, 0, b]
-        left_edge = offsets[0, 1, b]
+        owner, top, left_edge = places[0, b], places[1, b], places[2, b]
         joined = jnp.where(
             col >= left_edge, total[owner, 0, pl.ds(top, side), :], total[owner, 1, pl.ds(top, side), :]
         )
@@ -381,10 +372,20 @@
         copy.wait()
 
 
-def prepare_kernel(slots, side, coef, rows_high, rows_low, left, coef_buf, tap_buf):
+def prepare_kernel(
+    slots, side, coef, rows_high, rows_low, slot_tile, offsets, tile_place, *refs,
+):
+    left, places = refs[3:5]
+    coef_buf, tap_buf, semaphores = refs[8:]
+    wait, _ = fetch(refs[:3], refs[5:8], semaphores)
+    for b in range(slots):
+        places[0, b] = tile_place[slot_tile[0, b]]
+        places[1, b] = offsets[0, 0, b]
+        places[2, b] = offsets[0, 1, b]
     tap_rows(coef, coef_buf, tap_buf, rows_high, rows_low, slots)
     for b in range(slots):
         build_left(b, slots, side, tap_buf, left)
+    wait(0, 1, 2)
 
 
 def body(science, coef_first, coef_second, weight, slot_tile, offsets, counts, tile_place):
@@ -422,7 +423,9 @@
             function,
             out_shape=outs,
             in_specs=specs or [vmem] * len(ins),
-            out_specs=jax.tree.map(lambda _: out_space, outs),
+            out_specs=out_space
+            if isinstance(out_space, list)
+            else jax.tree.map(lambda _: out_space, outs),
             scratch_shapes=list(scratch),
             compiler_params=pltpu.CompilerParams(vmem_limit_bytes=VMEM_BYTES),
         )(*ins)
@@ -464,11 +467,17 @@
         + [pltpu.SMEM(a.shape, a.dtype) for a in first_far[6:]]
         + [pltpu.SemaphoreType.DMA((FIRST_FAR,))],
     )
-    left = call(
+    ready = (across_high, across_low, science)
+    left, places, *ready = call(
         lambda *refs: prepare_kernel(slots, side, *refs),
-        (far(coef_second), far(rows_high), far(rows_low)),
-        pltpu.VMEM(left_shape, BF16),
-        scratch=tap_scratch,
+        tuple(
+            map(far, (coef_second, rows_high, rows_low, slot_tile, offsets, tile_place, *ready))
+        ),
+        [pltpu.VMEM(left_shape, BF16), pltpu.SMEM((3, slots), jnp.int32)]
+        + [pltpu.VMEM(a.shape, a.dtype) for a in ready],
+        specs=[vmem] * 3 + [smem] * 3 + [anywhere] * 3,
+        scratch=tap_scratch + [pltpu.SemaphoreType.DMA((3,))],
+        out_space=[vmem, smem] + [vmem] * 3,
     )
     received = flip(send, "visit", visits, 1)
     pieces = call(
@@ -489,12 +498,12 @@
         + [pltpu.VMEM((tiles, 2, strip, LANES), F32)] * min(peers, 4),
     )
     arrived = exchange(pieces, "sky", tiles, 1)
-    strips = call(
+    strip_own = call(
         lambda *refs: template_kernel(tiles, strip, visits, meta_blocks, side, *refs),
         [near(a) for a in arrived],
         shape(2 * strip, LANES),
     )
-    strips = exchange([strips] * tiles, "sky", tiles, 1)
+    strips = exchange([strip_own] * tiles, "sky", tiles, 1)
     piece = call(
         lambda *refs: stack_kernel(tiles, strip, *refs),
         [near(a) for a in strips],
@@ -502,18 +511,16 @@
     )
     mine = exchange([piece] * peers, "visit", visits, 2)
     theirs = [flip(p, "visit", visits, 1) for p in mine]
-    second_far = (slot_tile, offsets, tile_place, science)
     template, difference = call(
         lambda *refs: second_kernel(slots, side, tiles, strip, peers, *refs),
-        (near(left), near(across_high), near(across_low), counts,
-         *map(far, second_far), *map(near, mine), *map(near, theirs)),
+        (near(left), *map(near, ready), counts,
+         pltpu.with_memory_space_constraint(places, pltpu.SMEM),
+         *map(near, mine), *map(near, theirs)),
         [jax.ShapeDtypeStruct(d, F32) for d in ((1, TILE, TILE), (1, slots, side, side))],
-        specs=[vmem] * 3 + [smem] + [anywhere] * SECOND_FAR + [vmem] * (2 * peers),
+        specs=[vmem] * 4 + [smem] * 2 + [vmem] * (2 * peers),
         scratch=pass_scratch
         + [pltpu.VMEM((TILE, TILE), F32), pltpu.VMEM((slots, side, side), F32)]
-        + [pltpu.SMEM(a.shape, a.dtype) for a in second_far[:3]]
-        + [pltpu.VMEM(a.shape, a.dtype) for a in second_far[3:]]
-        + [pltpu.SemaphoreType.DMA((SECOND_FAR,)), pltpu.SemaphoreType.DMA((slots + 1,))],
+        + [pltpu.SemaphoreType.DMA((slots + 1,))],
         out_space=anywhere,
     )
     return template, difference

time: 47.3 us -> 47.6 us (level)
  Pallas kernels: 10.5 us -> 11 us
  transfers between devices with their start and end apart: 17 -> 17, of which waited for: 10 -> 10; matrix products, arithmetic and copies ran while one was open for 0% -> 0% of each run, Pallas kernels for 5% -> 7%
where the time goes in v5:
time: 47.6 us; the launch traced here: 47.4 us
  starting transfers between devices  18 us (38%)
  waiting for transfers between devices  17.1 us (36%)
  Pallas kernels  11 us (23%)
  between operations  1.36 us (3%)
    ppermute x17, starting transfers between devices, flip(): return lax.ppermute(value, axis, [(d, d ^ mask) for d in range(size)])  18 us
    ppermute x17, waiting for transfers between devices, flip(): return lax.ppermute(value, axis, [(d, d ^ mask) for d in range(size)])  17.1 us
    pallas_call x7, Pallas kernels, call(): pl.pallas_call(function, out_shape=outs, in_specs=specs or [vmem] * len(i...  11 us
  transfers between devices with their start and end apart: 17, of which 10 were waited for; matrix products, arithmetic and copies ran while one was open for 0% of the time, Pallas kernels for 7%

profile of v5, /device:TPU:0, one launch (start us, length us, event | category | flops | bytes accessed | tf_op | source)
XLA Modules:
  0.0 47.4 jit_solution(12689459721891815906)
XLA Ops:
  1.3 3.6 %shard_map.132 = (f32[264,128]{1,0:T(8,128)S(1)}, f32[264,128]{1,0:T(8,128)S(1)}) custom-call(f32[1,3,4,49]{3,2,1,0:T(4,128)} %bitcast.3, bf16[64,896]{1,0:T(8,128)(2,1)} %constant.10.clone.refs_1_, bf16[64,896]{1,0:T(8,128)(2,1)} %constant.11.clone.refs_2_, f32[1,4,128,128]{3,2,1,0:T(8,128)} %refs_3_.3, bf16[128,896]{1,0:T(8,128)(2,1)} %constant.8.clone.refs_6_.refs_4_, ...), custom_call_target="tpu_custom_call" | custom-call | tf_op jit(solution)/shard_map/pallas_call | solution.py:422
  4.9 0.6 %collective-permute-start = (f32[264,128]{1,0:T(8,128)S(1)}, f32[264,128]{1,0:T(8,128)S(1)}, u32[]{:S(2)}, u32[]{:S(2)}) collective-permute-start(f32[264,128]{1,0:T(8,128)S(1)} %get-tuple-element.23), channel_id=1, source_target_pairs={{0,4},{4,0},{8,12},{12,8},{16,20},{20,16},{24,28},{28,24},{1,5},{5... | collective-permute-start | bytes 405512 | tf_op jit(solution)/shard_map/ppermute | solution.py:445
  5.5 1.0 %collective-permute-done.refs_1_ = f32[264,128]{1,0:T(8,128)S(1)} collective-permute-done((f32[264,128]{1,0:T(8,128)S(1)}, f32[264,128]{1,0:T(8,128)S(1)}, u32[]{:S(2)}, u32[]{:S(2)}) %collective-permute-start) | collective-permute-done | bytes 135200 | tf_op jit(solution)/shard_map/ppermute | solution.py:445
  6.5 2.9 %collective-permute-start.1 = (f32[136,128]{1,0:T(8,128)S(1)}, f32[136,128]{1,0:T(8,128)S(1)}, u32[]{:S(2)}, u32[]{:S(2)}) collective-permute-start(f32[136,128]{1,0:T(8,128)S(1)} %get-tuple-element.25), channel_id=1, source_target_pairs={{0,8},{4,12},{8,0},{12,4},{16,24},{20,28},{24,16},{28,20},{1,9},{5... | collective-permute-start | bytes 208904 | tf_op jit(solution)/shard_map/ppermute | solution.py:445
  9.4 1.5 %collective-permute-start.2 = (f32[136,128]{1,0:T(8,128)S(1)}, f32[136,128]{1,0:T(8,128)S(1)}, u32[]{:S(2)}, u32[]{:S(2)}) collective-permute-start(f32[136,128]{1,0:T(8,128)S(1)} %get-tuple-element.26), channel_id=1, source_target_pairs={{0,16},{4,20},{8,24},{12,28},{16,0},{20,4},{24,8},{28,12},{1,17},{... | collective-permute-start | bytes 208904 | tf_op jit(solution)/shard_map/ppermute | solution.py:445
  10.9 0.0 collective-permute-start.3
  10.9 1.0 %collective-permute-done.1.refs_1_ = f32[136,128]{1,0:T(8,128)S(1)} collective-permute-done((f32[136,128]{1,0:T(8,128)S(1)}, f32[136,128]{1,0:T(8,128)S(1)}, u32[]{:S(2)}, u32[]{:S(2)}) %collective-permute-start.1) | collective-permute-done | bytes 69664 | tf_op jit(solution)/shard_map/ppermute | solution.py:445
  11.9 1.8 %collective-permute-done.2.refs_2_ = f32[136,128]{1,0:T(8,128)S(1)} collective-permute-done((f32[136,128]{1,0:T(8,128)S(1)}, f32[136,128]{1,0:T(8,128)S(1)}, u32[]{:S(2)}, u32[]{:S(2)}) %collective-permute-start.2) | collective-permute-done | bytes 69664 | tf_op jit(solution)/shard_map/ppermute | solution.py:445
  13.7 2.4 %collective-permute-done.3.refs_3_ = f32[136,128]{1,0:T(8,128)S(1)} collective-permute-done((f32[136,128]{1,0:T(8,128)S(1)}, f32[136,128]{1,0:T(8,128)S(1)}, u32[]{:S(2)}, u32[]{:S(2)}) %collective-permute-start.3) | collective-permute-done | bytes 69664 | tf_op jit(solution)/shard_map/ppermute | solution.py:445
  16.1 1.0 %shard_map.134 = (f32[72,128]{1,0:T(8,128)S(1)}, f32[72,128]{1,0:T(8,128)S(1)}, f32[72,128]{1,0:T(8,128)S(1)}, f32[72,128]{1,0:T(8,128)S(1)}) custom-call(f32[136,128]{1,0:T(8,128)S(1)} %get-tuple-element.24.refs_0_, f32[136,128]{1,0:T(8,128)S(1)} %collective-permute-done.1.refs_1_, f32[136,128]{1,0:T(8,128)S(1)} %collective-permute-done.2.refs_2_, ...), custom_call_target="tpu_custom_call" | custom-call | tf_op jit(solution)/shard_map/pallas_call | solution.py:422
  17.1 1.6 %collective-permute-start.4 = (f32[72,128]{1,0:T(8,128)S(1)}, f32[72,128]{1,0:T(8,128)S(1)}, u32[]{:S(2)}, u32[]{:S(2)}) collective-permute-start(f32[72,128]{1,0:T(8,128)S(1)} %get-tuple-element.29), channel_id=1, source_target_pairs={{0,1},{1,0},{2,3},{3,2},{4,5},{5,4},{6,7},{7,6},{8,9},{9,8},{10,11... | collective-permute-start | bytes 110600 | tf_op jit(solution)/shard_map/ppermute | solution.py:445
  18.7 2.6 %collective-permute-start.5 = (f32[72,128]{1,0:T(8,128)S(1)}, f32[72,128]{1,0:T(8,128)S(1)}, u32[]{:S(2)}, u32[]{:S(2)}) collective-permute-start(f32[72,128]{1,0:T(8,128)S(1)} %get-tuple-element.30), channel_id=1, source_target_pairs={{0,2},{1,3},{2,0},{3,1},{4,6},{5,7},{6,4},{7,5},{8,10},{9,11},{10,... | collective-permute-start | bytes 110600 | tf_op jit(solution)/shard_map/ppermute | solution.py:445
  21.3 0.2 collective-permute-start.6
  21.6 0.0 collective-permute-done.4.refs_1_
  21.6 2.8 %collective-permute-done.5.refs_2_ = f32[72,128]{1,0:T(8,128)S(1)} collective-permute-done((f32[72,128]{1,0:T(8,128)S(1)}, f32[72,128]{1,0:T(8,128)S(1)}, u32[]{:S(2)}, u32[]{:S(2)}) %collective-permute-start.5) | collective-permute-done | bytes 36896 | tf_op jit(solution)/shard_map/ppermute | solution.py:445
  24.3 2.8 %collective-permute-done.6.refs_3_ = f32[72,128]{1,0:T(8,128)S(1)} collective-permute-done((f32[72,128]{1,0:T(8,128)S(1)}, f32[72,128]{1,0:T(8,128)S(1)}, u32[]{:S(2)}, u32[]{:S(2)}) %collective-permute-start.6) | collective-permute-done | bytes 36896 | tf_op jit(solution)/shard_map/ppermute | solution.py:445
  27.1 0.2 shard_map.135.refs_0_
  27.3 0.5 %collective-permute-start.9 = (f32[64,128]{1,0:T(8,128)S(1)}, f32[64,128]{1,0:T(8,128)S(1)}, u32[]{:S(2)}, u32[]{:S(2)}) collective-permute-start(f32[64,128]{1,0:T(8,128)S(1)} %shard_map.135.refs_0_), channel_id=1, source_target_pairs={{0,3},{1,2},{2,1},{3,0},{4,7},{5,6},{6,5},{7,4},{8,11},{9,10},{10,... | collective-permute-start | bytes 98312 | tf_op jit(solution)/shard_map/ppermute | solution.py:445
  27.8 0.0 collective-permute-start.8
  27.8 4.0 %collective-permute-start.7 = (f32[64,128]{1,0:T(8,128)S(1)}, f32[64,128]{1,0:T(8,128)S(1)}, u32[]{:S(2)}, u32[]{:S(2)}) collective-permute-start(f32[64,128]{1,0:T(8,128)S(1)} %shard_map.135.refs_0_), channel_id=1, source_target_pairs={{0,1},{1,0},{2,3},{3,2},{4,5},{5,4},{6,7},{7,6},{8,9},{9,8},{10,11... | collective-permute-start | bytes 98312 | tf_op jit(solution)/shard_map/ppermute | solution.py:445
  31.8 1.3 %collective-permute-done.9.refs_3_ = f32[64,128]{1,0:T(8,128)S(1)} collective-permute-done((f32[64,128]{1,0:T(8,128)S(1)}, f32[64,128]{1,0:T(8,128)S(1)}, u32[]{:S(2)}, u32[]{:S(2)}) %collective-permute-start.9) | collective-permute-done | bytes 32800 | tf_op jit(solution)/shard_map/ppermute | solution.py:445
  33.1 0.0 collective-permute-done.8.refs_2_
  33.1 0.6 %collective-permute-done.7.refs_1_ = f32[64,128]{1,0:T(8,128)S(1)} collective-permute-done((f32[64,128]{1,0:T(8,128)S(1)}, f32[64,128]{1,0:T(8,128)S(1)}, u32[]{:S(2)}, u32[]{:S(2)}) %collective-permute-start.7) | collective-permute-done | bytes 32800 | tf_op jit(solution)/shard_map/ppermute | solution.py:445
  33.7 0.6 %collective-permute-start.12 = (f32[256,128]{1,0:T(8,128)S(1)}, f32[256,128]{1,0:T(8,128)S(1)}, u32[]{:S(2)}, u32[]{:S(2)}) collective-permute-start(f32[256,128]{1,0:T(8,128)S(1)} %shard_map.136.refs_6_), channel_id=1, source_target_pairs={{0,24},{4,28},{8,16},{12,20},{16,8},{20,12},{24,0},{28,4},{1,25},{... | collective-permute-start | bytes 393224 | tf_op jit(solution)/shard_map/ppermute | solution.py:445
  34.3 1.4 %collective-permute-start.11 = (f32[256,128]{1,0:T(8,128)S(1)}, f32[256,128]{1,0:T(8,128)S(1)}, u32[]{:S(2)}, u32[]{:S(2)}) collective-permute-start(f32[256,128]{1,0:T(8,128)S(1)} %shard_map.136.refs_6_), channel_id=1, source_target_pairs={{0,16},{4,20},{8,24},{12,28},{16,0},{20,4},{24,8},{28,12},{1,17},{... | collective-permute-start | bytes 393224 | tf_op jit(solution)/shard_map/ppermute | solution.py:445
  35.7 1.5 %collective-permute-start.10 = (f32[256,128]{1,0:T(8,128)S(1)}, f32[256,128]{1,0:T(8,128)S(1)}, u32[]{:S(2)}, u32[]{:S(2)}) collective-permute-start(f32[256,128]{1,0:T(8,128)S(1)} %shard_map.136.refs_6_), channel_id=1, source_target_pairs={{0,8},{4,12},{8,0},{12,4},{16,24},{20,28},{24,16},{28,20},{1,9},{5... | collective-permute-start | bytes 393224 | tf_op jit(solution)/shard_map/ppermute | solution.py:445
  37.2 0.0 collective-permute-start.13
  37.2 2.5 %collective-permute-done.12.refs_9_ = f32[256,128]{1,0:T(8,128)S(1)} collective-permute-done((f32[256,128]{1,0:T(8,128)S(1)}, f32[256,128]{1,0:T(8,128)S(1)}, u32[]{:S(2)}, u32[]{:S(2)}) %collective-permute-start.12) | collective-permute-done | bytes 131104 | tf_op jit(solution)/shard_map/ppermute | solution.py:445
  39.7 0.0 collective-permute-start.16
  39.7 1.0 %collective-permute-done.11.refs_8_ = f32[256,128]{1,0:T(8,128)S(1)} collective-permute-done((f32[256,128]{1,0:T(8,128)S(1)}, f32[256,128]{1,0:T(8,128)S(1)}, u32[]{:S(2)}, u32[]{:S(2)}) %collective-permute-start.11) | collective-permute-done | bytes 131104 | tf_op jit(solution)/shard_map/ppermute | solution.py:445
  40.7 0.0 collective-permute-start.15
  40.7 0.0 collective-permute-done.10.refs_7_
  40.7 0.5 %collective-permute-start.14 = (f32[256,128]{1,0:T(8,128)S(1)}, f32[256,128]{1,0:T(8,128)S(1)}, u32[]{:S(2)}, u32[]{:S(2)}) collective-permute-start(f32[256,128]{1,0:T(8,128)S(1)} %collective-permute-done.10.refs_7_), channel_id=1, source_target_pairs={{0,4},{4,0},{8,12},{12,8},{16,20},{20,16},{24,28},{28,24},{1,5},{5... | collective-permute-start | bytes 393224 | tf_op jit(solution)/shard_map/ppermute | solution.py:445
  41.2 3.3 %shard_map.131 = (bf16[4,512,896]{2,1,0:T(8,128)(2,1)S(1)}, s32[3,4]{1,0:T(4,128)S(4)}, bf16[128,896]{1,0:T(8,128)(2,1)S(1)}, bf16[128,896]{1,0:T(8,128)(2,1)S(1)}, f32[1,4,128,128]{3,2,1,0:T(8,128)S(1)}) custom-call(f32[1,3,4,49]{3,2,1,0:T(4,128)} %bitcast.4, bf16[64,896]{1,0:T(8,128)(2,1)} %constant.10.clone.refs_1_, ...), custom_call_target="tpu_custom_call" | custom-call | tf_op jit(solution)/shard_map/pallas_call | solution.py:422
  44.5 0.0 collective-permute-done.13.refs_10_
  44.5 0.0 collective-permute-done.16.refs_13_
  44.5 0.0 collective-permute-done.15.refs_12_
  44.5 0.0 collective-permute-done.14.refs_11_
  44.6 2.8 %shard_map.137 = (f32[1,256,256]{2,1,0:T(8,128)}, f32[1,4,128,128]{3,2,1,0:T(8,128)}) custom-call(bf16[4,512,896]{2,1,0:T(8,128)(2,1)S(1)} %get-tuple-element.17.refs_0_, bf16[128,896]{1,0:T(8,128)(2,1)S(1)} %get-tuple-element.18.refs_1_, bf16[128,896]{1,0:T(8,128)(2,1)S(1)} %get-tuple-element.19.refs_2_, f32[1,4,128,128]{3,2,1,0:T(8,128)S(1)} %get-tuple-element.20.refs_3_, ...), custom_call_target="tpu_custom_call" | custom-call | tf_op jit(solution)/shard_map/pallas_call | solution.py:422
  (2 shorter events, 0.0 us)
Async XLA Ops:
  4.9 1.6 %collective-permute-start = (f32[264,128]{1,0:T(8,128)S(1)}, f32[264,128]{1,0:T(8,128)S(1)}, u32[]{:S(2)}, u32[]{:S(2)}) collective-permute-start(f32[264,128]{1,0:T(8,128)S(1)} %get-tuple-element.23), channel_id=1, source_target_pairs={{0,4},{4,0},{8,12},{12,8},{16,20},{20,16},{24,28},{28,24},{1,5},{5... | collective-permute-start | bytes 405512 | tf_op jit(solution)/shard_map/ppermute | solution.py:445
  6.5 5.4 %collective-permute-start.1 = (f32[136,128]{1,0:T(8,128)S(1)}, f32[136,128]{1,0:T(8,128)S(1)}, u32[]{:S(2)}, u32[]{:S(2)}) collective-permute-start(f32[136,128]{1,0:T(8,128)S(1)} %get-tuple-element.25), channel_id=1, source_target_pairs={{0,8},{4,12},{8,0},{12,4},{16,24},{20,28},{24,16},{28,20},{1,9},{5... | collective-permute-start | bytes 208904 | tf_op jit(solution)/shard_map/ppermute | solution.py:445
  9.4 4.3 %collective-permute-start.2 = (f32[136,128]{1,0:T(8,128)S(1)}, f32[136,128]{1,0:T(8,128)S(1)}, u32[]{:S(2)}, u32[]{:S(2)}) collective-permute-start(f32[136,128]{1,0:T(8,128)S(1)} %get-tuple-element.26), channel_id=1, source_target_pairs={{0,16},{4,20},{8,24},{12,28},{16,0},{20,4},{24,8},{28,12},{1,17},{... | collective-permute-start | bytes 208904 | tf_op jit(solution)/shard_map/ppermute | solution.py:445
  10.9 5.2 %collective-permute-start.3 = (f32[136,128]{1,0:T(8,128)S(1)}, f32[136,128]{1,0:T(8,128)S(1)}, u32[]{:S(2)}, u32[]{:S(2)}) collective-permute-start(f32[136,128]{1,0:T(8,128)S(1)} %get-tuple-element.27), channel_id=1, source_target_pairs={{0,24},{4,28},{8,16},{12,20},{16,8},{20,12},{24,0},{28,4},{1,25},{... | collective-permute-start | bytes 208904 | tf_op jit(solution)/shard_map/ppermute | solution.py:445
  17.1 4.5 %collective-permute-start.4 = (f32[72,128]{1,0:T(8,128)S(1)}, f32[72,128]{1,0:T(8,128)S(1)}, u32[]{:S(2)}, u32[]{:S(2)}) collective-permute-start(f32[72,128]{1,0:T(8,128)S(1)} %get-tuple-element.29), channel_id=1, source_target_pairs={{0,1},{1,0},{2,3},{3,2},{4,5},{5,4},{6,7},{7,6},{8,9},{9,8},{10,11... | collective-permute-start | bytes 110600 | tf_op jit(solution)/shard_map/ppermute | solution.py:445
  18.7 5.6 %collective-permute-start.5 = (f32[72,128]{1,0:T(8,128)S(1)}, f32[72,128]{1,0:T(8,128)S(1)}, u32[]{:S(2)}, u32[]{:S(2)}) collective-permute-start(f32[72,128]{1,0:T(8,128)S(1)} %get-tuple-element.30), channel_id=1, source_target_pairs={{0,2},{1,3},{2,0},{3,1},{4,6},{5,7},{6,4},{7,5},{8,10},{9,11},{10,... | collective-permute-start | bytes 110600 | tf_op jit(solution)/shard_map/ppermute | solution.py:445
  21.3 5.8 %collective-permute-start.6 = (f32[72,128]{1,0:T(8,128)S(1)}, f32[72,128]{1,0:T(8,128)S(1)}, u32[]{:S(2)}, u32[]{:S(2)}) collective-permute-start(f32[72,128]{1,0:T(8,128)S(1)} %get-tuple-element.31), channel_id=1, source_target_pairs={{0,3},{1,2},{2,1},{3,0},{4,7},{5,6},{6,5},{7,4},{8,11},{9,10},{10,... | collective-permute-start | bytes 110600 | tf_op jit(solution)/shard_map/ppermute | solution.py:445
  27.3 5.8 %collective-permute-start.9 = (f32[64,128]{1,0:T(8,128)S(1)}, f32[64,128]{1,0:T(8,128)S(1)}, u32[]{:S(2)}, u32[]{:S(2)}) collective-permute-start(f32[64,128]{1,0:T(8,128)S(1)} %shard_map.135.refs_0_), channel_id=1, source_target_pairs={{0,3},{1,2},{2,1},{3,0},{4,7},{5,6},{6,5},{7,4},{8,11},{9,10},{10,... | collective-permute-start | bytes 98312 | tf_op jit(solution)/shard_map/ppermute | solution.py:445
  27.8 5.3 %collective-permute-start.8 = (f32[64,128]{1,0:T(8,128)S(1)}, f32[64,128]{1,0:T(8,128)S(1)}, u32[]{:S(2)}, u32[]{:S(2)}) collective-permute-start(f32[64,128]{1,0:T(8,128)S(1)} %shard_map.135.refs_0_), channel_id=1, source_target_pairs={{0,2},{1,3},{2,0},{3,1},{4,6},{5,7},{6,4},{7,5},{8,10},{9,11},{10,... | collective-permute-start | bytes 98312 | tf_op jit(solution)/shard_map/ppermute | solution.py:445
  27.8 5.8 %collective-permute-start.7 = (f32[64,128]{1,0:T(8,128)S(1)}, f32[64,128]{1,0:T(8,128)S(1)}, u32[]{:S(2)}, u32[]{:S(2)}) collective-permute-start(f32[64,128]{1,0:T(8,128)S(1)} %shard_map.135.refs_0_), channel_id=1, source_target_pairs={{0,1},{1,0},{2,3},{3,2},{4,5},{5,4},{6,7},{7,6},{8,9},{9,8},{10,11... | collective-permute-start | bytes 98312 | tf_op jit(solution)/shard_map/ppermute | solution.py:445
  33.7 6.0 %collective-permute-start.12 = (f32[256,128]{1,0:T(8,128)S(1)}, f32[256,128]{1,0:T(8,128)S(1)}, u32[]{:S(2)}, u32[]{:S(2)}) collective-permute-start(f32[256,128]{1,0:T(8,128)S(1)} %shard_map.136.refs_6_), channel_id=1, source_target_pairs={{0,24},{4,28},{8,16},{12,20},{16,8},{20,12},{24,0},{28,4},{1,25},{... | collective-permute-start | bytes 393224 | tf_op jit(solution)/shard_map/ppermute | solution.py:445
  34.3 6.4 %collective-permute-start.11 = (f32[256,128]{1,0:T(8,128)S(1)}, f32[256,128]{1,0:T(8,128)S(1)}, u32[]{:S(2)}, u32[]{:S(2)}) collective-permute-start(f32[256,128]{1,0:T(8,128)S(1)} %shard_map.136.refs_6_), channel_id=1, source_target_pairs={{0,16},{4,20},{8,24},{12,28},{16,0},{20,4},{24,8},{28,12},{1,17},{... | collective-permute-start | bytes 393224 | tf_op jit(solution)/shard_map/ppermute | solution.py:445
  35.7 5.0 %collective-permute-start.10 = (f32[256,128]{1,0:T(8,128)S(1)}, f32[256,128]{1,0:T(8,128)S(1)}, u32[]{:S(2)}, u32[]{:S(2)}) collective-permute-start(f32[256,128]{1,0:T(8,128)S(1)} %shard_map.136.refs_6_), channel_id=1, source_target_pairs={{0,8},{4,12},{8,0},{12,4},{16,24},{20,28},{24,16},{28,20},{1,9},{5... | collective-permute-start | bytes 393224 | tf_op jit(solution)/shard_map/ppermute | solution.py:445
  37.2 7.3 %collective-permute-start.13 = (f32[256,128]{1,0:T(8,128)S(1)}, f32[256,128]{1,0:T(8,128)S(1)}, u32[]{:S(2)}, u32[]{:S(2)}) collective-permute-start(f32[256,128]{1,0:T(8,128)S(1)} %shard_map.136.refs_6_), channel_id=1, source_target_pairs={{0,4},{4,0},{8,12},{12,8},{16,20},{20,16},{24,28},{28,24},{1,5},{5... | collective-permute-start | bytes 393224 | tf_op jit(solution)/shard_map/ppermute | solution.py:445
  39.7 4.8 %collective-permute-start.16 = (f32[256,128]{1,0:T(8,128)S(1)}, f32[256,128]{1,0:T(8,128)S(1)}, u32[]{:S(2)}, u32[]{:S(2)}) collective-permute-start(f32[256,128]{1,0:T(8,128)S(1)} %collective-permute-done.12.refs_9_), channel_id=1, source_target_pairs={{0,4},{4,0},{8,12},{12,8},{16,20},{20,16},{24,28},{28,24},{1,5},{5... | collective-permute-start | bytes 393224 | tf_op jit(solution)/shard_map/ppermute | solution.py:445
  40.7 3.9 %collective-permute-start.15 = (f32[256,128]{1,0:T(8,128)S(1)}, f32[256,128]{1,0:T(8,128)S(1)}, u32[]{:S(2)}, u32[]{:S(2)}) collective-permute-start(f32[256,128]{1,0:T(8,128)S(1)} %collective-permute-done.11.refs_8_), channel_id=1, source_target_pairs={{0,4},{4,0},{8,12},{12,8},{16,20},{20,16},{24,28},{28,24},{1,5},{5... | collective-permute-start | bytes 393224 | tf_op jit(solution)/shard_map/ppermute | solution.py:445
  40.7 3.8 %collective-permute-start.14 = (f32[256,128]{1,0:T(8,128)S(1)}, f32[256,128]{1,0:T(8,128)S(1)}, u32[]{:S(2)}, u32[]{:S(2)}) collective-permute-start(f32[256,128]{1,0:T(8,128)S(1)} %collective-permute-done.10.refs_7_), channel_id=1, source_target_pairs={{0,4},{4,0},{8,12},{12,8},{16,20},{20,16},{24,28},{28,24},{1,5},{5... | collective-permute-start | bytes 393224 | tf_op jit(solution)/shard_map/ppermute | solution.py:445

commit v6 on v5

--- a/solution.py
+++ b/solution.py
@@ -15,6 +15,7 @@
 LANES = 128
 META = 8
 VMEM_BYTES = 24 * 2**20
+
 
 F32 = jnp.float32
 BF16 = jnp.bfloat16
@@ -163,8 +164,9 @@
     core = visit % 2
     peers = visits // 2
     share = side // visits
-    wait(*range(FIRST_FAR))
+    wait(0, 1, 2)
     tap_rows(coef, coef_buf, tap_buf, rows_high, rows_low, slots)
+    wait(*range(3, FIRST_FAR))
     for b in range(slots):
         put_block(science[0, b], b, side, images)
         build_left(b, slots, side, tap_buf, left)
@@ -238,12 +240,21 @@
         pieces[j][pl.ds(2 * rows, meta_rows), :] = meta
 
 
+def look_up(scalars, slot):
+    base, lane = 0, slot
+    if scalars.shape[0] > META:
+        base = quotient(slot, LANES)
+        lane = slot - base * LANES
+        base = base * META
+    return tuple(scalars[base + n, lane].astype(jnp.int32) for n in (1, 2, 3))
+
+
 def plane_kernel(slots, side, tiles, visits, meta_rows, *refs):
     peers = visits // 2
     share = side // visits
     size = 2 * (TILE // visits)
     sources, pieces = refs[:peers], refs[peers : peers + tiles]
-    table, scalars, semaphore = refs[peers + tiles : peers + tiles + 3]
+    scalars, table, semaphore = refs[peers + tiles : peers + tiles + 3]
     sums = refs[peers + tiles + 3 :]
     visit = lax.axis_index("visit")
     sky = lax.axis_index("sky")
@@ -265,15 +276,7 @@
         for p in range(peers):
             total = sums[p % len(sums)]
             sender = 2 * (place ^ p) + (core ^ h)
-            slot = (sender * tiles + sky) * slots + b
-            base, lane = 0, slot
-            if meta_rows > META:
-                base = quotient(slot, LANES)
-                lane = slot - base * LANES
-                base = base * META
-            top = scalars[base + 1, lane].astype(jnp.int32)
-            left_edge = scalars[base + 2, lane].astype(jnp.int32)
-            owner = scalars[base + 3, lane].astype(jnp.int32)
+            top, left_edge, owner = look_up(scalars, (sender * tiles + sky) * slots + b)
             rows = sources[p][pl.ds((h * slots + b) * share, share), :]
             where = pl.ds(first_row(top, visit, visits), share)
             total[owner, 0, where, :] += jnp.where(col >= left_edge, rows, 0.0)
@@ -321,22 +324,49 @@
         )
 
 
-def stack_kernel(tiles, strip, *refs):
-    sources, out = refs[:tiles], refs[tiles]
-    size = 2 * strip
+def hold_kernel(source, out):
+    out[...] = source[pl.ds(0, META), :]
+
+
+def select_kernel(slots, side, tiles, visits, scalars, *refs):
+    peers = visits // 2
+    share = side // visits
+    strip = TILE // visits
+    sources, pieces, tile_rows = refs[:tiles], refs[tiles : tiles + peers], refs[tiles + peers]
+    visit = lax.axis_index("visit")
+    sky = lax.axis_index("sky")
+    core = visit % 2
+    place = visit // 2
     for j in range(tiles):
-        out[pl.ds(j * size, size), :] = sources[j][...]
+        for h in range(2):
+            tile_rows[sky ^ j, h] = sources[j][pl.ds(h * strip, strip), :]
+    col = lax.broadcasted_iota(jnp.int32, (share, LANES), 1)
+    for j in range(peers):
+        piece = pieces[j]
+        piece[pl.ds(2 * slots * share, 2 * strip), :] = sources[0][...]
+
+        def pick(n, j=j, piece=piece):
+            h, b = quotient(n, slots), n % slots
+            reader = 2 * (place ^ j) + (core ^ h)
+            top, left_edge, owner = look_up(scalars, (reader * tiles + sky) * slots + b)
+            where = pl.ds(first_row(top, visit, visits), share)
+            piece[pl.ds(n * share, share), :] = jnp.where(
+                col >= left_edge, tile_rows[owner, 0, where, :], tile_rows[owner, 1, where, :]
+            )
+
+        repeat(2 * slots, peers, pick)
 
 
 def second_kernel(
-    slots, side, tiles, strip, peers,
+    slots, side, strip, peers,
     left, across_high, across_low, science, counts, places,
     *refs,
 ):
     pieces, refs = refs[: 2 * peers], refs[2 * peers :]
-    template, difference, images, right, total, staged, results, outward = refs
+    template, difference, images, right, total, windows, staged, results, outward = refs[-9:]
+    visits = 2 * peers
+    share = side // visits
     visit = lax.axis_index("visit")
-    sky = lax.axis_index("sky")
     core = visit % 2
     place = visit // 2
     for c in range(2):
@@ -344,24 +374,26 @@
             residue = 2 * (place ^ j) + (core ^ c)
             piece = pieces[c * peers + j]
 
-            def spread_rows(t, residue=residue, piece=piece):
-                for h in range(2):
-                    total[sky ^ t, h, pl.ds(residue, strip, stride=2 * peers), :] = piece[
-                        pl.ds((t * 2 + h) * strip, strip), :
-                    ]
-
-            repeat(tiles, peers, spread_rows)
+            for h in range(2):
+                total[h, pl.ds(residue, strip, stride=visits), :] = piece[
+                    pl.ds(2 * slots * share + h * strip, strip), :
+                ]
+
+            def spread_rows(b, c=c, residue=residue, piece=piece):
+                top = places[1, b]
+                start = first_row(top, residue, visits) * visits + residue - top
+                windows[b, pl.ds(start, share, stride=visits), :] = piece[
+                    pl.ds((c * slots + b) * share, share), :
+                ]
+
+            repeat(slots, peers, spread_rows)
     for h in range(2):
-        staged[:, h * LANES : (h + 1) * LANES] = total[sky, h]
+        staged[:, h * LANES : (h + 1) * LANES] = total[h]
     copies = [pltpu.make_async_copy(staged, template.at[0], outward.at[slots])]
     copies[0].start()
-    col = lax.broadcasted_iota(jnp.int32, (side, side), 1)
     for b in range(slots):
-        owner, top, left_edge = places[0, b], places[1, b], places[2, b]
-        joined = jnp.where(
-            col >= left_edge, total[owner, 0, pl.ds(top, side), :], total[owner, 1, pl.ds(top, side), :]
-        )
-        put_block(pltpu.roll(joined, (side - left_edge) % side, 1), b, side, images)
+        block = pltpu.roll(windows[b], (side - places[2, b]) % side, 1)
+        put_block(block, b, side, images)
     across_stage(slots, side, images, across_high, across_low, right)
     for b in range(slots):
         matched = down_stage(b, side, left, right)
@@ -438,7 +470,8 @@
     pass_scratch = [
         pltpu.VMEM((slots * side, 2 * side), BF16),
         pltpu.VMEM((slots, PROFILES * side, 2 * side), BF16),
-        pltpu.VMEM((tiles, 2, TILE, LANES), F32),
+        pltpu.VMEM((2, TILE, LANES), F32),
+        pltpu.VMEM((slots, side, LANES), F32),
     ]
 
     def flip(value, axis, size, mask):
@@ -486,15 +519,12 @@
         [shape(2 * rows + meta_rows, LANES)] * peers,
     )
     arrived = exchange(pieces, "visit", visits, 2)
-    pieces = call(
+    *pieces, scalars = call(
         lambda *refs: plane_kernel(slots, side, tiles, visits, meta_rows, *refs),
         [near(a) for a in arrived],
-        [shape(2 * strip + meta_rows, LANES)] * tiles,
-        scratch=[
-            pltpu.VMEM((meta_rows, LANES), F32),
-            pltpu.SMEM((meta_rows, LANES), F32),
-            pltpu.SemaphoreType.DMA,
-        ]
+        [shape(2 * strip + meta_rows, LANES)] * tiles + [pltpu.SMEM((meta_rows, LANES), F32)],
+        out_space=[vmem] * tiles + [smem],
+        scratch=[pltpu.VMEM((meta_rows, LANES), F32), pltpu.SemaphoreType.DMA]
         + [pltpu.VMEM((tiles, 2, strip, LANES), F32)] * min(peers, 4),
     )
     arrived = exchange(pieces, "sky", tiles, 1)
@@ -504,20 +534,26 @@
         shape(2 * strip, LANES),
     )
     strips = exchange([strip_own] * tiles, "sky", tiles, 1)
-    piece = call(
-        lambda *refs: stack_kernel(tiles, strip, *refs),
-        [near(a) for a in strips],
-        shape(tiles * 2 * strip, LANES),
-    )
-    mine = exchange([piece] * peers, "visit", visits, 2)
-    theirs = [flip(p, "visit", visits, 1) for p in mine]
+    pieces = call(
+        lambda *refs: select_kernel(slots, side, tiles, visits, *refs),
+        (pltpu.with_memory_space_constraint(scalars, pltpu.SMEM), *map(near, strips)),
+        [shape(2 * strip + 2 * rows, LANES)] * peers,
+        specs=[smem] + [vmem] * tiles,
+        scratch=[pltpu.VMEM((tiles, 2, strip, LANES), F32)],
+    )
+    mine = exchange(pieces, "visit", visits, 2)
+    theirs, markers = [], []
+    for j in range(peers):
+        theirs.append(flip(mine[j], "visit", visits, 1))
+        if j > 1:
+            markers.append(call(hold_kernel, (near(mine[j]),), shape(META, LANES)))
     template, difference = call(
-        lambda *refs: second_kernel(slots, side, tiles, strip, peers, *refs),
+        lambda *refs: second_kernel(slots, side, strip, peers, *refs),
         (near(left), *map(near, ready), counts,
          pltpu.with_memory_space_constraint(places, pltpu.SMEM),
-         *map(near, mine), *map(near, theirs)),
+         *map(near, mine), *map(near, theirs), *map(near, markers)),
         [jax.ShapeDtypeStruct(d, F32) for d in ((1, TILE, TILE), (1, slots, side, side))],
-        specs=[vmem] * 4 + [smem] * 2 + [vmem] * (2 * peers),
+        specs=[vmem] * 4 + [smem] * 2 + [vmem] * (2 * peers + len(markers)),
         scratch=pass_scratch
         + [pltpu.VMEM((TILE, TILE), F32), pltpu.VMEM((slots, side, side), F32)]
         + [pltpu.SemaphoreType.DMA((slots + 1,))],

time: 47.6 us -> 47 us (0.987)
  starting transfers between devices: 18 us -> 17.5 us
    ppermute x17, starting transfers between devices: 18 us -> 17.5 us  [flip(): return lax.ppermute(value, axis, [(d, d ^ mask) for d in range(size)])]
    pallas_call x7 -> x9, Pallas kernels: 11 us -> 11.1 us  [call(): pl.pallas_call(function, out_shape=outs, in_specs=specs or [vmem] * len(i...]
  transfers between devices with their start and end apart: 17 -> 17, of which waited for: 10 -> 11; matrix products, arithmetic and copies ran while one was open for 0% -> 0% of each run, Pallas kernels for 7% -> 7%
where the time goes in v6:
time: 47 us; the launch traced here: 46.8 us
  starting transfers between devices  17.5 us (37%)
  waiting for transfers between devices  16.8 us (36%)
  Pallas kernels  11.1 us (24%)
  between operations  1.38 us (3%)
    ppermute x17, starting transfers between devices, flip(): return lax.ppermute(value, axis, [(d, d ^ mask) for d in range(size)])  17.5 us
    ppermute x17, waiting for transfers between devices, flip(): return lax.ppermute(value, axis, [(d, d ^ mask) for d in range(size)])  16.8 us
    pallas_call x9, Pallas kernels, call(): pl.pallas_call(function, out_shape=outs, in_specs=specs or [vmem] * len(i...  11.1 us
  transfers between devices with their start and end apart: 17, of which 11 were waited for; matrix products, arithmetic and copies ran while one was open for 0% of the time, Pallas kernels for 7%

profile of v6, /device:TPU:0, one launch (start us, length us, event | category | flops | bytes accessed | tf_op | source)
XLA Modules:
  0.0 46.8 jit_solution(1483727587655723160)
XLA Ops:
  1.3 3.6 %shard_map.132 = (f32[264,128]{1,0:T(8,128)S(1)}, f32[264,128]{1,0:T(8,128)S(1)}) custom-call(f32[1,3,4,49]{3,2,1,0:T(4,128)} %bitcast.3, bf16[64,896]{1,0:T(8,128)(2,1)} %constant.10.clone.refs_1_, bf16[64,896]{1,0:T(8,128)(2,1)} %constant.11.clone.refs_2_, f32[1,4,128,128]{3,2,1,0:T(8,128)} %refs_3_.3, bf16[128,896]{1,0:T(8,128)(2,1)} %constant.8.clone.refs_6_.refs_4_, ...), custom_call_target="tpu_custom_call" | custom-call | tf_op jit(solution)/shard_map/pallas_call | solution.py:454
  4.8 0.6 %collective-permute-start = (f32[264,128]{1,0:T(8,128)S(1)}, f32[264,128]{1,0:T(8,128)S(1)}, u32[]{:S(2)}, u32[]{:S(2)}) collective-permute-start(f32[264,128]{1,0:T(8,128)S(1)} %get-tuple-element.28), channel_id=1, source_target_pairs={{0,4},{4,0},{8,12},{12,8},{16,20},{20,16},{24,28},{28,24},{1,5},{5... | collective-permute-start | bytes 405512 | tf_op jit(solution)/shard_map/ppermute | solution.py:478
  5.4 1.0 %collective-permute-done.refs_1_ = f32[264,128]{1,0:T(8,128)S(1)} collective-permute-done((f32[264,128]{1,0:T(8,128)S(1)}, f32[264,128]{1,0:T(8,128)S(1)}, u32[]{:S(2)}, u32[]{:S(2)}) %collective-permute-start) | collective-permute-done | bytes 135200 | tf_op jit(solution)/shard_map/ppermute | solution.py:478
  6.4 2.9 %collective-permute-start.1 = (f32[136,128]{1,0:T(8,128)S(1)}, f32[136,128]{1,0:T(8,128)S(1)}, u32[]{:S(2)}, u32[]{:S(2)}) collective-permute-start(f32[136,128]{1,0:T(8,128)S(1)} %get-tuple-element.30), channel_id=1, source_target_pairs={{0,8},{4,12},{8,0},{12,4},{16,24},{20,28},{24,16},{28,20},{1,9},{5... | collective-permute-start | bytes 208904 | tf_op jit(solution)/shard_map/ppermute | solution.py:478
  9.3 1.5 %collective-permute-start.2 = (f32[136,128]{1,0:T(8,128)S(1)}, f32[136,128]{1,0:T(8,128)S(1)}, u32[]{:S(2)}, u32[]{:S(2)}) collective-permute-start(f32[136,128]{1,0:T(8,128)S(1)} %get-tuple-element.31), channel_id=1, source_target_pairs={{0,16},{4,20},{8,24},{12,28},{16,0},{20,4},{24,8},{28,12},{1,17},{... | collective-permute-start | bytes 208904 | tf_op jit(solution)/shard_map/ppermute | solution.py:478
  10.8 0.0 collective-permute-start.3
  10.9 1.0 %collective-permute-done.1.refs_1_ = f32[136,128]{1,0:T(8,128)S(1)} collective-permute-done((f32[136,128]{1,0:T(8,128)S(1)}, f32[136,128]{1,0:T(8,128)S(1)}, u32[]{:S(2)}, u32[]{:S(2)}) %collective-permute-start.1) | collective-permute-done | bytes 69664 | tf_op jit(solution)/shard_map/ppermute | solution.py:478
  11.8 1.8 %collective-permute-done.2.refs_2_ = f32[136,128]{1,0:T(8,128)S(1)} collective-permute-done((f32[136,128]{1,0:T(8,128)S(1)}, f32[136,128]{1,0:T(8,128)S(1)}, u32[]{:S(2)}, u32[]{:S(2)}) %collective-permute-start.2) | collective-permute-done | bytes 69664 | tf_op jit(solution)/shard_map/ppermute | solution.py:478
  13.6 2.4 %collective-permute-done.3.refs_3_ = f32[136,128]{1,0:T(8,128)S(1)} collective-permute-done((f32[136,128]{1,0:T(8,128)S(1)}, f32[136,128]{1,0:T(8,128)S(1)}, u32[]{:S(2)}, u32[]{:S(2)}) %collective-permute-start.3) | collective-permute-done | bytes 69664 | tf_op jit(solution)/shard_map/ppermute | solution.py:478
  16.0 1.0 %shard_map.134 = (f32[72,128]{1,0:T(8,128)S(1)}, f32[72,128]{1,0:T(8,128)S(1)}, f32[72,128]{1,0:T(8,128)S(1)}, f32[72,128]{1,0:T(8,128)S(1)}, f32[8,128]{1,0:T(8,128)S(4)}) custom-call(f32[136,128]{1,0:T(8,128)S(1)} %get-tuple-element.29.refs_0_, f32[136,128]{1,0:T(8,128)S(1)} %collective-permute-done.1.refs_1_, ...), custom_call_target="tpu_custom_call" | custom-call | tf_op jit(solution)/shard_map/pallas_call | solution.py:454
  17.0 1.6 %collective-permute-start.4 = (f32[72,128]{1,0:T(8,128)S(1)}, f32[72,128]{1,0:T(8,128)S(1)}, u32[]{:S(2)}, u32[]{:S(2)}) collective-permute-start(f32[72,128]{1,0:T(8,128)S(1)} %get-tuple-element.35), channel_id=1, source_target_pairs={{0,1},{1,0},{2,3},{3,2},{4,5},{5,4},{6,7},{7,6},{8,9},{9,8},{10,11... | collective-permute-start | bytes 110600 | tf_op jit(solution)/shard_map/ppermute | solution.py:478
  18.7 2.6 %collective-permute-start.5 = (f32[72,128]{1,0:T(8,128)S(1)}, f32[72,128]{1,0:T(8,128)S(1)}, u32[]{:S(2)}, u32[]{:S(2)}) collective-permute-start(f32[72,128]{1,0:T(8,128)S(1)} %get-tuple-element.36), channel_id=1, source_target_pairs={{0,2},{1,3},{2,0},{3,1},{4,6},{5,7},{6,4},{7,5},{8,10},{9,11},{10,... | collective-permute-start | bytes 110600 | tf_op jit(solution)/shard_map/ppermute | solution.py:478
  21.3 0.2 collective-permute-start.6
  21.5 0.0 collective-permute-done.4.refs_1_
  21.5 2.8 %collective-permute-done.5.refs_2_ = f32[72,128]{1,0:T(8,128)S(1)} collective-permute-done((f32[72,128]{1,0:T(8,128)S(1)}, f32[72,128]{1,0:T(8,128)S(1)}, u32[]{:S(2)}, u32[]{:S(2)}) %collective-permute-start.5) | collective-permute-done | bytes 36896 | tf_op jit(solution)/shard_map/ppermute | solution.py:478
  24.3 2.8 %collective-permute-done.6.refs_3_ = f32[72,128]{1,0:T(8,128)S(1)} collective-permute-done((f32[72,128]{1,0:T(8,128)S(1)}, f32[72,128]{1,0:T(8,128)S(1)}, u32[]{:S(2)}, u32[]{:S(2)}) %collective-permute-start.6) | collective-permute-done | bytes 36896 | tf_op jit(solution)/shard_map/ppermute | solution.py:478
  27.0 0.2 shard_map.135.refs_1_
  27.2 0.5 %collective-permute-start.9 = (f32[64,128]{1,0:T(8,128)S(1)}, f32[64,128]{1,0:T(8,128)S(1)}, u32[]{:S(2)}, u32[]{:S(2)}) collective-permute-start(f32[64,128]{1,0:T(8,128)S(1)} %shard_map.135.refs_1_), channel_id=1, source_target_pairs={{0,3},{1,2},{2,1},{3,0},{4,7},{5,6},{6,5},{7,4},{8,11},{9,10},{10,... | collective-permute-start | bytes 98312 | tf_op jit(solution)/shard_map/ppermute | solution.py:478
  27.7 0.0 collective-permute-start.8
  27.7 4.0 %collective-permute-start.7 = (f32[64,128]{1,0:T(8,128)S(1)}, f32[64,128]{1,0:T(8,128)S(1)}, u32[]{:S(2)}, u32[]{:S(2)}) collective-permute-start(f32[64,128]{1,0:T(8,128)S(1)} %shard_map.135.refs_1_), channel_id=1, source_target_pairs={{0,1},{1,0},{2,3},{3,2},{4,5},{5,4},{6,7},{7,6},{8,9},{9,8},{10,11... | collective-permute-start | bytes 98312 | tf_op jit(solution)/shard_map/ppermute | solution.py:478
  31.7 1.3 %collective-permute-done.9.refs_4_ = f32[64,128]{1,0:T(8,128)S(1)} collective-permute-done((f32[64,128]{1,0:T(8,128)S(1)}, f32[64,128]{1,0:T(8,128)S(1)}, u32[]{:S(2)}, u32[]{:S(2)}) %collective-permute-start.9) | collective-permute-done | bytes 32800 | tf_op jit(solution)/shard_map/ppermute | solution.py:478
  33.0 0.0 collective-permute-done.8.refs_3_
  33.0 0.6 %collective-permute-done.7.refs_2_ = f32[64,128]{1,0:T(8,128)S(1)} collective-permute-done((f32[64,128]{1,0:T(8,128)S(1)}, f32[64,128]{1,0:T(8,128)S(1)}, u32[]{:S(2)}, u32[]{:S(2)}) %collective-permute-start.7) | collective-permute-done | bytes 32800 | tf_op jit(solution)/shard_map/ppermute | solution.py:478
  33.6 0.3 shard_map.136
  33.9 0.6 %collective-permute-start.10 = (f32[192,128]{1,0:T(8,128)S(1)}, f32[192,128]{1,0:T(8,128)S(1)}, u32[]{:S(2)}, u32[]{:S(2)}) collective-permute-start(f32[192,128]{1,0:T(8,128)S(1)} %get-tuple-element.39), channel_id=1, source_target_pairs={{0,8},{4,12},{8,0},{12,4},{16,24},{20,28},{24,16},{28,20},{1,9},{5... | collective-permute-start | bytes 294920 | tf_op jit(solution)/shard_map/ppermute | solution.py:478
  34.5 0.6 %collective-permute-start.11 = (f32[192,128]{1,0:T(8,128)S(1)}, f32[192,128]{1,0:T(8,128)S(1)}, u32[]{:S(2)}, u32[]{:S(2)}) collective-permute-start(f32[192,128]{1,0:T(8,128)S(1)} %get-tuple-element.40), channel_id=1, source_target_pairs={{0,16},{4,20},{8,24},{12,28},{16,0},{20,4},{24,8},{28,12},{1,17},{... | collective-permute-start | bytes 294920 | tf_op jit(solution)/shard_map/ppermute | solution.py:478
  35.1 2.4 %collective-permute-start.12 = (f32[192,128]{1,0:T(8,128)S(1)}, f32[192,128]{1,0:T(8,128)S(1)}, u32[]{:S(2)}, u32[]{:S(2)}) collective-permute-start(f32[192,128]{1,0:T(8,128)S(1)} %get-tuple-element.41), channel_id=1, source_target_pairs={{0,24},{4,28},{8,16},{12,20},{16,8},{20,12},{24,0},{28,4},{1,25},{... | collective-permute-start | bytes 294920 | tf_op jit(solution)/shard_map/ppermute | solution.py:478
  37.5 0.0 collective-permute-start.13
  37.5 1.1 %collective-permute-done.10.refs_7_ = f32[192,128]{1,0:T(8,128)S(1)} collective-permute-done((f32[192,128]{1,0:T(8,128)S(1)}, f32[192,128]{1,0:T(8,128)S(1)}, u32[]{:S(2)}, u32[]{:S(2)}) %collective-permute-start.10) | collective-permute-done | bytes 98336 | tf_op jit(solution)/shard_map/ppermute | solution.py:478
  38.6 0.0 collective-permute-start.14
  38.6 0.5 %collective-permute-done.11.source.refs_8_ = f32[192,128]{1,0:T(8,128)S(1)} collective-permute-done((f32[192,128]{1,0:T(8,128)S(1)}, f32[192,128]{1,0:T(8,128)S(1)}, u32[]{:S(2)}, u32[]{:S(2)}) %collective-permute-start.11) | collective-permute-done | bytes 98336 | tf_op jit(solution)/shard_map/ppermute | solution.py:478
  39.1 0.0 collective-permute-start.15
  39.1 1.5 %collective-permute-done.12.source.refs_9_ = f32[192,128]{1,0:T(8,128)S(1)} collective-permute-done((f32[192,128]{1,0:T(8,128)S(1)}, f32[192,128]{1,0:T(8,128)S(1)}, u32[]{:S(2)}, u32[]{:S(2)}) %collective-permute-start.12) | collective-permute-done | bytes 98336 | tf_op jit(solution)/shard_map/ppermute | solution.py:478
  40.6 0.0 collective-permute-start.16
  40.6 3.3 %shard_map.131 = (bf16[4,512,896]{2,1,0:T(8,128)(2,1)S(1)}, s32[3,4]{1,0:T(4,128)S(4)}, bf16[128,896]{1,0:T(8,128)(2,1)S(1)}, bf16[128,896]{1,0:T(8,128)(2,1)S(1)}, f32[1,4,128,128]{3,2,1,0:T(8,128)S(1)}) custom-call(f32[1,3,4,49]{3,2,1,0:T(4,128)} %bitcast.4, bf16[64,896]{1,0:T(8,128)(2,1)} %constant.10.clone.refs_1_, ...), custom_call_target="tpu_custom_call" | custom-call | tf_op jit(solution)/shard_map/pallas_call | solution.py:454
  44.0 0.0 collective-permute-done.13.refs_10_
  44.0 0.0 collective-permute-done.14.refs_11_
  44.0 0.0 collective-permute-done.15.refs_12_
  44.0 0.0 collective-permute-done.16.refs_13_
  44.0 2.8 %shard_map.139 = (f32[1,256,256]{2,1,0:T(8,128)}, f32[1,4,128,128]{3,2,1,0:T(8,128)}) custom-call(bf16[4,512,896]{2,1,0:T(8,128)(2,1)S(1)} %get-tuple-element.22.refs_0_, bf16[128,896]{1,0:T(8,128)(2,1)S(1)} %get-tuple-element.23.refs_1_, bf16[128,896]{1,0:T(8,128)(2,1)S(1)} %get-tuple-element.24.refs_2_, f32[1,4,128,128]{3,2,1,0:T(8,128)S(1)} %get-tuple-element.25.refs_3_, ...), custom_call_target="tpu_custom_call" | custom-call | tf_op jit(solution)/shard_map/pallas_call | solution.py:454
  (3 shorter events, 0.0 us)
Async XLA Ops:
  4.8 1.5 %collective-permute-start = (f32[264,128]{1,0:T(8,128)S(1)}, f32[264,128]{1,0:T(8,128)S(1)}, u32[]{:S(2)}, u32[]{:S(2)}) collective-permute-start(f32[264,128]{1,0:T(8,128)S(1)} %get-tuple-element.28), channel_id=1, source_target_pairs={{0,4},{4,0},{8,12},{12,8},{16,20},{20,16},{24,28},{28,24},{1,5},{5... | collective-permute-start | bytes 405512 | tf_op jit(solution)/shard_map/ppermute | solution.py:478
  6.4 5.4 %collective-permute-start.1 = (f32[136,128]{1,0:T(8,128)S(1)}, f32[136,128]{1,0:T(8,128)S(1)}, u32[]{:S(2)}, u32[]{:S(2)}) collective-permute-start(f32[136,128]{1,0:T(8,128)S(1)} %get-tuple-element.30), channel_id=1, source_target_pairs={{0,8},{4,12},{8,0},{12,4},{16,24},{20,28},{24,16},{28,20},{1,9},{5... | collective-permute-start | bytes 208904 | tf_op jit(solution)/shard_map/ppermute | solution.py:478
  9.3 4.3 %collective-permute-start.2 = (f32[136,128]{1,0:T(8,128)S(1)}, f32[136,128]{1,0:T(8,128)S(1)}, u32[]{:S(2)}, u32[]{:S(2)}) collective-permute-start(f32[136,128]{1,0:T(8,128)S(1)} %get-tuple-element.31), channel_id=1, source_target_pairs={{0,16},{4,20},{8,24},{12,28},{16,0},{20,4},{24,8},{28,12},{1,17},{... | collective-permute-start | bytes 208904 | tf_op jit(solution)/shard_map/ppermute | solution.py:478
  10.8 5.2 %collective-permute-start.3 = (f32[136,128]{1,0:T(8,128)S(1)}, f32[136,128]{1,0:T(8,128)S(1)}, u32[]{:S(2)}, u32[]{:S(2)}) collective-permute-start(f32[136,128]{1,0:T(8,128)S(1)} %get-tuple-element.32), channel_id=1, source_target_pairs={{0,24},{4,28},{8,16},{12,20},{16,8},{20,12},{24,0},{28,4},{1,25},{... | collective-permute-start | bytes 208904 | tf_op jit(solution)/shard_map/ppermute | solution.py:478
  17.0 4.5 %collective-permute-start.4 = (f32[72,128]{1,0:T(8,128)S(1)}, f32[72,128]{1,0:T(8,128)S(1)}, u32[]{:S(2)}, u32[]{:S(2)}) collective-permute-start(f32[72,128]{1,0:T(8,128)S(1)} %get-tuple-element.35), channel_id=1, source_target_pairs={{0,1},{1,0},{2,3},{3,2},{4,5},{5,4},{6,7},{7,6},{8,9},{9,8},{10,11... | collective-permute-start | bytes 110600 | tf_op jit(solution)/shard_map/ppermute | solution.py:478
  18.7 5.6 %collective-permute-start.5 = (f32[72,128]{1,0:T(8,128)S(1)}, f32[72,128]{1,0:T(8,128)S(1)}, u32[]{:S(2)}, u32[]{:S(2)}) collective-permute-start(f32[72,128]{1,0:T(8,128)S(1)} %get-tuple-element.36), channel_id=1, source_target_pairs={{0,2},{1,3},{2,0},{3,1},{4,6},{5,7},{6,4},{7,5},{8,10},{9,11},{10,... | collective-permute-start | bytes 110600 | tf_op jit(solution)/shard_map/ppermute | solution.py:478
  21.3 5.8 %collective-permute-start.6 = (f32[72,128]{1,0:T(8,128)S(1)}, f32[72,128]{1,0:T(8,128)S(1)}, u32[]{:S(2)}, u32[]{:S(2)}) collective-permute-start(f32[72,128]{1,0:T(8,128)S(1)} %get-tuple-element.37), channel_id=1, source_target_pairs={{0,3},{1,2},{2,1},{3,0},{4,7},{5,6},{6,5},{7,4},{8,11},{9,10},{10,... | collective-permute-start | bytes 110600 | tf_op jit(solution)/shard_map/ppermute | solution.py:478
  27.2 5.8 %collective-permute-start.9 = (f32[64,128]{1,0:T(8,128)S(1)}, f32[64,128]{1,0:T(8,128)S(1)}, u32[]{:S(2)}, u32[]{:S(2)}) collective-permute-start(f32[64,128]{1,0:T(8,128)S(1)} %shard_map.135.refs_1_), channel_id=1, source_target_pairs={{0,3},{1,2},{2,1},{3,0},{4,7},{5,6},{6,5},{7,4},{8,11},{9,10},{10,... | collective-permute-start | bytes 98312 | tf_op jit(solution)/shard_map/ppermute | solution.py:478
  27.7 5.3 %collective-permute-start.8 = (f32[64,128]{1,0:T(8,128)S(1)}, f32[64,128]{1,0:T(8,128)S(1)}, u32[]{:S(2)}, u32[]{:S(2)}) collective-permute-start(f32[64,128]{1,0:T(8,128)S(1)} %shard_map.135.refs_1_), channel_id=1, source_target_pairs={{0,2},{1,3},{2,0},{3,1},{4,6},{5,7},{6,4},{7,5},{8,10},{9,11},{10,... | collective-permute-start | bytes 98312 | tf_op jit(solution)/shard_map/ppermute | solution.py:478
  27.7 5.8 %collective-permute-start.7 = (f32[64,128]{1,0:T(8,128)S(1)}, f32[64,128]{1,0:T(8,128)S(1)}, u32[]{:S(2)}, u32[]{:S(2)}) collective-permute-start(f32[64,128]{1,0:T(8,128)S(1)} %shard_map.135.refs_1_), channel_id=1, source_target_pairs={{0,1},{1,0},{2,3},{3,2},{4,5},{5,4},{6,7},{7,6},{8,9},{9,8},{10,11... | collective-permute-start | bytes 98312 | tf_op jit(solution)/shard_map/ppermute | solution.py:478
  33.9 4.7 %collective-permute-start.10 = (f32[192,128]{1,0:T(8,128)S(1)}, f32[192,128]{1,0:T(8,128)S(1)}, u32[]{:S(2)}, u32[]{:S(2)}) collective-permute-start(f32[192,128]{1,0:T(8,128)S(1)} %get-tuple-element.39), channel_id=1, source_target_pairs={{0,8},{4,12},{8,0},{12,4},{16,24},{20,28},{24,16},{28,20},{1,9},{5... | collective-permute-start | bytes 294920 | tf_op jit(solution)/shard_map/ppermute | solution.py:478
  34.5 4.6 %collective-permute-start.11 = (f32[192,128]{1,0:T(8,128)S(1)}, f32[192,128]{1,0:T(8,128)S(1)}, u32[]{:S(2)}, u32[]{:S(2)}) collective-permute-start(f32[192,128]{1,0:T(8,128)S(1)} %get-tuple-element.40), channel_id=1, source_target_pairs={{0,16},{4,20},{8,24},{12,28},{16,0},{20,4},{24,8},{28,12},{1,17},{... | collective-permute-start | bytes 294920 | tf_op jit(solution)/shard_map/ppermute | solution.py:478
  35.1 5.5 %collective-permute-start.12 = (f32[192,128]{1,0:T(8,128)S(1)}, f32[192,128]{1,0:T(8,128)S(1)}, u32[]{:S(2)}, u32[]{:S(2)}) collective-permute-start(f32[192,128]{1,0:T(8,128)S(1)} %get-tuple-element.41), channel_id=1, source_target_pairs={{0,24},{4,28},{8,16},{12,20},{16,8},{20,12},{24,0},{28,4},{1,25},{... | collective-permute-start | bytes 294920 | tf_op jit(solution)/shard_map/ppermute | solution.py:478
  37.5 6.5 %collective-permute-start.13 = (f32[192,128]{1,0:T(8,128)S(1)}, f32[192,128]{1,0:T(8,128)S(1)}, u32[]{:S(2)}, u32[]{:S(2)}) collective-permute-start(f32[192,128]{1,0:T(8,128)S(1)} %get-tuple-element.38.refs_6_), channel_id=1, source_target_pairs={{0,4},{4,0},{8,12},{12,8},{16,20},{20,16},{24,28},{28,24},{1,5},{5... | collective-permute-start | bytes 294920 | tf_op jit(solution)/shard_map/ppermute | solution.py:478
  38.6 5.4 %collective-permute-start.14 = (f32[192,128]{1,0:T(8,128)S(1)}, f32[192,128]{1,0:T(8,128)S(1)}, u32[]{:S(2)}, u32[]{:S(2)}) collective-permute-start(f32[192,128]{1,0:T(8,128)S(1)} %collective-permute-done.10.refs_7_), channel_id=1, source_target_pairs={{0,4},{4,0},{8,12},{12,8},{16,20},{20,16},{24,28},{28,24},{1,5},{5... | collective-permute-start | bytes 294920 | tf_op jit(solution)/shard_map/ppermute | solution.py:478
  39.1 4.9 %collective-permute-start.15 = (f32[192,128]{1,0:T(8,128)S(1)}, f32[192,128]{1,0:T(8,128)S(1)}, u32[]{:S(2)}, u32[]{:S(2)}) collective-permute-start(f32[192,128]{1,0:T(8,128)S(1)} %collective-permute-done.11.source.refs_8_), channel_id=1, source_target_pairs={{0,4},{4,0},{8,12},{12,8},{16,20},{20,16},{24,28},{28,24},{1,5},{5... | collective-permute-start | bytes 294920 | tf_op jit(solution)/shard_map/ppermute | solution.py:478
  40.6 3.4 %collective-permute-start.16 = (f32[192,128]{1,0:T(8,128)S(1)}, f32[192,128]{1,0:T(8,128)S(1)}, u32[]{:S(2)}, u32[]{:S(2)}) collective-permute-start(f32[192,128]{1,0:T(8,128)S(1)} %collective-permute-done.12.source.refs_9_), channel_id=1, source_target_pairs={{0,4},{4,0},{8,12},{12,8},{16,20},{20,16},{24,28},{28,24},{1,5},{5... | collective-permute-start | bytes 294920 | tf_op jit(solution)/shard_map/ppermute | solution.py:478
